TPU v7x, 32 devices: a whole 2x2x4 slice. The times are simulated.
32 devices in a mesh: groups: 2 (over x), seq: 16 (over z, y, core).
Axes of the slice: x: 2, y: 2, z: 4, core: 2. Of those that a mesh axis runs over, the one named last changes fastest.
Arguments:
- query_rows: bfloat16 [1536, 4096], P(('groups', 'seq')), parts along dimension 0, may hold values from -160 to 160
- key_rows: bfloat16 [1536, 4096], P(('groups', 'seq')), parts along dimension 0, may hold values from -8 to 8
- value_rows: bfloat16 [1536, 4096], P(('groups', 'seq')), parts along dimension 0, may hold values from -6 to 6
- proj_weight: bfloat16 [4096, 128], replicated, may hold values from -0.09375 to 0.09375
- in_weight: bfloat16 [3, 3, 3, 128, 512], replicated, may hold values from -0.109375 to 0.109375
- in_bias: float32 [512], replicated, may hold values from -3 to 3
- mid_weight: bfloat16 [3, 3, 3, 512, 512], P(None, None, None, None, 'seq'), may hold values from -0.0546875 to 0.0546875
- mid_bias: float32 [512], replicated, may hold values from -3 to 3
Outputs:
- upsampled: bfloat16 [32, 2, 2, 48, 128], P(('groups', 'seq')), parts along dimension 0
There are 2 independent parts, one for each index of `groups`. A program takes and returns all parts, laid end to end along the dimension named above; an argument that names none is the same for every part. Nothing has to cross between parts.
All inputs are finite; a program needn't handle non-finite values.
Results may differ from a plain program's by a relative error of at most 0.01.
Values may be sent and summed in bfloat16 or wider, within the bound.
No kernel may reach another device: no remote copies, remote signals or barrier semaphores. Data moves between devices by JAX's collectives and lax.ppermute only.
A program may use at most 128 MiB of HBM per device.

v0:
```python
import functools
import math

import jax
import jax.numpy as jnp
from jax import lax
from jax.experimental import pallas as pl
from jax.experimental.pallas import tpu as pltpu
from jax.sharding import PartitionSpec as P


D = 4096
HEADS = 32
HD = 128
C_LAT = 128
CH = 512
W = 24
F = 2
HT = 1


def padded_2(block, sides, width):
    for axis, dim in sides:
        count = lax.axis_size(axis)
        forward = [(i, i + 1) for i in range(count - 1)]
        backward = [(target, source) for source, target in forward]
        low = lax.ppermute(
            lax.slice_in_dim(block, block.shape[dim] - width, None, axis=dim), axis, forward
        )
        high = lax.ppermute(lax.slice_in_dim(block, 0, width, axis=dim), axis, backward)
        block = jnp.concatenate([low, block, high], axis=dim)
    return block


def unfold(padded, frames, height, columns):
    pieces = [
        padded[
            frame_off : frame_off + frames, row_off : row_off + height, col_off : col_off + columns
        ]
        for frame_off in range(3)
        for row_off in range(3)
        for col_off in range(3)
    ]
    return jnp.concatenate(pieces, axis=-1).reshape(frames * height * columns, -1)


def normed_latents(token_rows, proj_weight):
    widened = token_rows.astype(jnp.float32)
    normed = (
        widened * lax.rsqrt(jnp.mean(widened * widened, axis=1, keepdims=True) + 1e-06)
    ).astype(jnp.bfloat16)
    return jnp.dot(normed, proj_weight, preferred_element_type=jnp.float32).astype(jnp.bfloat16)


def extend(tile_cells):
    bordered = padded_2(tile_cells, (("seq", 1),), 1)
    return jnp.pad(bordered, ((1, 1), (0, 0), (1, 1), (0, 0)))


def shuffle_tile(summed, frames, height, columns):
    channels = summed.shape[-1] // 4
    return (
        summed.reshape(frames, height, columns, channels, 2, 2)
        .transpose(0, 1, 4, 2, 5, 3)
        .reshape(frames, 2 * height, 2 * columns, channels)
    )


def shared_heads(
    query_rows, key_rows, value_rows, proj_weight, in_weight, in_bias, mid_weight, mid_bias
):
    devices = lax.axis_size("seq")
    halves = max(1, devices // HEADS)
    unit_count = HEADS * halves // devices
    local_tokens = query_rows.shape[0]
    shard_rows = local_tokens // W
    half_width = W // halves
    score_scale = 1.0 / math.sqrt(HD)

    def by_head(rows):
        shaped = rows.reshape(local_tokens, HEADS, HD).transpose(1, 0, 2)
        shaped = jnp.broadcast_to(shaped[:, None], (HEADS, halves, local_tokens, HD))
        return shaped.reshape(devices, unit_count, local_tokens, HD)

    shaped = query_rows.reshape(shard_rows, halves, half_width, HEADS, HD).transpose(3, 1, 0, 2, 4)
    query_units = lax.all_to_all(
        shaped.reshape(devices, unit_count, shard_rows, half_width, HD),
        "seq",
        split_axis=0,
        concat_axis=0,
        tiled=True,
    )
    key_units = lax.all_to_all(by_head(key_rows), "seq", split_axis=0, concat_axis=0, tiled=True)
    value_units = lax.all_to_all(
        by_head(value_rows), "seq", split_axis=0, concat_axis=0, tiled=True
    )
    key_heads = key_units.transpose(1, 0, 2, 3).reshape(unit_count, -1, HD)
    value_heads = value_units.transpose(1, 0, 2, 3).reshape(unit_count, -1, HD)
    query_total = devices * shard_rows * half_width
    block_rows = 512 if query_total % 512 == 0 else query_total
    query_heads = (
        query_units.transpose(1, 0, 2, 3, 4)
        .reshape(unit_count, query_total // block_rows, block_rows, HD)
        .transpose(1, 0, 2, 3)
    )

    def attend(query_block):
        scores = (
            jnp.einsum("uqd,ukd->uqk", query_block, key_heads, preferred_element_type=jnp.float32)
            * score_scale
        )
        largest = jnp.max(scores, axis=2, keepdims=True)
        weights = jnp.exp(scores - largest)
        totals = jnp.sum(weights, axis=2, keepdims=True)
        mixture = jnp.einsum(
            "uqk,ukd->uqd",
            weights.astype(jnp.bfloat16),
            value_heads,
            preferred_element_type=jnp.float32,
        )
        return (mixture / totals).astype(jnp.bfloat16)

    attended = lax.map(attend, query_heads)
    attended = attended.transpose(1, 0, 2, 3).reshape(
        unit_count, devices, shard_rows, half_width, HD
    )
    arranged = attended.reshape(unit_count, F, devices, HT, half_width, HD).transpose(
        2, 0, 1, 3, 4, 5
    )
    arrived = lax.all_to_all(arranged, "seq", split_axis=0, concat_axis=0, tiled=True)
    arrived = arrived.reshape(HEADS, halves, F, HT, half_width, HD).transpose(2, 3, 1, 4, 0, 5)
    latents = normed_latents(arrived.reshape(F * HT * W, D), proj_weight).reshape(F, HT, W, C_LAT)
    unfolded_in = unfold(extend(latents), F, HT, W)
    first = (
        jnp.dot(unfolded_in, in_weight.reshape(27 * C_LAT, CH), preferred_element_type=jnp.float32)
        + in_bias
    ).astype(jnp.bfloat16)
    active = jax.nn.silu(first.astype(jnp.float32)).astype(jnp.bfloat16)
    unfolded_mid = unfold(extend(active.reshape(F, HT, W, CH)), F, HT, W)
    piece = lax.all_gather(mid_weight, "seq", axis=4, tiled=True)
    column_span = piece.shape[4]
    middle = (
        jnp.dot(
            unfolded_mid, piece.reshape(27 * CH, column_span), preferred_element_type=jnp.float32
        )
        + mid_bias
    ).astype(jnp.bfloat16)
    summed = first.astype(jnp.float32) + middle.astype(jnp.float32)
    return shuffle_tile(summed, F, HT, W).astype(jnp.bfloat16)[None]


def dot_f32(left, right, left_dim=1, right_dim=0):
    return lax.dot_general(
        left, right, (((left_dim,), (right_dim,)), ((), ())), preferred_element_type=jnp.float32
    )


def pack_body(query_ref, key_ref, value_ref, *rest, steps, span):
    blocks, sems = rest[:-1], rest[-1]
    rank = lax.axis_index("seq")
    copies = []
    for place, step in enumerate(steps):
        start = pl.multiple_of((rank ^ step) * span, span)
        for which, ref in enumerate((query_ref, key_ref, value_ref)):
            copies.append(
                pltpu.make_async_copy(
                    ref.at[:, pl.ds(start, span)], blocks[place].at[which], sems.at[place, which]
                )
            )
    for copy in copies:
        copy.start()
    for copy in copies:
        copy.wait()


def slice_body(proj_ref, out_ref, sem):
    span = out_ref.shape[0]
    start = pl.multiple_of(lax.axis_index("seq") * span, span)
    copy = pltpu.make_async_copy(proj_ref.at[pl.ds(start, span), :], out_ref, sem)
    copy.start()
    copy.wait()


def read_sums(ref, count):
    cells = ref.shape[0] - (2 if ref.dtype == jnp.bfloat16 else 1) * count
    parts = ref[:cells].astype(jnp.float32).reshape(count, cells // count, C_LAT)
    tail = ref[cells:].astype(jnp.float32)
    squares = tail[:count] + tail[count:] if ref.dtype == jnp.bfloat16 else tail
    return [parts[i] for i in range(count)], [squares[i : i + 1] for i in range(count)]


def write_sums(ref, parts, squares):
    cells = len(parts) * parts[0].shape[0]
    across = jnp.concatenate(squares, axis=0)
    if ref.dtype == jnp.bfloat16:
        coarse = across.astype(jnp.bfloat16).astype(jnp.float32)
        across = jnp.concatenate([coarse, across - coarse], axis=0)
    ref[:cells] = jnp.concatenate(parts, axis=0).astype(ref.dtype)
    ref[cells:] = across.astype(ref.dtype)


def attend_body(mid_weight_ref, proj_ref, *rest, order):
    blocks, (keep_ref, send_ref, mid_ref, mid_sem) = rest[:-4], rest[-4:]
    fetch = pltpu.make_async_copy(mid_weight_ref, mid_ref, mid_sem)
    fetch.start()
    devices = len(blocks)
    _, local, span = blocks[0].shape
    tokens = devices * local
    query, key, value = (
        jnp.concatenate([block[which] for block in blocks], axis=0) for which in range(3)
    )
    sharpness = math.log2(math.e) / math.sqrt(HD)
    units = [slice(first, first + HD) for first in range(0, span, HD)]
    scores = [dot_f32(query[:, lanes], key[:, lanes], 1, 1) for lanes in units]
    heads = []
    for lanes, score in zip(units, scores):
        weights = jnp.exp2((score - jnp.max(score, axis=1, keepdims=True)) * sharpness)
        totals = jnp.sum(weights, axis=1, keepdims=True)
        mixture = dot_f32(weights.astype(jnp.bfloat16), value[:, lanes])
        heads.append((mixture / totals).astype(jnp.bfloat16))
    attended = jnp.concatenate(heads, axis=1)
    widened = attended.astype(jnp.float32)
    squares = jnp.sum(widened * widened, axis=1, keepdims=True)
    partial = dot_f32(attended, proj_ref[...]).reshape(devices, local, C_LAT)
    lane = lax.broadcasted_iota(jnp.int32, (devices, local, C_LAT), 2)
    row = lax.broadcasted_iota(jnp.int32, (devices, local, C_LAT), 1)
    spread = jnp.broadcast_to(squares, (tokens, C_LAT)).reshape(devices, local, C_LAT)
    across = jnp.sum(jnp.where(lane == row, spread, 0.0), axis=1)
    for ref, first in ((keep_ref, 0), (send_ref, 1)):
        chosen = [order.index(step) for step in range(first, devices, 2)]
        write_sums(ref, [partial[i] for i in chosen], [across[i : i + 1] for i in chosen])
    fetch.wait()


def fold_body(keep_ref, got_ref, next_ref, send_ref, count, split):
    parts, squares = read_sums(keep_ref, count)
    more_parts, more_squares = read_sums(got_ref, count)
    parts = [x + y for x, y in zip(parts, more_parts)]
    squares = [x + y for x, y in zip(squares, more_squares)]
    for ref, first in ((next_ref, 0), (send_ref, 1)):
        chosen = range(first, count, 2) if split else range(count)
        write_sums(ref, [parts[i] for i in chosen], [squares[i] for i in chosen])


def latents_body(keep_ref, *rest):
    gots, out_ref = rest[:-1], rest[-1]
    count = len(rest)
    local = out_ref.shape[0] // count
    parts, squares = read_sums(keep_ref, count)
    for step, got in enumerate(gots, 1):
        more_parts, more_squares = read_sums(got, count)
        parts = [parts[i] + more_parts[i ^ step] for i in range(count)]
        squares = [squares[i] + more_squares[i ^ step] for i in range(count)]
    lane = lax.broadcasted_iota(jnp.int32, (local, C_LAT), 1)
    row = lax.broadcasted_iota(jnp.int32, (local, C_LAT), 0)
    done = []
    for part, square in zip(parts, squares):
        column = jnp.sum(jnp.where(lane == row, square, 0.0), axis=1, keepdims=True)
        done.append(part * lax.rsqrt(column / D + 1e-06))
    out_ref[...] = jnp.concatenate(done, axis=0).astype(jnp.bfloat16)


def convolve_body(
    in_weight_ref, in_bias_ref, mid_weight_ref, mid_bias_ref, *rest
):
    quarters, (out_ref, latents_ref, cols) = rest[:-3], rest[-3:]
    rank = lax.axis_index("seq")
    frame = latents_ref.shape[0] // F
    count = out_ref.shape[0] // len(quarters)
    local = quarters[0].shape[0] // count
    for low, quarter in enumerate(quarters):
        for high in range(count):
            block = rank ^ (high * len(quarters) + low)
            latents_ref[pl.ds(pl.multiple_of(block * local, 16), local), :] = quarter[
                high * local : (high + 1) * local, :
            ]
    own = mid_weight_ref.shape[0] // 27
    column = lax.broadcasted_iota(jnp.int32, (frame, C_LAT), 0) % W
    for index in range(F):
        cells = latents_ref[index * frame : (index + 1) * frame, :].astype(jnp.float32)
        shifted = (
            jnp.where(column == 0, 0.0, pltpu.roll(cells, 1, 0)),
            cells,
            jnp.where(column == W - 1, 0.0, pltpu.roll(cells, frame - 1, 0)),
        )
        blank = jnp.zeros((W, C_LAT), jnp.float32)
        for col_off, moved in enumerate(shifted):
            above = jnp.concatenate([blank, moved[:-W]], axis=0)
            below = jnp.concatenate([moved[W:], blank], axis=0)
            for row_off, piece in enumerate((above, moved, below)):
                at = (row_off * 3 + col_off) * C_LAT
                cols[index * frame : (index + 1) * frame, at : at + C_LAT] = piece.astype(
                    jnp.bfloat16
                )
    deep = 9 * C_LAT
    sums = [None] * F
    for tap in range(3):
        low, high = max(0, tap - 1), min(F, F + tap - 1)
        product = dot_f32(
            cols[low * frame : high * frame, :], in_weight_ref[tap * deep : (tap + 1) * deep, :]
        )
        for index in range(low, high):
            piece = product[(index - low) * frame : (index - low + 1) * frame]
            target = index - tap + 1
            sums[target] = piece if sums[target] is None else sums[target] + piece
    firsts = [(total + in_bias_ref[...]).astype(jnp.bfloat16) for total in sums]
    taps = [None] * F
    for index in range(F):
        wide = firsts[index].astype(jnp.float32)
        active = (wide * lax.logistic(wide)).astype(jnp.bfloat16)
        low, high = max(0, index + 2 - F), min(3, index + 2)
        product = dot_f32(mid_weight_ref[low * 9 * own : high * 9 * own, :], active, 1, 1)
        for tap in range(low, high):
            piece = product[(tap - low) * 9 * own : (tap - low + 1) * 9 * own]
            target = index - tap + 1
            taps[target] = piece if taps[target] is None else taps[target] + piece
    channel = lax.broadcasted_iota(jnp.int32, (own, CH), 1)
    mine = channel == lax.broadcasted_iota(jnp.int32, (own, CH), 0) + rank * own
    bias = jnp.sum(jnp.where(mine, mid_bias_ref[...], 0.0), axis=1, keepdims=True)
    chosen = jnp.where(mine, 1.0, 0.0).astype(jnp.bfloat16)
    spot = lax.broadcasted_iota(jnp.int32, (own, frame), 1)
    spot_column = spot % W
    outs = []
    for index in range(F):
        total = None
        for col_off in range(3):
            merged = None
            for row_off in range(3):
                at = (row_off * 3 + col_off) * own
                piece = taps[index][at : at + own, :]
                if row_off == 0:
                    piece = jnp.where(spot < W, 0.0, pltpu.roll(piece, W, 1))
                elif row_off == 2:
                    piece = jnp.where(spot >= frame - W, 0.0, pltpu.roll(piece, frame - W, 1))
                merged = piece if merged is None else merged + piece
            if col_off == 0:
                merged = jnp.where(spot_column == 0, 0.0, pltpu.roll(merged, 1, 1))
            elif col_off == 2:
                merged = jnp.where(spot_column == W - 1, 0.0, pltpu.roll(merged, frame - 1, 1))
            total = merged if total is None else total + merged
        middle = (total + bias).astype(jnp.bfloat16).astype(jnp.float32)
        outs.append((dot_f32(chosen, firsts[index], 1, 1) + middle).astype(jnp.bfloat16))
    stacked = jnp.concatenate(outs, axis=0)
    source = lax.broadcasted_iota(jnp.int32, (F * own, 128), 0)
    target = lax.broadcasted_iota(jnp.int32, (F * own, 128), 1)
    inner = source % own
    place = (source // own) * own + (inner % 4) * (own // 4) + inner // 4
    moves = jnp.where(place == target % 64, 1.0, 0.0).astype(jnp.bfloat16)
    moved = dot_f32(stacked, moves, 0, 0).reshape(frame // W, W, 128)
    tail = jnp.concatenate([moved[:, 16:], jnp.zeros((frame // W, 32 - W, 128), jnp.float32)], axis=1)
    lane = lax.broadcasted_iota(jnp.int32, (frame // W, 16, 128), 2)
    out_ref[...] = jnp.where(lane < 64, moved[:, :16], tail).astype(jnp.bfloat16)


def shuffle_body(rows_ref, out_ref, wide):
    devices = rows_ref.shape[0]
    share = C_LAT // devices
    rows = rows_ref[...].astype(jnp.float32)
    lane = lax.broadcasted_iota(jnp.int32, (W, 128), 1) // share
    for index in range(F):
        for part in range(4):
            origin = (index * 4 + part) * share
            total = None
            for source in range(devices):
                shift = source * share - origin
                moved = jnp.concatenate(
                    [
                        pltpu.roll(rows[source], shift % 128, 1),
                        pltpu.roll(rows[source, : W - 16], (shift + 64) % 128, 1),
                    ],
                    axis=0,
                )
                total = moved if total is None else jnp.where(lane == source, moved, total)
            wide[index, part // 2, pl.ds(part % 2, W, stride=2), :] = total
    out_ref[0] = wide[...].astype(jnp.bfloat16)


def near(array):
    return pltpu.with_memory_space_constraint(array, pltpu.VMEM)


def far(array):
    return pltpu.with_memory_space_constraint(array, pltpu.HBM)


LOCAL = pl.BlockSpec(memory_space=pltpu.VMEM)
REMOTE = pl.BlockSpec(memory_space=pltpu.HBM)


def launch(body, outs, in_specs, operands, scratch=(), mib=8):
    return pl.pallas_call(
        body,
        out_shape=outs,
        in_specs=in_specs,
        out_specs=jax.tree.map(lambda _: LOCAL, outs),
        scratch_shapes=scratch,
        compiler_params=pltpu.CompilerParams(vmem_limit_bytes=mib << 20),
    )(*operands)


def exchange_order(devices):
    half = devices // 2
    order = [0, half]
    for step in range(1, half):
        order += [step, half + step]
    return order


def swap(array, step):
    devices = lax.axis_size("seq")
    return near(lax.ppermute(array, "seq", [(i, i ^ step) for i in range(devices)]))


def sums_shape(count, local, dtype):
    tail = 2 * count if dtype == jnp.bfloat16 else count
    return pltpu.VMEM((count * local + tail, C_LAT), dtype)


def whole_heads(
    query_rows, key_rows, value_rows, proj_weight, in_weight, in_bias, mid_weight, mid_bias
):
    devices = lax.axis_size("seq")
    local = query_rows.shape[0]
    span = D // devices
    frame = devices * local // F
    own = mid_weight.shape[4]
    order = exchange_order(devices)
    order = order[1:] + [0]
    landed = []
    for steps in (order[:2], order[2:]):
        blocks = launch(
            functools.partial(pack_body, steps=steps, span=span),
            [pltpu.VMEM((3, local, span), jnp.bfloat16)] * len(steps),
            [REMOTE] * 3,
            (far(query_rows), far(key_rows), far(value_rows)),
            [pltpu.SemaphoreType.DMA((len(steps), 3))],
        )
        landed += [swap(block, step) if step else near(block) for block, step in zip(blocks, steps)]
    proj_rows = launch(
        slice_body,
        pltpu.VMEM((span, C_LAT), jnp.bfloat16),
        [REMOTE],
        (far(proj_weight),),
        [pltpu.SemaphoreType.DMA(())],
    )
    half = devices // 2
    quarter = devices // 4
    keep, send, mid_near = launch(
        functools.partial(attend_body, order=order),
        [
            sums_shape(half, local, jnp.float32),
            sums_shape(half, local, jnp.bfloat16),
            pltpu.VMEM((27 * own, CH), jnp.bfloat16),
        ],
        [REMOTE] + [LOCAL] * (1 + devices),
        (
            far(mid_weight.transpose(0, 1, 2, 4, 3).reshape(27 * own, CH)),
            near(proj_rows),
            *landed,
        ),
        [pltpu.SemaphoreType.DMA(())],
        32,
    )
    keep, send = launch(
        functools.partial(fold_body, count=half, split=True),
        [sums_shape(quarter, local, jnp.float32), sums_shape(quarter, local, jnp.bfloat16)],
        [LOCAL] * 2,
        (near(keep), swap(send, 1)),
    )
    keep, send = launch(
        functools.partial(fold_body, count=quarter, split=False),
        [sums_shape(quarter, local, jnp.float32), sums_shape(quarter, local, jnp.bfloat16)],
        [LOCAL] * 2,
        (near(keep), swap(send, 2)),
    )
    gots = []
    for step in range(1, quarter):
        gots.append(swap(send, 4 * step))
    ready = launch(
        latents_body,
        pltpu.VMEM((quarter * local, C_LAT), jnp.bfloat16),
        [LOCAL] * (1 + len(gots)),
        (near(keep), *gots),
    )
    paired = swap(ready, 2)
    columns = launch(
        convolve_body,
        pltpu.VMEM((devices, 16, 128), jnp.bfloat16),
        [LOCAL] * 8,
        (
            near(in_weight.reshape(27 * C_LAT, CH)),
            near(in_bias.reshape(1, CH)),
            near(mid_near),
            near(mid_bias.reshape(1, CH)),
            near(ready),
            swap(ready, 1),
            paired,
            swap(paired, 1),
        ),
        [
            pltpu.VMEM((devices * local, C_LAT), jnp.bfloat16),
            pltpu.VMEM((F * frame, 9 * C_LAT), jnp.bfloat16),
        ],
        32,
    )
    arrived = lax.all_to_all(columns, "seq", split_axis=0, concat_axis=0, tiled=True)
    return pl.pallas_call(
        shuffle_body,
        out_shape=jax.ShapeDtypeStruct((1, F, 2, 2 * W, C_LAT), jnp.bfloat16),
        in_specs=[LOCAL],
        out_specs=LOCAL,
        scratch_shapes=[pltpu.VMEM((F, 2, 2 * W, C_LAT), jnp.float32)],
        compiler_params=pltpu.CompilerParams(vmem_limit_bytes=8 << 20),
        name="shuffle",
    )(near(arrived))


def local_heads(devices):
    return 16 <= devices <= HEADS and devices & (devices - 1) == 0


def on_device(*operands):
    if not local_heads(lax.axis_size("seq")):
        return shared_heads(*operands)
    return whole_heads(*operands)


def solution(mesh):
    whole = jax.shard_map(
        on_device,
        mesh=mesh,
        in_specs=(
            P(("groups", "seq"), None),
            P(("groups", "seq"), None),
            P(("groups", "seq"), None),
            P(),
            P(),
            P(),
            P(None, None, None, None, "seq"),
            P(),
        ),
        out_specs=P(("groups", "seq"), None, None, None, None),
        check_vma=False,
    )
    devices = mesh.shape["seq"]
    if not local_heads(devices):
        return whole
    return whole
```

profile of v0, /device:TPU:0, one launch (start us, length us, event | category | flops | bytes accessed | tf_op | source)
XLA Modules:
  0.0 69.8 jit_solution(5178941427170709771)
XLA Ops:
  0.0 1.0 %shard_map.83 = (bf16[3,48,256]{2,1,0:T(8,128)(2,1)S(1)}, bf16[3,48,256]{2,1,0:T(8,128)(2,1)S(1)}) custom-call(bf16[48,4096]{1,0:T(8,128)(2,1)} %query_ref.3, bf16[48,4096]{1,0:T(8,128)(2,1)} %key_ref.3, bf16[48,4096]{1,0:T(8,128)(2,1)} %value_ref.3), custom_call_target="tpu_custom_call" | custom-call | tf_op jit(solution)/shard_map/pallas_call | solution.py:391
  1.0 4.1 %collective-permute-start = (bf16[3,48,256]{2,1,0:T(8,128)(2,1)S(1)}, bf16[3,48,256]{2,1,0:T(8,128)(2,1)S(1)}, u32[]{:S(2)}, u32[]{:S(2)}) collective-permute-start(bf16[3,48,256]{2,1,0:T(8,128)(2,1)S(1)} %get-tuple-element.28), channel_id=1, source_target_pairs={{0,8},{1,9},{2,10},{3,11},{4,12},{5,13},{6,14},{7,15},{8,0},{9,1},... | collective-permute-start | bytes 221192 | tf_op jit(solution)/shard_map/ppermute | solution.py:411
  5.2 0.0 collective-permute-start.1
  5.2 1.6 %shard_map.84 = (bf16[3,48,256]{2,1,0:T(8,128)(2,1)S(1)}, bf16[3,48,256]{2,1,0:T(8,128)(2,1)S(1)}, bf16[3,48,256]{2,1,0:T(8,128)(2,1)S(1)}, bf16[3,48,256]{2,1,0...) custom-call(bf16[48,4096]{1,0:T(8,128)(2,1)} %query_ref.3, ...), custom_call_target="tpu_custom_call" | custom-call | tf_op jit(solution)/shard_map/pallas_call | solution.py:391
  6.8 0.3 collective-permute-start.2
  7.0 1.8 %collective-permute-start.3 = (bf16[3,48,256]{2,1,0:T(8,128)(2,1)S(1)}, bf16[3,48,256]{2,1,0:T(8,128)(2,1)S(1)}, u32[]{:S(2)}, u32[]{:S(2)}) collective-permute-start(bf16[3,48,256]{2,1,0:T(8,128)(2,1)S(1)} %get-tuple-element.31), channel_id=1, source_target_pairs={{0,2},{1,3},{2,0},{3,1},{4,6},{5,7},{6,4},{7,5},{8,10},{9,11},{10,... | collective-permute-start | bytes 221192 | tf_op jit(solution)/shard_map/ppermute | solution.py:411
  8.8 2.5 %collective-permute-start.4 = (bf16[3,48,256]{2,1,0:T(8,128)(2,1)S(1)}, bf16[3,48,256]{2,1,0:T(8,128)(2,1)S(1)}, u32[]{:S(2)}, u32[]{:S(2)}) collective-permute-start(bf16[3,48,256]{2,1,0:T(8,128)(2,1)S(1)} %get-tuple-element.32), channel_id=1, source_target_pairs={{0,10},{1,11},{2,8},{3,9},{4,14},{5,15},{6,12},{7,13},{8,2},{9,3},... | collective-permute-start | bytes 221192 | tf_op jit(solution)/shard_map/ppermute | solution.py:411
  11.3 0.0 collective-permute-done.rest_0_
  11.3 0.6 collective-permute-start.5
  11.9 0.0 collective-permute-done.1.rest_1_
  11.9 0.7 collective-permute-start.6
  12.6 3.6 %collective-permute-start.7 = (bf16[3,48,256]{2,1,0:T(8,128)(2,1)S(1)}, bf16[3,48,256]{2,1,0:T(8,128)(2,1)S(1)}, u32[]{:S(2)}, u32[]{:S(2)}) collective-permute-start(bf16[3,48,256]{2,1,0:T(8,128)(2,1)S(1)} %get-tuple-element.35), channel_id=1, source_target_pairs={{0,4},{1,5},{2,6},{3,7},{4,0},{5,1},{6,2},{7,3},{8,12},{9,13},{10,... | collective-permute-start | bytes 221192 | tf_op jit(solution)/shard_map/ppermute | solution.py:411
  16.2 0.7 collective-permute-start.8
  16.9 3.2 %collective-permute-done.4.rest_4_ = bf16[3,48,256]{2,1,0:T(8,128)(2,1)S(1)} collective-permute-done((bf16[3,48,256]{2,1,0:T(8,128)(2,1)S(1)}, bf16[3,48,256]{2,1,0:T(8,128)(2,1)S(1)}, u32[]{:S(2)}, u32[]{:S(2)}) %collective-permute-start.4) | collective-permute-done | bytes 73760 | tf_op jit(solution)/shard_map/ppermute | solution.py:411
  20.1 0.8 %collective-permute-start.10 = (bf16[3,48,256]{2,1,0:T(8,128)(2,1)S(1)}, bf16[3,48,256]{2,1,0:T(8,128)(2,1)S(1)}, u32[]{:S(2)}, u32[]{:S(2)}) collective-permute-start(bf16[3,48,256]{2,1,0:T(8,128)(2,1)S(1)} %get-tuple-element.38), channel_id=1, source_target_pairs={{0,13},{1,12},{2,15},{3,14},{4,9},{5,8},{6,11},{7,10},{8,5},{9,4},... | collective-permute-start | bytes 221192 | tf_op jit(solution)/shard_map/ppermute | solution.py:411
  21.0 1.5 %collective-permute-start.11 = (bf16[3,48,256]{2,1,0:T(8,128)(2,1)S(1)}, bf16[3,48,256]{2,1,0:T(8,128)(2,1)S(1)}, u32[]{:S(2)}, u32[]{:S(2)}) collective-permute-start(bf16[3,48,256]{2,1,0:T(8,128)(2,1)S(1)} %get-tuple-element.39), channel_id=1, source_target_pairs={{0,6},{1,7},{2,4},{3,5},{4,2},{5,3},{6,0},{7,1},{8,14},{9,15},{10,... | collective-permute-start | bytes 221192 | tf_op jit(solution)/shard_map/ppermute | solution.py:411
  22.5 0.0 collective-permute-done.7.rest_7_
  22.5 3.6 %collective-permute-start.12 = (bf16[3,48,256]{2,1,0:T(8,128)(2,1)S(1)}, bf16[3,48,256]{2,1,0:T(8,128)(2,1)S(1)}, u32[]{:S(2)}, u32[]{:S(2)}) collective-permute-start(bf16[3,48,256]{2,1,0:T(8,128)(2,1)S(1)} %get-tuple-element.40), channel_id=1, source_target_pairs={{0,14},{1,15},{2,12},{3,13},{4,10},{5,11},{6,8},{7,9},{8,6},{9,7},... | collective-permute-start | bytes 221192 | tf_op jit(solution)/shard_map/ppermute | solution.py:411
  26.1 0.0 collective-permute-done.8.rest_8_
  26.1 0.0 collective-permute-start.13
  26.1 2.9 %collective-permute-start.14 = (bf16[3,48,256]{2,1,0:T(8,128)(2,1)S(1)}, bf16[3,48,256]{2,1,0:T(8,128)(2,1)S(1)}, u32[]{:S(2)}, u32[]{:S(2)}) collective-permute-start(bf16[3,48,256]{2,1,0:T(8,128)(2,1)S(1)} %get-tuple-element.42), channel_id=1, source_target_pairs={{0,15},{1,14},{2,13},{3,12},{4,11},{5,10},{6,9},{7,8},{8,7},{9,6},... | collective-permute-start | bytes 221192 | tf_op jit(solution)/shard_map/ppermute | solution.py:411
  28.9 0.8 %shard_map.82.proj_ref = bf16[256,128]{1,0:T(8,128)(2,1)S(1)} custom-call(bf16[4096,128]{1,0:T(8,128)(2,1)} %proj_ref.1), custom_call_target="tpu_custom_call" | custom-call | tf_op jit(solution)/shard_map/pallas_call | solution.py:391
  29.8 0.0 collective-permute-done.10.rest_10_
  29.8 0.0 collective-permute-done.11.rest_11_
  29.8 0.6 collective-permute-done.12.rest_12_
  30.4 1.3 %collective-permute-done.13.rest_13_ = bf16[3,48,256]{2,1,0:T(8,128)(2,1)S(1)} collective-permute-done((bf16[3,48,256]{2,1,0:T(8,128)(2,1)S(1)}, bf16[3,48,256]{2,1,0:T(8,128)(2,1)S(1)}, u32[]{:S(2)}, u32[]{:S(2)}) %collective-permute-start.13) | collective-permute-done | bytes 73760 | tf_op jit(solution)/shard_map/ppermute | solution.py:411
  31.7 1.7 %collective-permute-done.14.rest_14_ = bf16[3,48,256]{2,1,0:T(8,128)(2,1)S(1)} collective-permute-done((bf16[3,48,256]{2,1,0:T(8,128)(2,1)S(1)}, bf16[3,48,256]{2,1,0:T(8,128)(2,1)S(1)}, u32[]{:S(2)}, u32[]{:S(2)}) %collective-permute-start.14) | collective-permute-done | bytes 73760 | tf_op jit(solution)/shard_map/ppermute | solution.py:411
  33.5 2.4 %shard_map.85 = (f32[392,128]{1,0:T(8,128)S(1)}, bf16[400,128]{1,0:T(8,128)(2,1)S(1)}, bf16[864,512]{1,0:T(8,128)(2,1)S(1)}) custom-call(bf16[864,512]{1,0:T(8,128)(2,1)} %bitcast.9, bf16[256,128]{1,0:T(8,128)(2,1)S(1)} %shard_map.82.proj_ref, bf16[3,48,256]{2,1,0:T(8,128)(2,1)S(1)} %collective-permute-done.rest_0_, ...), custom_call_target="tpu_custom_call" | custom-call | tf_op jit(solution)/shard_map/pallas_call | solution.py:391
  35.9 0.1 collective-permute-start.15
  36.1 1.2 %collective-permute-done.15.got_ref = bf16[400,128]{1,0:T(8,128)(2,1)S(1)} collective-permute-done((bf16[400,128]{1,0:T(8,128)(2,1)S(1)}, bf16[400,128]{1,0:T(8,128)(2,1)S(1)}, u32[]{:S(2)}, u32[]{:S(2)}) %collective-permute-start.15) | collective-permute-done | bytes 102432 | tf_op jit(solution)/shard_map/ppermute | solution.py:411
  37.3 0.9 %collective-permute-start.16 = (bf16[200,128]{1,0:T(8,128)(2,1)S(1)}, bf16[200,128]{1,0:T(8,128)(2,1)S(1)}, u32[]{:S(2)}, u32[]{:S(2)}) collective-permute-start(bf16[200,128]{1,0:T(8,128)(2,1)S(1)} %get-tuple-element.48), channel_id=1, source_target_pairs={{0,2},{1,3},{2,0},{3,1},{4,6},{5,7},{6,4},{7,5},{8,10},{9,11},{10,... | collective-permute-start | bytes 153608 | tf_op jit(solution)/shard_map/ppermute | solution.py:411
  38.3 3.2 %collective-permute-done.16.got_ref = bf16[200,128]{1,0:T(8,128)(2,1)S(1)} collective-permute-done((bf16[200,128]{1,0:T(8,128)(2,1)S(1)}, bf16[200,128]{1,0:T(8,128)(2,1)S(1)}, u32[]{:S(2)}, u32[]{:S(2)}) %collective-permute-start.16) | collective-permute-done | bytes 51232 | tf_op jit(solution)/shard_map/ppermute | solution.py:411
  41.5 2.0 %collective-permute-start.19 = (bf16[200,128]{1,0:T(8,128)(2,1)S(1)}, bf16[200,128]{1,0:T(8,128)(2,1)S(1)}, u32[]{:S(2)}, u32[]{:S(2)}) collective-permute-start(bf16[200,128]{1,0:T(8,128)(2,1)S(1)} %get-tuple-element.50), channel_id=1, source_target_pairs={{0,12},{1,13},{2,14},{3,15},{4,8},{5,9},{6,10},{7,11},{8,4},{9,5},... | collective-permute-start | bytes 153608 | tf_op jit(solution)/shard_map/ppermute | solution.py:411
  43.5 0.2 collective-permute-start.18
  43.7 2.3 %collective-permute-start.17 = (bf16[200,128]{1,0:T(8,128)(2,1)S(1)}, bf16[200,128]{1,0:T(8,128)(2,1)S(1)}, u32[]{:S(2)}, u32[]{:S(2)}) collective-permute-start(bf16[200,128]{1,0:T(8,128)(2,1)S(1)} %get-tuple-element.50), channel_id=1, source_target_pairs={{0,4},{1,5},{2,6},{3,7},{4,0},{5,1},{6,2},{7,3},{8,12},{9,13},{10,... | collective-permute-start | bytes 153608 | tf_op jit(solution)/shard_map/ppermute | solution.py:411
  46.0 2.1 %collective-permute-done.19.rest_2_ = bf16[200,128]{1,0:T(8,128)(2,1)S(1)} collective-permute-done((bf16[200,128]{1,0:T(8,128)(2,1)S(1)}, bf16[200,128]{1,0:T(8,128)(2,1)S(1)}, u32[]{:S(2)}, u32[]{:S(2)}) %collective-permute-start.19) | collective-permute-done | bytes 51232 | tf_op jit(solution)/shard_map/ppermute | solution.py:411
  48.1 1.0 %collective-permute-done.18.rest_1_ = bf16[200,128]{1,0:T(8,128)(2,1)S(1)} collective-permute-done((bf16[200,128]{1,0:T(8,128)(2,1)S(1)}, bf16[200,128]{1,0:T(8,128)(2,1)S(1)}, u32[]{:S(2)}, u32[]{:S(2)}) %collective-permute-start.18) | collective-permute-done | bytes 51232 | tf_op jit(solution)/shard_map/ppermute | solution.py:411
  49.1 0.0 collective-permute-done.17.rest_0_
  49.1 0.1 shard_map.88.rest_0_
  49.3 1.2 %collective-permute-start.21 = (bf16[192,128]{1,0:T(8,128)(2,1)S(1)}, bf16[192,128]{1,0:T(8,128)(2,1)S(1)}, u32[]{:S(2)}, u32[]{:S(2)}) collective-permute-start(bf16[192,128]{1,0:T(8,128)(2,1)S(1)} %shard_map.88.rest_0_), channel_id=1, source_target_pairs={{0,2},{1,3},{2,0},{3,1},{4,6},{5,7},{6,4},{7,5},{8,10},{9,11},{10,... | collective-permute-start | bytes 147464 | tf_op jit(solution)/shard_map/ppermute | solution.py:411
  50.5 0.0 collective-permute-start.20
  50.5 3.0 %collective-permute-done.21.rest_2_ = bf16[192,128]{1,0:T(8,128)(2,1)S(1)} collective-permute-done((bf16[192,128]{1,0:T(8,128)(2,1)S(1)}, bf16[192,128]{1,0:T(8,128)(2,1)S(1)}, u32[]{:S(2)}, u32[]{:S(2)}) %collective-permute-start.21) | collective-permute-done | bytes 49184 | tf_op jit(solution)/shard_map/ppermute | solution.py:411
  53.4 0.0 collective-permute-start.22
  53.4 0.0 collective-permute-done.20.rest_1_
  53.4 1.2 %collective-permute-done.22.rest_3_ = bf16[192,128]{1,0:T(8,128)(2,1)S(1)} collective-permute-done((bf16[192,128]{1,0:T(8,128)(2,1)S(1)}, bf16[192,128]{1,0:T(8,128)(2,1)S(1)}, u32[]{:S(2)}, u32[]{:S(2)}) %collective-permute-start.22) | collective-permute-done | bytes 49184 | tf_op jit(solution)/shard_map/ppermute | solution.py:411
  54.7 3.5 %shard_map.89 = bf16[16,16,128]{2,1,0:T(8,128)(2,1)S(1)} custom-call(bf16[3456,512]{1,0:T(8,128)(2,1)S(1)} %bitcast.6, f32[1,512]{1,0:T(1,128)S(1)} %bitcast.7, bf16[864,512]{1,0:T(8,128)(2,1)S(1)} %get-tuple-element.44.mid_weight_ref, f32[1,512]{1,0:T(1,128)S(1)} %bitcast.8, bf16[192,128]{1,0:T(8,128)(2,1)S(1)} %shard_map.88.rest_0_, ...), custom_call_target="tpu_custom_call" | custom-call | tf_op jit(solution)/shard_map/pallas_call | solution.py:391
  58.2 10.7 %all_to_all.5.rows_ref = bf16[16,16,128]{2,1,0:T(8,128)(2,1)S(1)} all-to-all(bf16[16,16,128]{2,1,0:T(8,128)(2,1)S(1)} %shard_map.89), channel_id=1, replica_groups=mesh['groups'=2,'seq'=16] {'seq'}, dimensions={0} | all-to-all | bytes 131072 | tf_op jit(solution)/shard_map/all_to_all | solution.py:506
  68.9 0.9 %shuffle.1 = bf16[1,2,2,48,128]{4,3,2,1,0:T(8,128)(2,1)} custom-call(bf16[16,16,128]{2,1,0:T(8,128)(2,1)S(1)} %all_to_all.5.rows_ref), custom_call_target="tpu_custom_call" | custom-call | tf_op jit(solution)/shard_map/shuffle/pallas_call | solution.py:507
  (14 shorter events, 0.1 us)
Async XLA Ops:
  0.0 54.6 %copy-start.2 = (f32[512]{0:T(512)S(1)}, f32[512]{0:T(512)}, u32[]{:S(2)}) copy-start(f32[512]{0:T(512)} %param.15) | copy-start | bytes 6148
  0.0 54.6 %copy-start.1 = (f32[512]{0:T(512)S(1)}, f32[512]{0:T(512)}, u32[]{:S(2)}) copy-start(f32[512]{0:T(512)} %param.13) | copy-start | bytes 6148
  0.0 54.6 %copy-start = (bf16[3,3,3,128,512]{4,3,2,1,0:T(8,128)(2,1)S(1)}, bf16[3,3,3,128,512]{4,3,2,1,0:T(8,128)(2,1)}, u32[]{:S(2)}) copy-start(bf16[3,3,3,128,512]{4,3,2,1,0:T(8,128)(2,1)} %param.12) | copy-start | bytes 10616836
  1.0 10.3 %collective-permute-start = (bf16[3,48,256]{2,1,0:T(8,128)(2,1)S(1)}, bf16[3,48,256]{2,1,0:T(8,128)(2,1)S(1)}, u32[]{:S(2)}, u32[]{:S(2)}) collective-permute-start(bf16[3,48,256]{2,1,0:T(8,128)(2,1)S(1)} %get-tuple-element.28), channel_id=1, source_target_pairs={{0,8},{1,9},{2,10},{3,11},{4,12},{5,13},{6,14},{7,15},{8,0},{9,1},... | collective-permute-start | bytes 221192 | tf_op jit(solution)/shard_map/ppermute | solution.py:411
  5.2 6.7 %collective-permute-start.1 = (bf16[3,48,256]{2,1,0:T(8,128)(2,1)S(1)}, bf16[3,48,256]{2,1,0:T(8,128)(2,1)S(1)}, u32[]{:S(2)}, u32[]{:S(2)}) collective-permute-start(bf16[3,48,256]{2,1,0:T(8,128)(2,1)S(1)} %get-tuple-element.29), channel_id=1, source_target_pairs={{0,1},{1,0},{2,3},{3,2},{4,5},{5,4},{6,7},{7,6},{8,9},{9,8},{10,11... | collective-permute-start | bytes 221192 | tf_op jit(solution)/shard_map/ppermute | solution.py:411
  6.8 5.8 %collective-permute-start.2 = (bf16[3,48,256]{2,1,0:T(8,128)(2,1)S(1)}, bf16[3,48,256]{2,1,0:T(8,128)(2,1)S(1)}, u32[]{:S(2)}, u32[]{:S(2)}) collective-permute-start(bf16[3,48,256]{2,1,0:T(8,128)(2,1)S(1)} %get-tuple-element.30), channel_id=1, source_target_pairs={{0,9},{1,8},{2,11},{3,10},{4,13},{5,12},{6,15},{7,14},{8,1},{9,0},... | collective-permute-start | bytes 221192 | tf_op jit(solution)/shard_map/ppermute | solution.py:411
  7.0 9.2 %collective-permute-start.3 = (bf16[3,48,256]{2,1,0:T(8,128)(2,1)S(1)}, bf16[3,48,256]{2,1,0:T(8,128)(2,1)S(1)}, u32[]{:S(2)}, u32[]{:S(2)}) collective-permute-start(bf16[3,48,256]{2,1,0:T(8,128)(2,1)S(1)} %get-tuple-element.31), channel_id=1, source_target_pairs={{0,2},{1,3},{2,0},{3,1},{4,6},{5,7},{6,4},{7,5},{8,10},{9,11},{10,... | collective-permute-start | bytes 221192 | tf_op jit(solution)/shard_map/ppermute | solution.py:411
  8.8 11.3 %collective-permute-start.4 = (bf16[3,48,256]{2,1,0:T(8,128)(2,1)S(1)}, bf16[3,48,256]{2,1,0:T(8,128)(2,1)S(1)}, u32[]{:S(2)}, u32[]{:S(2)}) collective-permute-start(bf16[3,48,256]{2,1,0:T(8,128)(2,1)S(1)} %get-tuple-element.32), channel_id=1, source_target_pairs={{0,10},{1,11},{2,8},{3,9},{4,14},{5,15},{6,12},{7,13},{8,2},{9,3},... | collective-permute-start | bytes 221192 | tf_op jit(solution)/shard_map/ppermute | solution.py:411
  11.3 8.8 %collective-permute-start.5 = (bf16[3,48,256]{2,1,0:T(8,128)(2,1)S(1)}, bf16[3,48,256]{2,1,0:T(8,128)(2,1)S(1)}, u32[]{:S(2)}, u32[]{:S(2)}) collective-permute-start(bf16[3,48,256]{2,1,0:T(8,128)(2,1)S(1)} %get-tuple-element.33), channel_id=1, source_target_pairs={{0,3},{1,2},{2,1},{3,0},{4,7},{5,6},{6,5},{7,4},{8,11},{9,10},{10,... | collective-permute-start | bytes 221192 | tf_op jit(solution)/shard_map/ppermute | solution.py:411
  11.9 9.1 %collective-permute-start.6 = (bf16[3,48,256]{2,1,0:T(8,128)(2,1)S(1)}, bf16[3,48,256]{2,1,0:T(8,128)(2,1)S(1)}, u32[]{:S(2)}, u32[]{:S(2)}) collective-permute-start(bf16[3,48,256]{2,1,0:T(8,128)(2,1)S(1)} %get-tuple-element.34), channel_id=1, source_target_pairs={{0,11},{1,10},{2,9},{3,8},{4,15},{5,14},{6,13},{7,12},{8,3},{9,2},... | collective-permute-start | bytes 221192 | tf_op jit(solution)/shard_map/ppermute | solution.py:411
  12.6 9.9 %collective-permute-start.7 = (bf16[3,48,256]{2,1,0:T(8,128)(2,1)S(1)}, bf16[3,48,256]{2,1,0:T(8,128)(2,1)S(1)}, u32[]{:S(2)}, u32[]{:S(2)}) collective-permute-start(bf16[3,48,256]{2,1,0:T(8,128)(2,1)S(1)} %get-tuple-element.35), channel_id=1, source_target_pairs={{0,4},{1,5},{2,6},{3,7},{4,0},{5,1},{6,2},{7,3},{8,12},{9,13},{10,... | collective-permute-start | bytes 221192 | tf_op jit(solution)/shard_map/ppermute | solution.py:411
  16.2 9.8 %collective-permute-start.8 = (bf16[3,48,256]{2,1,0:T(8,128)(2,1)S(1)}, bf16[3,48,256]{2,1,0:T(8,128)(2,1)S(1)}, u32[]{:S(2)}, u32[]{:S(2)}) collective-permute-start(bf16[3,48,256]{2,1,0:T(8,128)(2,1)S(1)} %get-tuple-element.36), channel_id=1, source_target_pairs={{0,12},{1,13},{2,14},{3,15},{4,8},{5,9},{6,10},{7,11},{8,4},{9,5},... | collective-permute-start | bytes 221192 | tf_op jit(solution)/shard_map/ppermute | solution.py:411
  20.1 5.9 %collective-permute-start.9 = (bf16[3,48,256]{2,1,0:T(8,128)(2,1)S(1)}, bf16[3,48,256]{2,1,0:T(8,128)(2,1)S(1)}, u32[]{:S(2)}, u32[]{:S(2)}) collective-permute-start(bf16[3,48,256]{2,1,0:T(8,128)(2,1)S(1)} %get-tuple-element.37), channel_id=1, source_target_pairs={{0,5},{1,4},{2,7},{3,6},{4,1},{5,0},{6,3},{7,2},{8,13},{9,12},{10,... | collective-permute-start | bytes 221192 | tf_op jit(solution)/shard_map/ppermute | solution.py:411
  20.1 9.7 %collective-permute-start.10 = (bf16[3,48,256]{2,1,0:T(8,128)(2,1)S(1)}, bf16[3,48,256]{2,1,0:T(8,128)(2,1)S(1)}, u32[]{:S(2)}, u32[]{:S(2)}) collective-permute-start(bf16[3,48,256]{2,1,0:T(8,128)(2,1)S(1)} %get-tuple-element.38), channel_id=1, source_target_pairs={{0,13},{1,12},{2,15},{3,14},{4,9},{5,8},{6,11},{7,10},{8,5},{9,4},... | collective-permute-start | bytes 221192 | tf_op jit(solution)/shard_map/ppermute | solution.py:411
  21.0 8.9 %collective-permute-start.11 = (bf16[3,48,256]{2,1,0:T(8,128)(2,1)S(1)}, bf16[3,48,256]{2,1,0:T(8,128)(2,1)S(1)}, u32[]{:S(2)}, u32[]{:S(2)}) collective-permute-start(bf16[3,48,256]{2,1,0:T(8,128)(2,1)S(1)} %get-tuple-element.39), channel_id=1, source_target_pairs={{0,6},{1,7},{2,4},{3,5},{4,2},{5,3},{6,0},{7,1},{8,14},{9,15},{10,... | collective-permute-start | bytes 221192 | tf_op jit(solution)/shard_map/ppermute | solution.py:411
  22.5 7.9 %collective-permute-start.12 = (bf16[3,48,256]{2,1,0:T(8,128)(2,1)S(1)}, bf16[3,48,256]{2,1,0:T(8,128)(2,1)S(1)}, u32[]{:S(2)}, u32[]{:S(2)}) collective-permute-start(bf16[3,48,256]{2,1,0:T(8,128)(2,1)S(1)} %get-tuple-element.40), channel_id=1, source_target_pairs={{0,14},{1,15},{2,12},{3,13},{4,10},{5,11},{6,8},{7,9},{8,6},{9,7},... | collective-permute-start | bytes 221192 | tf_op jit(solution)/shard_map/ppermute | solution.py:411
  26.1 5.7 %collective-permute-start.13 = (bf16[3,48,256]{2,1,0:T(8,128)(2,1)S(1)}, bf16[3,48,256]{2,1,0:T(8,128)(2,1)S(1)}, u32[]{:S(2)}, u32[]{:S(2)}) collective-permute-start(bf16[3,48,256]{2,1,0:T(8,128)(2,1)S(1)} %get-tuple-element.41), channel_id=1, source_target_pairs={{0,7},{1,6},{2,5},{3,4},{4,3},{5,2},{6,1},{7,0},{8,15},{9,14},{10,... | collective-permute-start | bytes 221192 | tf_op jit(solution)/shard_map/ppermute | solution.py:411
  26.1 7.4 %collective-permute-start.14 = (bf16[3,48,256]{2,1,0:T(8,128)(2,1)S(1)}, bf16[3,48,256]{2,1,0:T(8,128)(2,1)S(1)}, u32[]{:S(2)}, u32[]{:S(2)}) collective-permute-start(bf16[3,48,256]{2,1,0:T(8,128)(2,1)S(1)} %get-tuple-element.42), channel_id=1, source_target_pairs={{0,15},{1,14},{2,13},{3,12},{4,11},{5,10},{6,9},{7,8},{8,7},{9,6},... | collective-permute-start | bytes 221192 | tf_op jit(solution)/shard_map/ppermute | solution.py:411
  35.9 1.4 %collective-permute-start.15 = (bf16[400,128]{1,0:T(8,128)(2,1)S(1)}, bf16[400,128]{1,0:T(8,128)(2,1)S(1)}, u32[]{:S(2)}, u32[]{:S(2)}) collective-permute-start(bf16[400,128]{1,0:T(8,128)(2,1)S(1)} %get-tuple-element.46), channel_id=1, source_target_pairs={{0,1},{1,0},{2,3},{3,2},{4,5},{5,4},{6,7},{7,6},{8,9},{9,8},{10,11... | collective-permute-start | bytes 307208 | tf_op jit(solution)/shard_map/ppermute | solution.py:411
  37.3 4.2 %collective-permute-start.16 = (bf16[200,128]{1,0:T(8,128)(2,1)S(1)}, bf16[200,128]{1,0:T(8,128)(2,1)S(1)}, u32[]{:S(2)}, u32[]{:S(2)}) collective-permute-start(bf16[200,128]{1,0:T(8,128)(2,1)S(1)} %get-tuple-element.48), channel_id=1, source_target_pairs={{0,2},{1,3},{2,0},{3,1},{4,6},{5,7},{6,4},{7,5},{8,10},{9,11},{10,... | collective-permute-start | bytes 153608 | tf_op jit(solution)/shard_map/ppermute | solution.py:411
  41.5 6.6 %collective-permute-start.19 = (bf16[200,128]{1,0:T(8,128)(2,1)S(1)}, bf16[200,128]{1,0:T(8,128)(2,1)S(1)}, u32[]{:S(2)}, u32[]{:S(2)}) collective-permute-start(bf16[200,128]{1,0:T(8,128)(2,1)S(1)} %get-tuple-element.50), channel_id=1, source_target_pairs={{0,12},{1,13},{2,14},{3,15},{4,8},{5,9},{6,10},{7,11},{8,4},{9,5},... | collective-permute-start | bytes 153608 | tf_op jit(solution)/shard_map/ppermute | solution.py:411
  43.5 5.6 %collective-permute-start.18 = (bf16[200,128]{1,0:T(8,128)(2,1)S(1)}, bf16[200,128]{1,0:T(8,128)(2,1)S(1)}, u32[]{:S(2)}, u32[]{:S(2)}) collective-permute-start(bf16[200,128]{1,0:T(8,128)(2,1)S(1)} %get-tuple-element.50), channel_id=1, source_target_pairs={{0,8},{1,9},{2,10},{3,11},{4,12},{5,13},{6,14},{7,15},{8,0},{9,1},... | collective-permute-start | bytes 153608 | tf_op jit(solution)/shard_map/ppermute | solution.py:411
  43.7 5.4 %collective-permute-start.17 = (bf16[200,128]{1,0:T(8,128)(2,1)S(1)}, bf16[200,128]{1,0:T(8,128)(2,1)S(1)}, u32[]{:S(2)}, u32[]{:S(2)}) collective-permute-start(bf16[200,128]{1,0:T(8,128)(2,1)S(1)} %get-tuple-element.50), channel_id=1, source_target_pairs={{0,4},{1,5},{2,6},{3,7},{4,0},{5,1},{6,2},{7,3},{8,12},{9,13},{10,... | collective-permute-start | bytes 153608 | tf_op jit(solution)/shard_map/ppermute | solution.py:411
  49.3 4.2 %collective-permute-start.21 = (bf16[192,128]{1,0:T(8,128)(2,1)S(1)}, bf16[192,128]{1,0:T(8,128)(2,1)S(1)}, u32[]{:S(2)}, u32[]{:S(2)}) collective-permute-start(bf16[192,128]{1,0:T(8,128)(2,1)S(1)} %shard_map.88.rest_0_), channel_id=1, source_target_pairs={{0,2},{1,3},{2,0},{3,1},{4,6},{5,7},{6,4},{7,5},{8,10},{9,11},{10,... | collective-permute-start | bytes 147464 | tf_op jit(solution)/shard_map/ppermute | solution.py:411
  50.5 3.0 %collective-permute-start.20 = (bf16[192,128]{1,0:T(8,128)(2,1)S(1)}, bf16[192,128]{1,0:T(8,128)(2,1)S(1)}, u32[]{:S(2)}, u32[]{:S(2)}) collective-permute-start(bf16[192,128]{1,0:T(8,128)(2,1)S(1)} %shard_map.88.rest_0_), channel_id=1, source_target_pairs={{0,1},{1,0},{2,3},{3,2},{4,5},{5,4},{6,7},{7,6},{8,9},{9,8},{10,11... | collective-permute-start | bytes 147464 | tf_op jit(solution)/shard_map/ppermute | solution.py:411
  53.4 1.2 %collective-permute-start.22 = (bf16[192,128]{1,0:T(8,128)(2,1)S(1)}, bf16[192,128]{1,0:T(8,128)(2,1)S(1)}, u32[]{:S(2)}, u32[]{:S(2)}) collective-permute-start(bf16[192,128]{1,0:T(8,128)(2,1)S(1)} %collective-permute-done.21.rest_2_), channel_id=1, source_target_pairs={{0,1},{1,0},{2,3},{3,2},{4,5},{5,4},{6,7},{7,6},{8,9},{9,8},{10,11... | collective-permute-start | bytes 147464 | tf_op jit(solution)/shard_map/ppermute | solution.py:411
where the time goes:
time: 70.1 us; the launch traced here: 69.8 us
  starting transfers between devices  29.8 us (43%)
  waiting for transfers between devices  18.7 us (27%)
  blocking collectives  10.7 us (15%)
  Pallas kernels  10.4 us (15%)
    ppermute x23, starting transfers between devices, swap(): lax.ppermute(array, 'seq', [(i, i ^ step) for i in range(devices)])  29.8 us
    ppermute x23, waiting for transfers between devices, swap(): lax.ppermute(array, 'seq', [(i, i ^ step) for i in range(devices)])  18.7 us
    all_to_all x1, blocking collectives, whole_heads(): lax.all_to_all(columns, 'seq', split_axis=0, concat_axis=0, tiled=True)  10.7 us
    pallas_call x8, Pallas kernels, launch(): pl.pallas_call(body, out_shape=outs, in_specs=in_specs, out_specs=jax.tre...  9.54 us
  transfers between devices with their start and end apart: 23, of which 10 were waited for; matrix products, arithmetic and copies ran while one was open for 0% of the time, Pallas kernels for 3%

commit v1 on v0

--- a/solution.py
+++ b/solution.py
@@ -173,12 +173,17 @@
         copy.wait()
 
 
-def slice_body(proj_ref, out_ref, sem):
-    span = out_ref.shape[0]
+def fetch_body(proj_ref, mid_weight_ref, rows_ref, mid_ref, sems):
+    span = rows_ref.shape[0]
     start = pl.multiple_of(lax.axis_index("seq") * span, span)
-    copy = pltpu.make_async_copy(proj_ref.at[pl.ds(start, span), :], out_ref, sem)
-    copy.start()
-    copy.wait()
+    copies = (
+        pltpu.make_async_copy(proj_ref.at[pl.ds(start, span), :], rows_ref, sems.at[0]),
+        pltpu.make_async_copy(mid_weight_ref, mid_ref, sems.at[1]),
+    )
+    for copy in copies:
+        copy.start()
+    for copy in copies:
+        copy.wait()
 
 
 def read_sums(ref, count):
@@ -199,10 +204,8 @@
     ref[cells:] = across.astype(ref.dtype)
 
 
-def attend_body(mid_weight_ref, proj_ref, *rest, order):
-    blocks, (keep_ref, send_ref, mid_ref, mid_sem) = rest[:-4], rest[-4:]
-    fetch = pltpu.make_async_copy(mid_weight_ref, mid_ref, mid_sem)
-    fetch.start()
+def attend_body(proj_ref, *rest, order):
+    blocks, (keep_ref, send_ref) = rest[:-2], rest[-2:]
     devices = len(blocks)
     _, local, span = blocks[0].shape
     tokens = devices * local
@@ -229,7 +232,6 @@
     for ref, first in ((keep_ref, 0), (send_ref, 1)):
         chosen = [order.index(step) for step in range(first, devices, 2)]
         write_sums(ref, [partial[i] for i in chosen], [across[i : i + 1] for i in chosen])
-    fetch.wait()
 
 
 def fold_body(keep_ref, got_ref, next_ref, send_ref, count, split):
@@ -274,7 +276,7 @@
             latents_ref[pl.ds(pl.multiple_of(block * local, 16), local), :] = quarter[
                 high * local : (high + 1) * local, :
             ]
-    own = mid_weight_ref.shape[0] // 27
+    own = mid_weight_ref.shape[1] // 9
     column = lax.broadcasted_iota(jnp.int32, (frame, C_LAT), 0) % W
     for index in range(F):
         cells = latents_ref[index * frame : (index + 1) * frame, :].astype(jnp.float32)
@@ -288,32 +290,19 @@
             above = jnp.concatenate([blank, moved[:-W]], axis=0)
             below = jnp.concatenate([moved[W:], blank], axis=0)
             for row_off, piece in enumerate((above, moved, below)):
-                at = (row_off * 3 + col_off) * C_LAT
-                cols[index * frame : (index + 1) * frame, at : at + C_LAT] = piece.astype(
-                    jnp.bfloat16
-                )
+                at = ((index * 3 + row_off) * 3 + col_off) * C_LAT
+                cols[:, at : at + C_LAT] = piece.astype(jnp.bfloat16)
     deep = 9 * C_LAT
-    sums = [None] * F
-    for tap in range(3):
-        low, high = max(0, tap - 1), min(F, F + tap - 1)
-        product = dot_f32(
-            cols[low * frame : high * frame, :], in_weight_ref[tap * deep : (tap + 1) * deep, :]
-        )
-        for index in range(low, high):
-            piece = product[(index - low) * frame : (index - low + 1) * frame]
-            target = index - tap + 1
-            sums[target] = piece if sums[target] is None else sums[target] + piece
-    firsts = [(total + in_bias_ref[...]).astype(jnp.bfloat16) for total in sums]
-    taps = [None] * F
+    firsts = []
+    actives = []
     for index in range(F):
-        wide = firsts[index].astype(jnp.float32)
-        active = (wide * lax.logistic(wide)).astype(jnp.bfloat16)
-        low, high = max(0, index + 2 - F), min(3, index + 2)
-        product = dot_f32(mid_weight_ref[low * 9 * own : high * 9 * own, :], active, 1, 1)
-        for tap in range(low, high):
-            piece = product[(tap - low) * 9 * own : (tap - low + 1) * 9 * own]
-            target = index - tap + 1
-            taps[target] = piece if taps[target] is None else taps[target] + piece
+        low = (F - 1 - index) * deep
+        first = (
+            dot_f32(cols[...], in_weight_ref[low : low + F * deep, :]) + in_bias_ref[...]
+        ).astype(jnp.bfloat16)
+        wide = first.astype(jnp.float32)
+        firsts.append(first)
+        actives.append((wide * lax.logistic(wide)).astype(jnp.bfloat16))
     channel = lax.broadcasted_iota(jnp.int32, (own, CH), 1)
     mine = channel == lax.broadcasted_iota(jnp.int32, (own, CH), 0) + rank * own
     bias = jnp.sum(jnp.where(mine, mid_bias_ref[...], 0.0), axis=1, keepdims=True)
@@ -322,12 +311,16 @@
     spot_column = spot % W
     outs = []
     for index in range(F):
+        taps = sum(
+            dot_f32(mid_weight_ref[source - index + 1], actives[source], 1, 1)
+            for source in range(F)
+        )
         total = None
         for col_off in range(3):
             merged = None
             for row_off in range(3):
                 at = (row_off * 3 + col_off) * own
-                piece = taps[index][at : at + own, :]
+                piece = taps[at : at + own, :]
                 if row_off == 0:
                     piece = jnp.where(spot < W, 0.0, pltpu.roll(piece, W, 1))
                 elif row_off == 2:
@@ -436,30 +429,27 @@
             [pltpu.SemaphoreType.DMA((len(steps), 3))],
         )
         landed += [swap(block, step) if step else near(block) for block, step in zip(blocks, steps)]
-    proj_rows = launch(
-        slice_body,
-        pltpu.VMEM((span, C_LAT), jnp.bfloat16),
-        [REMOTE],
-        (far(proj_weight),),
-        [pltpu.SemaphoreType.DMA(())],
+    proj_rows, mid_near = launch(
+        fetch_body,
+        [
+            pltpu.VMEM((span, C_LAT), jnp.bfloat16),
+            pltpu.VMEM((3, 9 * own, CH), jnp.bfloat16),
+        ],
+        [REMOTE] * 2,
+        (
+            far(proj_weight),
+            far(mid_weight.transpose(0, 1, 2, 4, 3).reshape(3, 9 * own, CH)),
+        ),
+        [pltpu.SemaphoreType.DMA((2,))],
     )
     half = devices // 2
     quarter = devices // 4
-    keep, send, mid_near = launch(
+    keep, send = launch(
         functools.partial(attend_body, order=order),
-        [
-            sums_shape(half, local, jnp.float32),
-            sums_shape(half, local, jnp.bfloat16),
-            pltpu.VMEM((27 * own, CH), jnp.bfloat16),
-        ],
-        [REMOTE] + [LOCAL] * (1 + devices),
-        (
-            far(mid_weight.transpose(0, 1, 2, 4, 3).reshape(27 * own, CH)),
-            near(proj_rows),
-            *landed,
-        ),
-        [pltpu.SemaphoreType.DMA(())],
-        32,
+        [sums_shape(half, local, jnp.float32), sums_shape(half, local, jnp.bfloat16)],
+        [LOCAL] * (1 + devices),
+        (near(proj_rows), *landed),
+        mib=32,
     )
     keep, send = launch(
         functools.partial(fold_body, count=half, split=True),
@@ -499,7 +489,7 @@
         ),
         [
             pltpu.VMEM((devices * local, C_LAT), jnp.bfloat16),
-            pltpu.VMEM((F * frame, 9 * C_LAT), jnp.bfloat16),
+            pltpu.VMEM((frame, F * 9 * C_LAT), jnp.bfloat16),
         ],
         32,
     )

time: 70.1 us -> 69.3 us (0.989)
  transfers between devices with their start and end apart: 23 -> 23, of which waited for: 10 -> 10; matrix products, arithmetic and copies ran while one was open for 0% -> 0% of each run, Pallas kernels for 3% -> 4%
where the time goes in v1:
time: 69.3 us; the launch traced here: 69.1 us
  starting transfers between devices  29.8 us (43%)
  waiting for transfers between devices  18.3 us (26%)
  blocking collectives  10.7 us (15%)
  Pallas kernels  10.2 us (15%)
    ppermute x23, starting transfers between devices, swap(): lax.ppermute(array, 'seq', [(i, i ^ step) for i in range(devices)])  29.8 us
    ppermute x23, waiting for transfers between devices, swap(): lax.ppermute(array, 'seq', [(i, i ^ step) for i in range(devices)])  18.3 us
    all_to_all x1, blocking collectives, whole_heads(): lax.all_to_all(columns, 'seq', split_axis=0, concat_axis=0, tiled=True)  10.7 us
    pallas_call x8, Pallas kernels, launch(): pl.pallas_call(body, out_shape=outs, in_specs=in_specs, out_specs=jax.tre...  9.26 us
  transfers between devices with their start and end apart: 23, of which 10 were waited for; matrix products, arithmetic and copies ran while one was open for 0% of the time, Pallas kernels for 4%

profile of v1, /device:TPU:0, one launch (start us, length us, event | category | flops | bytes accessed | tf_op | source)
XLA Modules:
  0.0 69.1 jit_solution(5914893602734566796)
XLA Ops:
  0.0 1.0 %shard_map.83 = (bf16[3,48,256]{2,1,0:T(8,128)(2,1)S(1)}, bf16[3,48,256]{2,1,0:T(8,128)(2,1)S(1)}) custom-call(bf16[48,4096]{1,0:T(8,128)(2,1)} %query_ref.3, bf16[48,4096]{1,0:T(8,128)(2,1)} %key_ref.3, bf16[48,4096]{1,0:T(8,128)(2,1)} %value_ref.3), custom_call_target="tpu_custom_call" | custom-call | tf_op jit(solution)/shard_map/pallas_call | solution.py:384
  1.0 4.1 %collective-permute-start = (bf16[3,48,256]{2,1,0:T(8,128)(2,1)S(1)}, bf16[3,48,256]{2,1,0:T(8,128)(2,1)S(1)}, u32[]{:S(2)}, u32[]{:S(2)}) collective-permute-start(bf16[3,48,256]{2,1,0:T(8,128)(2,1)S(1)} %get-tuple-element.31), channel_id=1, source_target_pairs={{0,8},{1,9},{2,10},{3,11},{4,12},{5,13},{6,14},{7,15},{8,0},{9,1},... | collective-permute-start | bytes 221192 | tf_op jit(solution)/shard_map/ppermute | solution.py:404
  5.2 0.0 collective-permute-start.1
  5.2 1.6 %shard_map.84 = (bf16[3,48,256]{2,1,0:T(8,128)(2,1)S(1)}, bf16[3,48,256]{2,1,0:T(8,128)(2,1)S(1)}, bf16[3,48,256]{2,1,0:T(8,128)(2,1)S(1)}, bf16[3,48,256]{2,1,0...) custom-call(bf16[48,4096]{1,0:T(8,128)(2,1)} %query_ref.3, ...), custom_call_target="tpu_custom_call" | custom-call | tf_op jit(solution)/shard_map/pallas_call | solution.py:384
  6.8 0.3 collective-permute-start.2
  7.0 1.8 %collective-permute-start.3 = (bf16[3,48,256]{2,1,0:T(8,128)(2,1)S(1)}, bf16[3,48,256]{2,1,0:T(8,128)(2,1)S(1)}, u32[]{:S(2)}, u32[]{:S(2)}) collective-permute-start(bf16[3,48,256]{2,1,0:T(8,128)(2,1)S(1)} %get-tuple-element.34), channel_id=1, source_target_pairs={{0,2},{1,3},{2,0},{3,1},{4,6},{5,7},{6,4},{7,5},{8,10},{9,11},{10,... | collective-permute-start | bytes 221192 | tf_op jit(solution)/shard_map/ppermute | solution.py:404
  8.8 2.5 %collective-permute-start.4 = (bf16[3,48,256]{2,1,0:T(8,128)(2,1)S(1)}, bf16[3,48,256]{2,1,0:T(8,128)(2,1)S(1)}, u32[]{:S(2)}, u32[]{:S(2)}) collective-permute-start(bf16[3,48,256]{2,1,0:T(8,128)(2,1)S(1)} %get-tuple-element.35), channel_id=1, source_target_pairs={{0,10},{1,11},{2,8},{3,9},{4,14},{5,15},{6,12},{7,13},{8,2},{9,3},... | collective-permute-start | bytes 221192 | tf_op jit(solution)/shard_map/ppermute | solution.py:404
  11.3 0.0 collective-permute-done.rest_0_
  11.3 0.6 collective-permute-start.5
  11.9 0.0 collective-permute-done.1.rest_1_
  11.9 0.7 %collective-permute-start.6 = (bf16[3,48,256]{2,1,0:T(8,128)(2,1)S(1)}, bf16[3,48,256]{2,1,0:T(8,128)(2,1)S(1)}, u32[]{:S(2)}, u32[]{:S(2)}) collective-permute-start(bf16[3,48,256]{2,1,0:T(8,128)(2,1)S(1)} %get-tuple-element.37), channel_id=1, source_target_pairs={{0,11},{1,10},{2,9},{3,8},{4,15},{5,14},{6,13},{7,12},{8,3},{9,2},... | collective-permute-start | bytes 221192 | tf_op jit(solution)/shard_map/ppermute | solution.py:404
  12.6 0.0 collective-permute-done.2.rest_2_
  12.6 3.6 %collective-permute-start.7 = (bf16[3,48,256]{2,1,0:T(8,128)(2,1)S(1)}, bf16[3,48,256]{2,1,0:T(8,128)(2,1)S(1)}, u32[]{:S(2)}, u32[]{:S(2)}) collective-permute-start(bf16[3,48,256]{2,1,0:T(8,128)(2,1)S(1)} %get-tuple-element.38), channel_id=1, source_target_pairs={{0,4},{1,5},{2,6},{3,7},{4,0},{5,1},{6,2},{7,3},{8,12},{9,13},{10,... | collective-permute-start | bytes 221192 | tf_op jit(solution)/shard_map/ppermute | solution.py:404
  16.2 0.7 collective-permute-start.8
  16.9 3.2 %collective-permute-done.4.rest_4_ = bf16[3,48,256]{2,1,0:T(8,128)(2,1)S(1)} collective-permute-done((bf16[3,48,256]{2,1,0:T(8,128)(2,1)S(1)}, bf16[3,48,256]{2,1,0:T(8,128)(2,1)S(1)}, u32[]{:S(2)}, u32[]{:S(2)}) %collective-permute-start.4) | collective-permute-done | bytes 73760 | tf_op jit(solution)/shard_map/ppermute | solution.py:404
  20.1 0.8 %collective-permute-start.10 = (bf16[3,48,256]{2,1,0:T(8,128)(2,1)S(1)}, bf16[3,48,256]{2,1,0:T(8,128)(2,1)S(1)}, u32[]{:S(2)}, u32[]{:S(2)}) collective-permute-start(bf16[3,48,256]{2,1,0:T(8,128)(2,1)S(1)} %get-tuple-element.41), channel_id=1, source_target_pairs={{0,13},{1,12},{2,15},{3,14},{4,9},{5,8},{6,11},{7,10},{8,5},{9,4},... | collective-permute-start | bytes 221192 | tf_op jit(solution)/shard_map/ppermute | solution.py:404
  21.0 1.5 %collective-permute-start.11 = (bf16[3,48,256]{2,1,0:T(8,128)(2,1)S(1)}, bf16[3,48,256]{2,1,0:T(8,128)(2,1)S(1)}, u32[]{:S(2)}, u32[]{:S(2)}) collective-permute-start(bf16[3,48,256]{2,1,0:T(8,128)(2,1)S(1)} %get-tuple-element.42), channel_id=1, source_target_pairs={{0,6},{1,7},{2,4},{3,5},{4,2},{5,3},{6,0},{7,1},{8,14},{9,15},{10,... | collective-permute-start | bytes 221192 | tf_op jit(solution)/shard_map/ppermute | solution.py:404
  22.5 0.0 collective-permute-done.7.rest_7_
  22.5 3.6 %collective-permute-start.12 = (bf16[3,48,256]{2,1,0:T(8,128)(2,1)S(1)}, bf16[3,48,256]{2,1,0:T(8,128)(2,1)S(1)}, u32[]{:S(2)}, u32[]{:S(2)}) collective-permute-start(bf16[3,48,256]{2,1,0:T(8,128)(2,1)S(1)} %get-tuple-element.43), channel_id=1, source_target_pairs={{0,14},{1,15},{2,12},{3,13},{4,10},{5,11},{6,8},{7,9},{8,6},{9,7},... | collective-permute-start | bytes 221192 | tf_op jit(solution)/shard_map/ppermute | solution.py:404
  26.1 0.0 collective-permute-done.8.rest_8_
  26.1 0.0 collective-permute-start.13
  26.1 2.9 %collective-permute-start.14 = (bf16[3,48,256]{2,1,0:T(8,128)(2,1)S(1)}, bf16[3,48,256]{2,1,0:T(8,128)(2,1)S(1)}, u32[]{:S(2)}, u32[]{:S(2)}) collective-permute-start(bf16[3,48,256]{2,1,0:T(8,128)(2,1)S(1)} %get-tuple-element.45), channel_id=1, source_target_pairs={{0,15},{1,14},{2,13},{3,12},{4,11},{5,10},{6,9},{7,8},{8,7},{9,6},... | collective-permute-start | bytes 221192 | tf_op jit(solution)/shard_map/ppermute | solution.py:404
  28.9 1.2 %shard_map.82 = (bf16[256,128]{1,0:T(8,128)(2,1)S(1)}, bf16[3,288,512]{2,1,0:T(8,128)(2,1)S(1)}) custom-call(bf16[4096,128]{1,0:T(8,128)(2,1)} %proj_ref.1, bf16[3,288,512]{2,1,0:T(8,128)(2,1)} %bitcast.9), custom_call_target="tpu_custom_call" | custom-call | tf_op jit(solution)/shard_map/pallas_call | solution.py:384
  30.2 0.0 collective-permute-done.10.rest_10_
  30.2 0.0 collective-permute-done.11.rest_11_
  30.2 0.2 collective-permute-done.12.rest_12_
  30.4 1.3 %collective-permute-done.13.rest_13_ = bf16[3,48,256]{2,1,0:T(8,128)(2,1)S(1)} collective-permute-done((bf16[3,48,256]{2,1,0:T(8,128)(2,1)S(1)}, bf16[3,48,256]{2,1,0:T(8,128)(2,1)S(1)}, u32[]{:S(2)}, u32[]{:S(2)}) %collective-permute-start.13) | collective-permute-done | bytes 73760 | tf_op jit(solution)/shard_map/ppermute | solution.py:404
  31.7 1.7 %collective-permute-done.14.rest_14_ = bf16[3,48,256]{2,1,0:T(8,128)(2,1)S(1)} collective-permute-done((bf16[3,48,256]{2,1,0:T(8,128)(2,1)S(1)}, bf16[3,48,256]{2,1,0:T(8,128)(2,1)S(1)}, u32[]{:S(2)}, u32[]{:S(2)}) %collective-permute-start.14) | collective-permute-done | bytes 73760 | tf_op jit(solution)/shard_map/ppermute | solution.py:404
  33.5 1.9 %shard_map.85 = (f32[392,128]{1,0:T(8,128)S(1)}, bf16[400,128]{1,0:T(8,128)(2,1)S(1)}) custom-call(bf16[256,128]{1,0:T(8,128)(2,1)S(1)} %get-tuple-element.30.proj_ref, bf16[3,48,256]{2,1,0:T(8,128)(2,1)S(1)} %collective-permute-done.rest_0_, bf16[3,48,256]{2,1,0:T(8,128)(2,1)S(1)} %collective-permute-done.1.rest_1_, ...), custom_call_target="tpu_custom_call" | custom-call | tf_op jit(solution)/shard_map/pallas_call | solution.py:384
  35.4 0.1 collective-permute-start.15
  35.6 1.2 %collective-permute-done.15.got_ref = bf16[400,128]{1,0:T(8,128)(2,1)S(1)} collective-permute-done((bf16[400,128]{1,0:T(8,128)(2,1)S(1)}, bf16[400,128]{1,0:T(8,128)(2,1)S(1)}, u32[]{:S(2)}, u32[]{:S(2)}) %collective-permute-start.15) | collective-permute-done | bytes 102432 | tf_op jit(solution)/shard_map/ppermute | solution.py:404
  36.8 0.9 %collective-permute-start.16 = (bf16[200,128]{1,0:T(8,128)(2,1)S(1)}, bf16[200,128]{1,0:T(8,128)(2,1)S(1)}, u32[]{:S(2)}, u32[]{:S(2)}) collective-permute-start(bf16[200,128]{1,0:T(8,128)(2,1)S(1)} %get-tuple-element.50), channel_id=1, source_target_pairs={{0,2},{1,3},{2,0},{3,1},{4,6},{5,7},{6,4},{7,5},{8,10},{9,11},{10,... | collective-permute-start | bytes 153608 | tf_op jit(solution)/shard_map/ppermute | solution.py:404
  37.8 3.2 %collective-permute-done.16.got_ref = bf16[200,128]{1,0:T(8,128)(2,1)S(1)} collective-permute-done((bf16[200,128]{1,0:T(8,128)(2,1)S(1)}, bf16[200,128]{1,0:T(8,128)(2,1)S(1)}, u32[]{:S(2)}, u32[]{:S(2)}) %collective-permute-start.16) | collective-permute-done | bytes 51232 | tf_op jit(solution)/shard_map/ppermute | solution.py:404
  41.0 2.0 %collective-permute-start.19 = (bf16[200,128]{1,0:T(8,128)(2,1)S(1)}, bf16[200,128]{1,0:T(8,128)(2,1)S(1)}, u32[]{:S(2)}, u32[]{:S(2)}) collective-permute-start(bf16[200,128]{1,0:T(8,128)(2,1)S(1)} %get-tuple-element.52), channel_id=1, source_target_pairs={{0,12},{1,13},{2,14},{3,15},{4,8},{5,9},{6,10},{7,11},{8,4},{9,5},... | collective-permute-start | bytes 153608 | tf_op jit(solution)/shard_map/ppermute | solution.py:404
  43.1 0.2 collective-permute-start.18
  43.2 2.3 %collective-permute-start.17 = (bf16[200,128]{1,0:T(8,128)(2,1)S(1)}, bf16[200,128]{1,0:T(8,128)(2,1)S(1)}, u32[]{:S(2)}, u32[]{:S(2)}) collective-permute-start(bf16[200,128]{1,0:T(8,128)(2,1)S(1)} %get-tuple-element.52), channel_id=1, source_target_pairs={{0,4},{1,5},{2,6},{3,7},{4,0},{5,1},{6,2},{7,3},{8,12},{9,13},{10,... | collective-permute-start | bytes 153608 | tf_op jit(solution)/shard_map/ppermute | solution.py:404
  45.5 2.2 %collective-permute-done.19.rest_2_ = bf16[200,128]{1,0:T(8,128)(2,1)S(1)} collective-permute-done((bf16[200,128]{1,0:T(8,128)(2,1)S(1)}, bf16[200,128]{1,0:T(8,128)(2,1)S(1)}, u32[]{:S(2)}, u32[]{:S(2)}) %collective-permute-start.19) | collective-permute-done | bytes 51232 | tf_op jit(solution)/shard_map/ppermute | solution.py:404
  47.6 1.0 %collective-permute-done.18.rest_1_ = bf16[200,128]{1,0:T(8,128)(2,1)S(1)} collective-permute-done((bf16[200,128]{1,0:T(8,128)(2,1)S(1)}, bf16[200,128]{1,0:T(8,128)(2,1)S(1)}, u32[]{:S(2)}, u32[]{:S(2)}) %collective-permute-start.18) | collective-permute-done | bytes 51232 | tf_op jit(solution)/shard_map/ppermute | solution.py:404
  48.6 0.0 collective-permute-done.17.rest_0_
  48.6 0.1 shard_map.88.rest_0_
  48.8 1.2 %collective-permute-start.21 = (bf16[192,128]{1,0:T(8,128)(2,1)S(1)}, bf16[192,128]{1,0:T(8,128)(2,1)S(1)}, u32[]{:S(2)}, u32[]{:S(2)}) collective-permute-start(bf16[192,128]{1,0:T(8,128)(2,1)S(1)} %shard_map.88.rest_0_), channel_id=1, source_target_pairs={{0,2},{1,3},{2,0},{3,1},{4,6},{5,7},{6,4},{7,5},{8,10},{9,11},{10,... | collective-permute-start | bytes 147464 | tf_op jit(solution)/shard_map/ppermute | solution.py:404
  50.0 0.0 collective-permute-start.20
  50.0 3.0 %collective-permute-done.21.rest_2_ = bf16[192,128]{1,0:T(8,128)(2,1)S(1)} collective-permute-done((bf16[192,128]{1,0:T(8,128)(2,1)S(1)}, bf16[192,128]{1,0:T(8,128)(2,1)S(1)}, u32[]{:S(2)}, u32[]{:S(2)}) %collective-permute-start.21) | collective-permute-done | bytes 49184 | tf_op jit(solution)/shard_map/ppermute | solution.py:404
  52.9 0.0 collective-permute-done.20.rest_1_
  52.9 1.2 %collective-permute-done.22.rest_3_ = bf16[192,128]{1,0:T(8,128)(2,1)S(1)} collective-permute-done((bf16[192,128]{1,0:T(8,128)(2,1)S(1)}, bf16[192,128]{1,0:T(8,128)(2,1)S(1)}, u32[]{:S(2)}, u32[]{:S(2)}) %collective-permute-start.22) | collective-permute-done | bytes 49184 | tf_op jit(solution)/shard_map/ppermute | solution.py:404
  54.2 3.3 %shard_map.89 = bf16[16,16,128]{2,1,0:T(8,128)(2,1)S(1)} custom-call(bf16[3456,512]{1,0:T(8,128)(2,1)S(1)} %bitcast.6, f32[1,512]{1,0:T(1,128)S(1)} %bitcast.7, bf16[3,288,512]{2,1,0:T(8,128)(2,1)S(1)} %get-tuple-element.29.mid_weight_ref, f32[1,512]{1,0:T(1,128)S(1)} %bitcast.8, bf16[192,128]{1,0:T(8,128)(2,1)S(1)} %shard_map.88.rest_0_, ...), custom_call_target="tpu_custom_call" | custom-call | tf_op jit(solution)/shard_map/pallas_call | solution.py:384
  57.5 10.7 %all_to_all.5.rows_ref = bf16[16,16,128]{2,1,0:T(8,128)(2,1)S(1)} all-to-all(bf16[16,16,128]{2,1,0:T(8,128)(2,1)S(1)} %shard_map.89), channel_id=1, replica_groups=mesh['groups'=2,'seq'=16] {'seq'}, dimensions={0} | all-to-all | bytes 131072 | tf_op jit(solution)/shard_map/all_to_all | solution.py:496
  68.2 0.9 %shuffle.1 = bf16[1,2,2,48,128]{4,3,2,1,0:T(8,128)(2,1)} custom-call(bf16[16,16,128]{2,1,0:T(8,128)(2,1)S(1)} %all_to_all.5.rows_ref), custom_call_target="tpu_custom_call" | custom-call | tf_op jit(solution)/shard_map/shuffle/pallas_call | solution.py:497
  (14 shorter events, 0.1 us)
Async XLA Ops:
  0.0 54.2 %copy-start.2 = (f32[512]{0:T(512)S(1)}, f32[512]{0:T(512)}, u32[]{:S(2)}) copy-start(f32[512]{0:T(512)} %param.15) | copy-start | bytes 6148
  0.0 54.2 %copy-start.1 = (f32[512]{0:T(512)S(1)}, f32[512]{0:T(512)}, u32[]{:S(2)}) copy-start(f32[512]{0:T(512)} %param.13) | copy-start | bytes 6148
  0.0 54.2 %copy-start = (bf16[3,3,3,128,512]{4,3,2,1,0:T(8,128)(2,1)S(1)}, bf16[3,3,3,128,512]{4,3,2,1,0:T(8,128)(2,1)}, u32[]{:S(2)}) copy-start(bf16[3,3,3,128,512]{4,3,2,1,0:T(8,128)(2,1)} %param.12) | copy-start | bytes 10616836
  1.0 10.3 %collective-permute-start = (bf16[3,48,256]{2,1,0:T(8,128)(2,1)S(1)}, bf16[3,48,256]{2,1,0:T(8,128)(2,1)S(1)}, u32[]{:S(2)}, u32[]{:S(2)}) collective-permute-start(bf16[3,48,256]{2,1,0:T(8,128)(2,1)S(1)} %get-tuple-element.31), channel_id=1, source_target_pairs={{0,8},{1,9},{2,10},{3,11},{4,12},{5,13},{6,14},{7,15},{8,0},{9,1},... | collective-permute-start | bytes 221192 | tf_op jit(solution)/shard_map/ppermute | solution.py:404
  5.2 6.7 %collective-permute-start.1 = (bf16[3,48,256]{2,1,0:T(8,128)(2,1)S(1)}, bf16[3,48,256]{2,1,0:T(8,128)(2,1)S(1)}, u32[]{:S(2)}, u32[]{:S(2)}) collective-permute-start(bf16[3,48,256]{2,1,0:T(8,128)(2,1)S(1)} %get-tuple-element.32), channel_id=1, source_target_pairs={{0,1},{1,0},{2,3},{3,2},{4,5},{5,4},{6,7},{7,6},{8,9},{9,8},{10,11... | collective-permute-start | bytes 221192 | tf_op jit(solution)/shard_map/ppermute | solution.py:404
  6.8 5.8 %collective-permute-start.2 = (bf16[3,48,256]{2,1,0:T(8,128)(2,1)S(1)}, bf16[3,48,256]{2,1,0:T(8,128)(2,1)S(1)}, u32[]{:S(2)}, u32[]{:S(2)}) collective-permute-start(bf16[3,48,256]{2,1,0:T(8,128)(2,1)S(1)} %get-tuple-element.33), channel_id=1, source_target_pairs={{0,9},{1,8},{2,11},{3,10},{4,13},{5,12},{6,15},{7,14},{8,1},{9,0},... | collective-permute-start | bytes 221192 | tf_op jit(solution)/shard_map/ppermute | solution.py:404
  7.0 9.2 %collective-permute-start.3 = (bf16[3,48,256]{2,1,0:T(8,128)(2,1)S(1)}, bf16[3,48,256]{2,1,0:T(8,128)(2,1)S(1)}, u32[]{:S(2)}, u32[]{:S(2)}) collective-permute-start(bf16[3,48,256]{2,1,0:T(8,128)(2,1)S(1)} %get-tuple-element.34), channel_id=1, source_target_pairs={{0,2},{1,3},{2,0},{3,1},{4,6},{5,7},{6,4},{7,5},{8,10},{9,11},{10,... | collective-permute-start | bytes 221192 | tf_op jit(solution)/shard_map/ppermute | solution.py:404
  8.8 11.3 %collective-permute-start.4 = (bf16[3,48,256]{2,1,0:T(8,128)(2,1)S(1)}, bf16[3,48,256]{2,1,0:T(8,128)(2,1)S(1)}, u32[]{:S(2)}, u32[]{:S(2)}) collective-permute-start(bf16[3,48,256]{2,1,0:T(8,128)(2,1)S(1)} %get-tuple-element.35), channel_id=1, source_target_pairs={{0,10},{1,11},{2,8},{3,9},{4,14},{5,15},{6,12},{7,13},{8,2},{9,3},... | collective-permute-start | bytes 221192 | tf_op jit(solution)/shard_map/ppermute | solution.py:404
  11.3 8.8 %collective-permute-start.5 = (bf16[3,48,256]{2,1,0:T(8,128)(2,1)S(1)}, bf16[3,48,256]{2,1,0:T(8,128)(2,1)S(1)}, u32[]{:S(2)}, u32[]{:S(2)}) collective-permute-start(bf16[3,48,256]{2,1,0:T(8,128)(2,1)S(1)} %get-tuple-element.36), channel_id=1, source_target_pairs={{0,3},{1,2},{2,1},{3,0},{4,7},{5,6},{6,5},{7,4},{8,11},{9,10},{10,... | collective-permute-start | bytes 221192 | tf_op jit(solution)/shard_map/ppermute | solution.py:404
  11.9 9.1 %collective-permute-start.6 = (bf16[3,48,256]{2,1,0:T(8,128)(2,1)S(1)}, bf16[3,48,256]{2,1,0:T(8,128)(2,1)S(1)}, u32[]{:S(2)}, u32[]{:S(2)}) collective-permute-start(bf16[3,48,256]{2,1,0:T(8,128)(2,1)S(1)} %get-tuple-element.37), channel_id=1, source_target_pairs={{0,11},{1,10},{2,9},{3,8},{4,15},{5,14},{6,13},{7,12},{8,3},{9,2},... | collective-permute-start | bytes 221192 | tf_op jit(solution)/shard_map/ppermute | solution.py:404
  12.6 9.9 %collective-permute-start.7 = (bf16[3,48,256]{2,1,0:T(8,128)(2,1)S(1)}, bf16[3,48,256]{2,1,0:T(8,128)(2,1)S(1)}, u32[]{:S(2)}, u32[]{:S(2)}) collective-permute-start(bf16[3,48,256]{2,1,0:T(8,128)(2,1)S(1)} %get-tuple-element.38), channel_id=1, source_target_pairs={{0,4},{1,5},{2,6},{3,7},{4,0},{5,1},{6,2},{7,3},{8,12},{9,13},{10,... | collective-permute-start | bytes 221192 | tf_op jit(solution)/shard_map/ppermute | solution.py:404
  16.2 9.8 %collective-permute-start.8 = (bf16[3,48,256]{2,1,0:T(8,128)(2,1)S(1)}, bf16[3,48,256]{2,1,0:T(8,128)(2,1)S(1)}, u32[]{:S(2)}, u32[]{:S(2)}) collective-permute-start(bf16[3,48,256]{2,1,0:T(8,128)(2,1)S(1)} %get-tuple-element.39), channel_id=1, source_target_pairs={{0,12},{1,13},{2,14},{3,15},{4,8},{5,9},{6,10},{7,11},{8,4},{9,5},... | collective-permute-start | bytes 221192 | tf_op jit(solution)/shard_map/ppermute | solution.py:404
  20.1 5.9 %collective-permute-start.9 = (bf16[3,48,256]{2,1,0:T(8,128)(2,1)S(1)}, bf16[3,48,256]{2,1,0:T(8,128)(2,1)S(1)}, u32[]{:S(2)}, u32[]{:S(2)}) collective-permute-start(bf16[3,48,256]{2,1,0:T(8,128)(2,1)S(1)} %get-tuple-element.40), channel_id=1, source_target_pairs={{0,5},{1,4},{2,7},{3,6},{4,1},{5,0},{6,3},{7,2},{8,13},{9,12},{10,... | collective-permute-start | bytes 221192 | tf_op jit(solution)/shard_map/ppermute | solution.py:404
  20.1 10.0 %collective-permute-start.10 = (bf16[3,48,256]{2,1,0:T(8,128)(2,1)S(1)}, bf16[3,48,256]{2,1,0:T(8,128)(2,1)S(1)}, u32[]{:S(2)}, u32[]{:S(2)}) collective-permute-start(bf16[3,48,256]{2,1,0:T(8,128)(2,1)S(1)} %get-tuple-element.41), channel_id=1, source_target_pairs={{0,13},{1,12},{2,15},{3,14},{4,9},{5,8},{6,11},{7,10},{8,5},{9,4},... | collective-permute-start | bytes 221192 | tf_op jit(solution)/shard_map/ppermute | solution.py:404
  21.0 9.2 %collective-permute-start.11 = (bf16[3,48,256]{2,1,0:T(8,128)(2,1)S(1)}, bf16[3,48,256]{2,1,0:T(8,128)(2,1)S(1)}, u32[]{:S(2)}, u32[]{:S(2)}) collective-permute-start(bf16[3,48,256]{2,1,0:T(8,128)(2,1)S(1)} %get-tuple-element.42), channel_id=1, source_target_pairs={{0,6},{1,7},{2,4},{3,5},{4,2},{5,3},{6,0},{7,1},{8,14},{9,15},{10,... | collective-permute-start | bytes 221192 | tf_op jit(solution)/shard_map/ppermute | solution.py:404
  22.5 7.9 %collective-permute-start.12 = (bf16[3,48,256]{2,1,0:T(8,128)(2,1)S(1)}, bf16[3,48,256]{2,1,0:T(8,128)(2,1)S(1)}, u32[]{:S(2)}, u32[]{:S(2)}) collective-permute-start(bf16[3,48,256]{2,1,0:T(8,128)(2,1)S(1)} %get-tuple-element.43), channel_id=1, source_target_pairs={{0,14},{1,15},{2,12},{3,13},{4,10},{5,11},{6,8},{7,9},{8,6},{9,7},... | collective-permute-start | bytes 221192 | tf_op jit(solution)/shard_map/ppermute | solution.py:404
  26.1 5.7 %collective-permute-start.13 = (bf16[3,48,256]{2,1,0:T(8,128)(2,1)S(1)}, bf16[3,48,256]{2,1,0:T(8,128)(2,1)S(1)}, u32[]{:S(2)}, u32[]{:S(2)}) collective-permute-start(bf16[3,48,256]{2,1,0:T(8,128)(2,1)S(1)} %get-tuple-element.44), channel_id=1, source_target_pairs={{0,7},{1,6},{2,5},{3,4},{4,3},{5,2},{6,1},{7,0},{8,15},{9,14},{10,... | collective-permute-start | bytes 221192 | tf_op jit(solution)/shard_map/ppermute | solution.py:404
  26.1 7.4 %collective-permute-start.14 = (bf16[3,48,256]{2,1,0:T(8,128)(2,1)S(1)}, bf16[3,48,256]{2,1,0:T(8,128)(2,1)S(1)}, u32[]{:S(2)}, u32[]{:S(2)}) collective-permute-start(bf16[3,48,256]{2,1,0:T(8,128)(2,1)S(1)} %get-tuple-element.45), channel_id=1, source_target_pairs={{0,15},{1,14},{2,13},{3,12},{4,11},{5,10},{6,9},{7,8},{8,7},{9,6},... | collective-permute-start | bytes 221192 | tf_op jit(solution)/shard_map/ppermute | solution.py:404
  35.4 1.4 %collective-permute-start.15 = (bf16[400,128]{1,0:T(8,128)(2,1)S(1)}, bf16[400,128]{1,0:T(8,128)(2,1)S(1)}, u32[]{:S(2)}, u32[]{:S(2)}) collective-permute-start(bf16[400,128]{1,0:T(8,128)(2,1)S(1)} %get-tuple-element.48), channel_id=1, source_target_pairs={{0,1},{1,0},{2,3},{3,2},{4,5},{5,4},{6,7},{7,6},{8,9},{9,8},{10,11... | collective-permute-start | bytes 307208 | tf_op jit(solution)/shard_map/ppermute | solution.py:404
  36.8 4.2 %collective-permute-start.16 = (bf16[200,128]{1,0:T(8,128)(2,1)S(1)}, bf16[200,128]{1,0:T(8,128)(2,1)S(1)}, u32[]{:S(2)}, u32[]{:S(2)}) collective-permute-start(bf16[200,128]{1,0:T(8,128)(2,1)S(1)} %get-tuple-element.50), channel_id=1, source_target_pairs={{0,2},{1,3},{2,0},{3,1},{4,6},{5,7},{6,4},{7,5},{8,10},{9,11},{10,... | collective-permute-start | bytes 153608 | tf_op jit(solution)/shard_map/ppermute | solution.py:404
  41.0 6.6 %collective-permute-start.19 = (bf16[200,128]{1,0:T(8,128)(2,1)S(1)}, bf16[200,128]{1,0:T(8,128)(2,1)S(1)}, u32[]{:S(2)}, u32[]{:S(2)}) collective-permute-start(bf16[200,128]{1,0:T(8,128)(2,1)S(1)} %get-tuple-element.52), channel_id=1, source_target_pairs={{0,12},{1,13},{2,14},{3,15},{4,8},{5,9},{6,10},{7,11},{8,4},{9,5},... | collective-permute-start | bytes 153608 | tf_op jit(solution)/shard_map/ppermute | solution.py:404
  43.1 5.6 %collective-permute-start.18 = (bf16[200,128]{1,0:T(8,128)(2,1)S(1)}, bf16[200,128]{1,0:T(8,128)(2,1)S(1)}, u32[]{:S(2)}, u32[]{:S(2)}) collective-permute-start(bf16[200,128]{1,0:T(8,128)(2,1)S(1)} %get-tuple-element.52), channel_id=1, source_target_pairs={{0,8},{1,9},{2,10},{3,11},{4,12},{5,13},{6,14},{7,15},{8,0},{9,1},... | collective-permute-start | bytes 153608 | tf_op jit(solution)/shard_map/ppermute | solution.py:404
  43.2 5.4 %collective-permute-start.17 = (bf16[200,128]{1,0:T(8,128)(2,1)S(1)}, bf16[200,128]{1,0:T(8,128)(2,1)S(1)}, u32[]{:S(2)}, u32[]{:S(2)}) collective-permute-start(bf16[200,128]{1,0:T(8,128)(2,1)S(1)} %get-tuple-element.52), channel_id=1, source_target_pairs={{0,4},{1,5},{2,6},{3,7},{4,0},{5,1},{6,2},{7,3},{8,12},{9,13},{10,... | collective-permute-start | bytes 153608 | tf_op jit(solution)/shard_map/ppermute | solution.py:404
  48.8 4.2 %collective-permute-start.21 = (bf16[192,128]{1,0:T(8,128)(2,1)S(1)}, bf16[192,128]{1,0:T(8,128)(2,1)S(1)}, u32[]{:S(2)}, u32[]{:S(2)}) collective-permute-start(bf16[192,128]{1,0:T(8,128)(2,1)S(1)} %shard_map.88.rest_0_), channel_id=1, source_target_pairs={{0,2},{1,3},{2,0},{3,1},{4,6},{5,7},{6,4},{7,5},{8,10},{9,11},{10,... | collective-permute-start | bytes 147464 | tf_op jit(solution)/shard_map/ppermute | solution.py:404
  50.0 3.0 %collective-permute-start.20 = (bf16[192,128]{1,0:T(8,128)(2,1)S(1)}, bf16[192,128]{1,0:T(8,128)(2,1)S(1)}, u32[]{:S(2)}, u32[]{:S(2)}) collective-permute-start(bf16[192,128]{1,0:T(8,128)(2,1)S(1)} %shard_map.88.rest_0_), channel_id=1, source_target_pairs={{0,1},{1,0},{2,3},{3,2},{4,5},{5,4},{6,7},{7,6},{8,9},{9,8},{10,11... | collective-permute-start | bytes 147464 | tf_op jit(solution)/shard_map/ppermute | solution.py:404
  52.9 1.2 %collective-permute-start.22 = (bf16[192,128]{1,0:T(8,128)(2,1)S(1)}, bf16[192,128]{1,0:T(8,128)(2,1)S(1)}, u32[]{:S(2)}, u32[]{:S(2)}) collective-permute-start(bf16[192,128]{1,0:T(8,128)(2,1)S(1)} %collective-permute-done.21.rest_2_), channel_id=1, source_target_pairs={{0,1},{1,0},{2,3},{3,2},{4,5},{5,4},{6,7},{7,6},{8,9},{9,8},{10,11... | collective-permute-start | bytes 147464 | tf_op jit(solution)/shard_map/ppermute | solution.py:404

commit v2 on v1

--- a/solution.py
+++ b/solution.py
@@ -472,7 +472,9 @@
         [LOCAL] * (1 + len(gots)),
         (near(keep), *gots),
     )
-    paired = swap(ready, 2)
+    quarters = [near(ready)]
+    for step in range(1, 4):
+        quarters.append(swap(ready, step))
     columns = launch(
         convolve_body,
         pltpu.VMEM((devices, 16, 128), jnp.bfloat16),
@@ -482,10 +484,7 @@
             near(in_bias.reshape(1, CH)),
             near(mid_near),
             near(mid_bias.reshape(1, CH)),
-            near(ready),
-            swap(ready, 1),
-            paired,
-            swap(paired, 1),
+            *quarters,
         ),
         [
             pltpu.VMEM((devices * local, C_LAT), jnp.bfloat16),

time: 69.3 us -> 68.6 us (0.990)
  waiting for transfers between devices: 18.3 us -> 17 us
  starting transfers between devices: 29.8 us -> 30.5 us
    ppermute x23, waiting for transfers between devices: 18.3 us -> 17 us  [swap(): lax.ppermute(array, 'seq', [(i, i ^ step) for i in range(devices)])]
    ppermute x23, starting transfers between devices: 29.8 us -> 30.5 us  [swap(): lax.ppermute(array, 'seq', [(i, i ^ step) for i in range(devices)])]
where the time goes in v2:
time: 68.6 us; the launch traced here: 68.3 us
  starting transfers between devices  30.5 us (44%)
  waiting for transfers between devices  17 us (25%)
  blocking collectives  10.6 us (15%)
  Pallas kernels  10.2 us (15%)
    ppermute x23, starting transfers between devices, swap(): lax.ppermute(array, 'seq', [(i, i ^ step) for i in range(devices)])  30.5 us
    ppermute x23, waiting for transfers between devices, swap(): lax.ppermute(array, 'seq', [(i, i ^ step) for i in range(devices)])  17 us
    all_to_all x1, blocking collectives, whole_heads(): lax.all_to_all(columns, 'seq', split_axis=0, concat_axis=0, tiled=True)  10.6 us
    pallas_call x8, Pallas kernels, launch(): pl.pallas_call(body, out_shape=outs, in_specs=in_specs, out_specs=jax.tre...  9.25 us
  transfers between devices with their start and end apart: 23, of which 10 were waited for; matrix products, arithmetic and copies ran while one was open for 0% of the time, Pallas kernels for 4%

profile of v2, /device:TPU:0, one launch (start us, length us, event | category | flops | bytes accessed | tf_op | source)
XLA Modules:
  0.0 68.3 jit_solution(7731646754839454951)
XLA Ops:
  0.0 1.0 %shard_map.83 = (bf16[3,48,256]{2,1,0:T(8,128)(2,1)S(1)}, bf16[3,48,256]{2,1,0:T(8,128)(2,1)S(1)}) custom-call(bf16[48,4096]{1,0:T(8,128)(2,1)} %query_ref.3, bf16[48,4096]{1,0:T(8,128)(2,1)} %key_ref.3, bf16[48,4096]{1,0:T(8,128)(2,1)} %value_ref.3), custom_call_target="tpu_custom_call" | custom-call | tf_op jit(solution)/shard_map/pallas_call | solution.py:384
  1.0 4.1 %collective-permute-start = (bf16[3,48,256]{2,1,0:T(8,128)(2,1)S(1)}, bf16[3,48,256]{2,1,0:T(8,128)(2,1)S(1)}, u32[]{:S(2)}, u32[]{:S(2)}) collective-permute-start(bf16[3,48,256]{2,1,0:T(8,128)(2,1)S(1)} %get-tuple-element.31), channel_id=1, source_target_pairs={{0,8},{1,9},{2,10},{3,11},{4,12},{5,13},{6,14},{7,15},{8,0},{9,1},... | collective-permute-start | bytes 221192 | tf_op jit(solution)/shard_map/ppermute | solution.py:404
  5.2 0.0 collective-permute-start.1
  5.2 1.6 %shard_map.84 = (bf16[3,48,256]{2,1,0:T(8,128)(2,1)S(1)}, bf16[3,48,256]{2,1,0:T(8,128)(2,1)S(1)}, bf16[3,48,256]{2,1,0:T(8,128)(2,1)S(1)}, bf16[3,48,256]{2,1,0...) custom-call(bf16[48,4096]{1,0:T(8,128)(2,1)} %query_ref.3, ...), custom_call_target="tpu_custom_call" | custom-call | tf_op jit(solution)/shard_map/pallas_call | solution.py:384
  6.8 0.3 collective-permute-start.2
  7.0 1.8 %collective-permute-start.3 = (bf16[3,48,256]{2,1,0:T(8,128)(2,1)S(1)}, bf16[3,48,256]{2,1,0:T(8,128)(2,1)S(1)}, u32[]{:S(2)}, u32[]{:S(2)}) collective-permute-start(bf16[3,48,256]{2,1,0:T(8,128)(2,1)S(1)} %get-tuple-element.34), channel_id=1, source_target_pairs={{0,2},{1,3},{2,0},{3,1},{4,6},{5,7},{6,4},{7,5},{8,10},{9,11},{10,... | collective-permute-start | bytes 221192 | tf_op jit(solution)/shard_map/ppermute | solution.py:404
  8.8 2.5 %collective-permute-start.4 = (bf16[3,48,256]{2,1,0:T(8,128)(2,1)S(1)}, bf16[3,48,256]{2,1,0:T(8,128)(2,1)S(1)}, u32[]{:S(2)}, u32[]{:S(2)}) collective-permute-start(bf16[3,48,256]{2,1,0:T(8,128)(2,1)S(1)} %get-tuple-element.35), channel_id=1, source_target_pairs={{0,10},{1,11},{2,8},{3,9},{4,14},{5,15},{6,12},{7,13},{8,2},{9,3},... | collective-permute-start | bytes 221192 | tf_op jit(solution)/shard_map/ppermute | solution.py:404
  11.3 0.0 collective-permute-done.rest_0_
  11.3 0.6 collective-permute-start.5
  11.9 0.0 collective-permute-done.1.rest_1_
  11.9 0.7 %collective-permute-start.6 = (bf16[3,48,256]{2,1,0:T(8,128)(2,1)S(1)}, bf16[3,48,256]{2,1,0:T(8,128)(2,1)S(1)}, u32[]{:S(2)}, u32[]{:S(2)}) collective-permute-start(bf16[3,48,256]{2,1,0:T(8,128)(2,1)S(1)} %get-tuple-element.37), channel_id=1, source_target_pairs={{0,11},{1,10},{2,9},{3,8},{4,15},{5,14},{6,13},{7,12},{8,3},{9,2},... | collective-permute-start | bytes 221192 | tf_op jit(solution)/shard_map/ppermute | solution.py:404
  12.6 0.0 collective-permute-done.2.rest_2_
  12.6 3.6 %collective-permute-start.7 = (bf16[3,48,256]{2,1,0:T(8,128)(2,1)S(1)}, bf16[3,48,256]{2,1,0:T(8,128)(2,1)S(1)}, u32[]{:S(2)}, u32[]{:S(2)}) collective-permute-start(bf16[3,48,256]{2,1,0:T(8,128)(2,1)S(1)} %get-tuple-element.38), channel_id=1, source_target_pairs={{0,4},{1,5},{2,6},{3,7},{4,0},{5,1},{6,2},{7,3},{8,12},{9,13},{10,... | collective-permute-start | bytes 221192 | tf_op jit(solution)/shard_map/ppermute | solution.py:404
  16.2 0.7 collective-permute-start.8
  16.9 3.2 %collective-permute-done.4.rest_4_ = bf16[3,48,256]{2,1,0:T(8,128)(2,1)S(1)} collective-permute-done((bf16[3,48,256]{2,1,0:T(8,128)(2,1)S(1)}, bf16[3,48,256]{2,1,0:T(8,128)(2,1)S(1)}, u32[]{:S(2)}, u32[]{:S(2)}) %collective-permute-start.4) | collective-permute-done | bytes 73760 | tf_op jit(solution)/shard_map/ppermute | solution.py:404
  20.1 0.8 %collective-permute-start.10 = (bf16[3,48,256]{2,1,0:T(8,128)(2,1)S(1)}, bf16[3,48,256]{2,1,0:T(8,128)(2,1)S(1)}, u32[]{:S(2)}, u32[]{:S(2)}) collective-permute-start(bf16[3,48,256]{2,1,0:T(8,128)(2,1)S(1)} %get-tuple-element.41), channel_id=1, source_target_pairs={{0,13},{1,12},{2,15},{3,14},{4,9},{5,8},{6,11},{7,10},{8,5},{9,4},... | collective-permute-start | bytes 221192 | tf_op jit(solution)/shard_map/ppermute | solution.py:404
  21.0 1.5 %collective-permute-start.11 = (bf16[3,48,256]{2,1,0:T(8,128)(2,1)S(1)}, bf16[3,48,256]{2,1,0:T(8,128)(2,1)S(1)}, u32[]{:S(2)}, u32[]{:S(2)}) collective-permute-start(bf16[3,48,256]{2,1,0:T(8,128)(2,1)S(1)} %get-tuple-element.42), channel_id=1, source_target_pairs={{0,6},{1,7},{2,4},{3,5},{4,2},{5,3},{6,0},{7,1},{8,14},{9,15},{10,... | collective-permute-start | bytes 221192 | tf_op jit(solution)/shard_map/ppermute | solution.py:404
  22.5 0.0 collective-permute-done.7.rest_7_
  22.5 3.6 %collective-permute-start.12 = (bf16[3,48,256]{2,1,0:T(8,128)(2,1)S(1)}, bf16[3,48,256]{2,1,0:T(8,128)(2,1)S(1)}, u32[]{:S(2)}, u32[]{:S(2)}) collective-permute-start(bf16[3,48,256]{2,1,0:T(8,128)(2,1)S(1)} %get-tuple-element.43), channel_id=1, source_target_pairs={{0,14},{1,15},{2,12},{3,13},{4,10},{5,11},{6,8},{7,9},{8,6},{9,7},... | collective-permute-start | bytes 221192 | tf_op jit(solution)/shard_map/ppermute | solution.py:404
  26.1 0.0 collective-permute-done.8.rest_8_
  26.1 0.0 collective-permute-start.13
  26.1 2.9 %collective-permute-start.14 = (bf16[3,48,256]{2,1,0:T(8,128)(2,1)S(1)}, bf16[3,48,256]{2,1,0:T(8,128)(2,1)S(1)}, u32[]{:S(2)}, u32[]{:S(2)}) collective-permute-start(bf16[3,48,256]{2,1,0:T(8,128)(2,1)S(1)} %get-tuple-element.45), channel_id=1, source_target_pairs={{0,15},{1,14},{2,13},{3,12},{4,11},{5,10},{6,9},{7,8},{8,7},{9,6},... | collective-permute-start | bytes 221192 | tf_op jit(solution)/shard_map/ppermute | solution.py:404
  28.9 1.2 %shard_map.82 = (bf16[256,128]{1,0:T(8,128)(2,1)S(1)}, bf16[3,288,512]{2,1,0:T(8,128)(2,1)S(1)}) custom-call(bf16[4096,128]{1,0:T(8,128)(2,1)} %proj_ref.1, bf16[3,288,512]{2,1,0:T(8,128)(2,1)} %bitcast.9), custom_call_target="tpu_custom_call" | custom-call | tf_op jit(solution)/shard_map/pallas_call | solution.py:384
  30.2 0.0 collective-permute-done.10.rest_10_
  30.2 0.0 collective-permute-done.11.rest_11_
  30.2 0.2 collective-permute-done.12.rest_12_
  30.4 1.3 %collective-permute-done.13.rest_13_ = bf16[3,48,256]{2,1,0:T(8,128)(2,1)S(1)} collective-permute-done((bf16[3,48,256]{2,1,0:T(8,128)(2,1)S(1)}, bf16[3,48,256]{2,1,0:T(8,128)(2,1)S(1)}, u32[]{:S(2)}, u32[]{:S(2)}) %collective-permute-start.13) | collective-permute-done | bytes 73760 | tf_op jit(solution)/shard_map/ppermute | solution.py:404
  31.7 1.7 %collective-permute-done.14.rest_14_ = bf16[3,48,256]{2,1,0:T(8,128)(2,1)S(1)} collective-permute-done((bf16[3,48,256]{2,1,0:T(8,128)(2,1)S(1)}, bf16[3,48,256]{2,1,0:T(8,128)(2,1)S(1)}, u32[]{:S(2)}, u32[]{:S(2)}) %collective-permute-start.14) | collective-permute-done | bytes 73760 | tf_op jit(solution)/shard_map/ppermute | solution.py:404
  33.5 1.9 %shard_map.85 = (f32[392,128]{1,0:T(8,128)S(1)}, bf16[400,128]{1,0:T(8,128)(2,1)S(1)}) custom-call(bf16[256,128]{1,0:T(8,128)(2,1)S(1)} %get-tuple-element.30.proj_ref, bf16[3,48,256]{2,1,0:T(8,128)(2,1)S(1)} %collective-permute-done.rest_0_, bf16[3,48,256]{2,1,0:T(8,128)(2,1)S(1)} %collective-permute-done.1.rest_1_, ...), custom_call_target="tpu_custom_call" | custom-call | tf_op jit(solution)/shard_map/pallas_call | solution.py:384
  35.4 0.1 collective-permute-start.15
  35.6 1.2 %collective-permute-done.15.got_ref = bf16[400,128]{1,0:T(8,128)(2,1)S(1)} collective-permute-done((bf16[400,128]{1,0:T(8,128)(2,1)S(1)}, bf16[400,128]{1,0:T(8,128)(2,1)S(1)}, u32[]{:S(2)}, u32[]{:S(2)}) %collective-permute-start.15) | collective-permute-done | bytes 102432 | tf_op jit(solution)/shard_map/ppermute | solution.py:404
  36.8 0.9 %collective-permute-start.16 = (bf16[200,128]{1,0:T(8,128)(2,1)S(1)}, bf16[200,128]{1,0:T(8,128)(2,1)S(1)}, u32[]{:S(2)}, u32[]{:S(2)}) collective-permute-start(bf16[200,128]{1,0:T(8,128)(2,1)S(1)} %get-tuple-element.50), channel_id=1, source_target_pairs={{0,2},{1,3},{2,0},{3,1},{4,6},{5,7},{6,4},{7,5},{8,10},{9,11},{10,... | collective-permute-start | bytes 153608 | tf_op jit(solution)/shard_map/ppermute | solution.py:404
  37.8 3.2 %collective-permute-done.16.got_ref = bf16[200,128]{1,0:T(8,128)(2,1)S(1)} collective-permute-done((bf16[200,128]{1,0:T(8,128)(2,1)S(1)}, bf16[200,128]{1,0:T(8,128)(2,1)S(1)}, u32[]{:S(2)}, u32[]{:S(2)}) %collective-permute-start.16) | collective-permute-done | bytes 51232 | tf_op jit(solution)/shard_map/ppermute | solution.py:404
  41.0 2.0 %collective-permute-start.19 = (bf16[200,128]{1,0:T(8,128)(2,1)S(1)}, bf16[200,128]{1,0:T(8,128)(2,1)S(1)}, u32[]{:S(2)}, u32[]{:S(2)}) collective-permute-start(bf16[200,128]{1,0:T(8,128)(2,1)S(1)} %get-tuple-element.52), channel_id=1, source_target_pairs={{0,12},{1,13},{2,14},{3,15},{4,8},{5,9},{6,10},{7,11},{8,4},{9,5},... | collective-permute-start | bytes 153608 | tf_op jit(solution)/shard_map/ppermute | solution.py:404
  43.1 0.2 collective-permute-start.18
  43.2 2.3 %collective-permute-start.17 = (bf16[200,128]{1,0:T(8,128)(2,1)S(1)}, bf16[200,128]{1,0:T(8,128)(2,1)S(1)}, u32[]{:S(2)}, u32[]{:S(2)}) collective-permute-start(bf16[200,128]{1,0:T(8,128)(2,1)S(1)} %get-tuple-element.52), channel_id=1, source_target_pairs={{0,4},{1,5},{2,6},{3,7},{4,0},{5,1},{6,2},{7,3},{8,12},{9,13},{10,... | collective-permute-start | bytes 153608 | tf_op jit(solution)/shard_map/ppermute | solution.py:404
  45.5 2.2 %collective-permute-done.19.rest_2_ = bf16[200,128]{1,0:T(8,128)(2,1)S(1)} collective-permute-done((bf16[200,128]{1,0:T(8,128)(2,1)S(1)}, bf16[200,128]{1,0:T(8,128)(2,1)S(1)}, u32[]{:S(2)}, u32[]{:S(2)}) %collective-permute-start.19) | collective-permute-done | bytes 51232 | tf_op jit(solution)/shard_map/ppermute | solution.py:404
  47.6 1.0 %collective-permute-done.18.rest_1_ = bf16[200,128]{1,0:T(8,128)(2,1)S(1)} collective-permute-done((bf16[200,128]{1,0:T(8,128)(2,1)S(1)}, bf16[200,128]{1,0:T(8,128)(2,1)S(1)}, u32[]{:S(2)}, u32[]{:S(2)}) %collective-permute-start.18) | collective-permute-done | bytes 51232 | tf_op jit(solution)/shard_map/ppermute | solution.py:404
  48.6 0.0 collective-permute-done.17.rest_0_
  48.6 0.1 shard_map.88.rest_0_
  48.8 0.1 collective-permute-start.22
  48.8 1.2 %collective-permute-start.21 = (bf16[192,128]{1,0:T(8,128)(2,1)S(1)}, bf16[192,128]{1,0:T(8,128)(2,1)S(1)}, u32[]{:S(2)}, u32[]{:S(2)}) collective-permute-start(bf16[192,128]{1,0:T(8,128)(2,1)S(1)} %shard_map.88.rest_0_), channel_id=1, source_target_pairs={{0,2},{1,3},{2,0},{3,1},{4,6},{5,7},{6,4},{7,5},{8,10},{9,11},{10,... | collective-permute-start | bytes 147464 | tf_op jit(solution)/shard_map/ppermute | solution.py:404
  50.0 0.7 collective-permute-start.20
  50.7 1.9 %collective-permute-done.22.rest_3_ = bf16[192,128]{1,0:T(8,128)(2,1)S(1)} collective-permute-done((bf16[192,128]{1,0:T(8,128)(2,1)S(1)}, bf16[192,128]{1,0:T(8,128)(2,1)S(1)}, u32[]{:S(2)}, u32[]{:S(2)}) %collective-permute-start.22) | collective-permute-done | bytes 49184 | tf_op jit(solution)/shard_map/ppermute | solution.py:404
  52.6 0.9 %collective-permute-done.21.rest_2_ = bf16[192,128]{1,0:T(8,128)(2,1)S(1)} collective-permute-done((bf16[192,128]{1,0:T(8,128)(2,1)S(1)}, bf16[192,128]{1,0:T(8,128)(2,1)S(1)}, u32[]{:S(2)}, u32[]{:S(2)}) %collective-permute-start.21) | collective-permute-done | bytes 49184 | tf_op jit(solution)/shard_map/ppermute | solution.py:404
  53.5 3.3 %shard_map.89 = bf16[16,16,128]{2,1,0:T(8,128)(2,1)S(1)} custom-call(bf16[3456,512]{1,0:T(8,128)(2,1)S(1)} %bitcast.6, f32[1,512]{1,0:T(1,128)S(1)} %bitcast.7, bf16[3,288,512]{2,1,0:T(8,128)(2,1)S(1)} %get-tuple-element.29.mid_weight_ref, f32[1,512]{1,0:T(1,128)S(1)} %bitcast.8, bf16[192,128]{1,0:T(8,128)(2,1)S(1)} %shard_map.88.rest_0_, ...), custom_call_target="tpu_custom_call" | custom-call | tf_op jit(solution)/shard_map/pallas_call | solution.py:384
  56.9 10.6 %all_to_all.5.rows_ref = bf16[16,16,128]{2,1,0:T(8,128)(2,1)S(1)} all-to-all(bf16[16,16,128]{2,1,0:T(8,128)(2,1)S(1)} %shard_map.89), channel_id=1, replica_groups=mesh['groups'=2,'seq'=16] {'seq'}, dimensions={0} | all-to-all | bytes 131072 | tf_op jit(solution)/shard_map/all_to_all | solution.py:495
  67.4 0.9 %shuffle.1 = bf16[1,2,2,48,128]{4,3,2,1,0:T(8,128)(2,1)} custom-call(bf16[16,16,128]{2,1,0:T(8,128)(2,1)S(1)} %all_to_all.5.rows_ref), custom_call_target="tpu_custom_call" | custom-call | tf_op jit(solution)/shard_map/shuffle/pallas_call | solution.py:496
  (14 shorter events, 0.1 us)
Async XLA Ops:
  0.0 53.5 %copy-start.2 = (f32[512]{0:T(512)S(1)}, f32[512]{0:T(512)}, u32[]{:S(2)}) copy-start(f32[512]{0:T(512)} %param.15) | copy-start | bytes 6148
  0.0 53.5 %copy-start.1 = (f32[512]{0:T(512)S(1)}, f32[512]{0:T(512)}, u32[]{:S(2)}) copy-start(f32[512]{0:T(512)} %param.13) | copy-start | bytes 6148
  0.0 53.5 %copy-start = (bf16[3,3,3,128,512]{4,3,2,1,0:T(8,128)(2,1)S(1)}, bf16[3,3,3,128,512]{4,3,2,1,0:T(8,128)(2,1)}, u32[]{:S(2)}) copy-start(bf16[3,3,3,128,512]{4,3,2,1,0:T(8,128)(2,1)} %param.12) | copy-start | bytes 10616836
  1.0 10.3 %collective-permute-start = (bf16[3,48,256]{2,1,0:T(8,128)(2,1)S(1)}, bf16[3,48,256]{2,1,0:T(8,128)(2,1)S(1)}, u32[]{:S(2)}, u32[]{:S(2)}) collective-permute-start(bf16[3,48,256]{2,1,0:T(8,128)(2,1)S(1)} %get-tuple-element.31), channel_id=1, source_target_pairs={{0,8},{1,9},{2,10},{3,11},{4,12},{5,13},{6,14},{7,15},{8,0},{9,1},... | collective-permute-start | bytes 221192 | tf_op jit(solution)/shard_map/ppermute | solution.py:404
  5.2 6.7 %collective-permute-start.1 = (bf16[3,48,256]{2,1,0:T(8,128)(2,1)S(1)}, bf16[3,48,256]{2,1,0:T(8,128)(2,1)S(1)}, u32[]{:S(2)}, u32[]{:S(2)}) collective-permute-start(bf16[3,48,256]{2,1,0:T(8,128)(2,1)S(1)} %get-tuple-element.32), channel_id=1, source_target_pairs={{0,1},{1,0},{2,3},{3,2},{4,5},{5,4},{6,7},{7,6},{8,9},{9,8},{10,11... | collective-permute-start | bytes 221192 | tf_op jit(solution)/shard_map/ppermute | solution.py:404
  6.8 5.8 %collective-permute-start.2 = (bf16[3,48,256]{2,1,0:T(8,128)(2,1)S(1)}, bf16[3,48,256]{2,1,0:T(8,128)(2,1)S(1)}, u32[]{:S(2)}, u32[]{:S(2)}) collective-permute-start(bf16[3,48,256]{2,1,0:T(8,128)(2,1)S(1)} %get-tuple-element.33), channel_id=1, source_target_pairs={{0,9},{1,8},{2,11},{3,10},{4,13},{5,12},{6,15},{7,14},{8,1},{9,0},... | collective-permute-start | bytes 221192 | tf_op jit(solution)/shard_map/ppermute | solution.py:404
  7.0 9.2 %collective-permute-start.3 = (bf16[3,48,256]{2,1,0:T(8,128)(2,1)S(1)}, bf16[3,48,256]{2,1,0:T(8,128)(2,1)S(1)}, u32[]{:S(2)}, u32[]{:S(2)}) collective-permute-start(bf16[3,48,256]{2,1,0:T(8,128)(2,1)S(1)} %get-tuple-element.34), channel_id=1, source_target_pairs={{0,2},{1,3},{2,0},{3,1},{4,6},{5,7},{6,4},{7,5},{8,10},{9,11},{10,... | collective-permute-start | bytes 221192 | tf_op jit(solution)/shard_map/ppermute | solution.py:404
  8.8 11.3 %collective-permute-start.4 = (bf16[3,48,256]{2,1,0:T(8,128)(2,1)S(1)}, bf16[3,48,256]{2,1,0:T(8,128)(2,1)S(1)}, u32[]{:S(2)}, u32[]{:S(2)}) collective-permute-start(bf16[3,48,256]{2,1,0:T(8,128)(2,1)S(1)} %get-tuple-element.35), channel_id=1, source_target_pairs={{0,10},{1,11},{2,8},{3,9},{4,14},{5,15},{6,12},{7,13},{8,2},{9,3},... | collective-permute-start | bytes 221192 | tf_op jit(solution)/shard_map/ppermute | solution.py:404
  11.3 8.8 %collective-permute-start.5 = (bf16[3,48,256]{2,1,0:T(8,128)(2,1)S(1)}, bf16[3,48,256]{2,1,0:T(8,128)(2,1)S(1)}, u32[]{:S(2)}, u32[]{:S(2)}) collective-permute-start(bf16[3,48,256]{2,1,0:T(8,128)(2,1)S(1)} %get-tuple-element.36), channel_id=1, source_target_pairs={{0,3},{1,2},{2,1},{3,0},{4,7},{5,6},{6,5},{7,4},{8,11},{9,10},{10,... | collective-permute-start | bytes 221192 | tf_op jit(solution)/shard_map/ppermute | solution.py:404
  11.9 9.1 %collective-permute-start.6 = (bf16[3,48,256]{2,1,0:T(8,128)(2,1)S(1)}, bf16[3,48,256]{2,1,0:T(8,128)(2,1)S(1)}, u32[]{:S(2)}, u32[]{:S(2)}) collective-permute-start(bf16[3,48,256]{2,1,0:T(8,128)(2,1)S(1)} %get-tuple-element.37), channel_id=1, source_target_pairs={{0,11},{1,10},{2,9},{3,8},{4,15},{5,14},{6,13},{7,12},{8,3},{9,2},... | collective-permute-start | bytes 221192 | tf_op jit(solution)/shard_map/ppermute | solution.py:404
  12.6 9.9 %collective-permute-start.7 = (bf16[3,48,256]{2,1,0:T(8,128)(2,1)S(1)}, bf16[3,48,256]{2,1,0:T(8,128)(2,1)S(1)}, u32[]{:S(2)}, u32[]{:S(2)}) collective-permute-start(bf16[3,48,256]{2,1,0:T(8,128)(2,1)S(1)} %get-tuple-element.38), channel_id=1, source_target_pairs={{0,4},{1,5},{2,6},{3,7},{4,0},{5,1},{6,2},{7,3},{8,12},{9,13},{10,... | collective-permute-start | bytes 221192 | tf_op jit(solution)/shard_map/ppermute | solution.py:404
  16.2 9.8 %collective-permute-start.8 = (bf16[3,48,256]{2,1,0:T(8,128)(2,1)S(1)}, bf16[3,48,256]{2,1,0:T(8,128)(2,1)S(1)}, u32[]{:S(2)}, u32[]{:S(2)}) collective-permute-start(bf16[3,48,256]{2,1,0:T(8,128)(2,1)S(1)} %get-tuple-element.39), channel_id=1, source_target_pairs={{0,12},{1,13},{2,14},{3,15},{4,8},{5,9},{6,10},{7,11},{8,4},{9,5},... | collective-permute-start | bytes 221192 | tf_op jit(solution)/shard_map/ppermute | solution.py:404
  20.1 5.9 %collective-permute-start.9 = (bf16[3,48,256]{2,1,0:T(8,128)(2,1)S(1)}, bf16[3,48,256]{2,1,0:T(8,128)(2,1)S(1)}, u32[]{:S(2)}, u32[]{:S(2)}) collective-permute-start(bf16[3,48,256]{2,1,0:T(8,128)(2,1)S(1)} %get-tuple-element.40), channel_id=1, source_target_pairs={{0,5},{1,4},{2,7},{3,6},{4,1},{5,0},{6,3},{7,2},{8,13},{9,12},{10,... | collective-permute-start | bytes 221192 | tf_op jit(solution)/shard_map/ppermute | solution.py:404
  20.1 10.0 %collective-permute-start.10 = (bf16[3,48,256]{2,1,0:T(8,128)(2,1)S(1)}, bf16[3,48,256]{2,1,0:T(8,128)(2,1)S(1)}, u32[]{:S(2)}, u32[]{:S(2)}) collective-permute-start(bf16[3,48,256]{2,1,0:T(8,128)(2,1)S(1)} %get-tuple-element.41), channel_id=1, source_target_pairs={{0,13},{1,12},{2,15},{3,14},{4,9},{5,8},{6,11},{7,10},{8,5},{9,4},... | collective-permute-start | bytes 221192 | tf_op jit(solution)/shard_map/ppermute | solution.py:404
  21.0 9.2 %collective-permute-start.11 = (bf16[3,48,256]{2,1,0:T(8,128)(2,1)S(1)}, bf16[3,48,256]{2,1,0:T(8,128)(2,1)S(1)}, u32[]{:S(2)}, u32[]{:S(2)}) collective-permute-start(bf16[3,48,256]{2,1,0:T(8,128)(2,1)S(1)} %get-tuple-element.42), channel_id=1, source_target_pairs={{0,6},{1,7},{2,4},{3,5},{4,2},{5,3},{6,0},{7,1},{8,14},{9,15},{10,... | collective-permute-start | bytes 221192 | tf_op jit(solution)/shard_map/ppermute | solution.py:404
  22.5 7.9 %collective-permute-start.12 = (bf16[3,48,256]{2,1,0:T(8,128)(2,1)S(1)}, bf16[3,48,256]{2,1,0:T(8,128)(2,1)S(1)}, u32[]{:S(2)}, u32[]{:S(2)}) collective-permute-start(bf16[3,48,256]{2,1,0:T(8,128)(2,1)S(1)} %get-tuple-element.43), channel_id=1, source_target_pairs={{0,14},{1,15},{2,12},{3,13},{4,10},{5,11},{6,8},{7,9},{8,6},{9,7},... | collective-permute-start | bytes 221192 | tf_op jit(solution)/shard_map/ppermute | solution.py:404
  26.1 5.7 %collective-permute-start.13 = (bf16[3,48,256]{2,1,0:T(8,128)(2,1)S(1)}, bf16[3,48,256]{2,1,0:T(8,128)(2,1)S(1)}, u32[]{:S(2)}, u32[]{:S(2)}) collective-permute-start(bf16[3,48,256]{2,1,0:T(8,128)(2,1)S(1)} %get-tuple-element.44), channel_id=1, source_target_pairs={{0,7},{1,6},{2,5},{3,4},{4,3},{5,2},{6,1},{7,0},{8,15},{9,14},{10,... | collective-permute-start | bytes 221192 | tf_op jit(solution)/shard_map/ppermute | solution.py:404
  26.1 7.4 %collective-permute-start.14 = (bf16[3,48,256]{2,1,0:T(8,128)(2,1)S(1)}, bf16[3,48,256]{2,1,0:T(8,128)(2,1)S(1)}, u32[]{:S(2)}, u32[]{:S(2)}) collective-permute-start(bf16[3,48,256]{2,1,0:T(8,128)(2,1)S(1)} %get-tuple-element.45), channel_id=1, source_target_pairs={{0,15},{1,14},{2,13},{3,12},{4,11},{5,10},{6,9},{7,8},{8,7},{9,6},... | collective-permute-start | bytes 221192 | tf_op jit(solution)/shard_map/ppermute | solution.py:404
  35.4 1.4 %collective-permute-start.15 = (bf16[400,128]{1,0:T(8,128)(2,1)S(1)}, bf16[400,128]{1,0:T(8,128)(2,1)S(1)}, u32[]{:S(2)}, u32[]{:S(2)}) collective-permute-start(bf16[400,128]{1,0:T(8,128)(2,1)S(1)} %get-tuple-element.48), channel_id=1, source_target_pairs={{0,1},{1,0},{2,3},{3,2},{4,5},{5,4},{6,7},{7,6},{8,9},{9,8},{10,11... | collective-permute-start | bytes 307208 | tf_op jit(solution)/shard_map/ppermute | solution.py:404
  36.8 4.2 %collective-permute-start.16 = (bf16[200,128]{1,0:T(8,128)(2,1)S(1)}, bf16[200,128]{1,0:T(8,128)(2,1)S(1)}, u32[]{:S(2)}, u32[]{:S(2)}) collective-permute-start(bf16[200,128]{1,0:T(8,128)(2,1)S(1)} %get-tuple-element.50), channel_id=1, source_target_pairs={{0,2},{1,3},{2,0},{3,1},{4,6},{5,7},{6,4},{7,5},{8,10},{9,11},{10,... | collective-permute-start | bytes 153608 | tf_op jit(solution)/shard_map/ppermute | solution.py:404
  41.0 6.6 %collective-permute-start.19 = (bf16[200,128]{1,0:T(8,128)(2,1)S(1)}, bf16[200,128]{1,0:T(8,128)(2,1)S(1)}, u32[]{:S(2)}, u32[]{:S(2)}) collective-permute-start(bf16[200,128]{1,0:T(8,128)(2,1)S(1)} %get-tuple-element.52), channel_id=1, source_target_pairs={{0,12},{1,13},{2,14},{3,15},{4,8},{5,9},{6,10},{7,11},{8,4},{9,5},... | collective-permute-start | bytes 153608 | tf_op jit(solution)/shard_map/ppermute | solution.py:404
  43.1 5.6 %collective-permute-start.18 = (bf16[200,128]{1,0:T(8,128)(2,1)S(1)}, bf16[200,128]{1,0:T(8,128)(2,1)S(1)}, u32[]{:S(2)}, u32[]{:S(2)}) collective-permute-start(bf16[200,128]{1,0:T(8,128)(2,1)S(1)} %get-tuple-element.52), channel_id=1, source_target_pairs={{0,8},{1,9},{2,10},{3,11},{4,12},{5,13},{6,14},{7,15},{8,0},{9,1},... | collective-permute-start | bytes 153608 | tf_op jit(solution)/shard_map/ppermute | solution.py:404
  43.2 5.4 %collective-permute-start.17 = (bf16[200,128]{1,0:T(8,128)(2,1)S(1)}, bf16[200,128]{1,0:T(8,128)(2,1)S(1)}, u32[]{:S(2)}, u32[]{:S(2)}) collective-permute-start(bf16[200,128]{1,0:T(8,128)(2,1)S(1)} %get-tuple-element.52), channel_id=1, source_target_pairs={{0,4},{1,5},{2,6},{3,7},{4,0},{5,1},{6,2},{7,3},{8,12},{9,13},{10,... | collective-permute-start | bytes 153608 | tf_op jit(solution)/shard_map/ppermute | solution.py:404
  48.8 3.9 %collective-permute-start.22 = (bf16[192,128]{1,0:T(8,128)(2,1)S(1)}, bf16[192,128]{1,0:T(8,128)(2,1)S(1)}, u32[]{:S(2)}, u32[]{:S(2)}) collective-permute-start(bf16[192,128]{1,0:T(8,128)(2,1)S(1)} %shard_map.88.rest_0_), channel_id=1, source_target_pairs={{0,3},{1,2},{2,1},{3,0},{4,7},{5,6},{6,5},{7,4},{8,11},{9,10},{10,... | collective-permute-start | bytes 147464 | tf_op jit(solution)/shard_map/ppermute | solution.py:404
  48.8 4.6 %collective-permute-start.21 = (bf16[192,128]{1,0:T(8,128)(2,1)S(1)}, bf16[192,128]{1,0:T(8,128)(2,1)S(1)}, u32[]{:S(2)}, u32[]{:S(2)}) collective-permute-start(bf16[192,128]{1,0:T(8,128)(2,1)S(1)} %shard_map.88.rest_0_), channel_id=1, source_target_pairs={{0,2},{1,3},{2,0},{3,1},{4,6},{5,7},{6,4},{7,5},{8,10},{9,11},{10,... | collective-permute-start | bytes 147464 | tf_op jit(solution)/shard_map/ppermute | solution.py:404
  50.0 3.5 %collective-permute-start.20 = (bf16[192,128]{1,0:T(8,128)(2,1)S(1)}, bf16[192,128]{1,0:T(8,128)(2,1)S(1)}, u32[]{:S(2)}, u32[]{:S(2)}) collective-permute-start(bf16[192,128]{1,0:T(8,128)(2,1)S(1)} %shard_map.88.rest_0_), channel_id=1, source_target_pairs={{0,1},{1,0},{2,3},{3,2},{4,5},{5,4},{6,7},{7,6},{8,9},{9,8},{10,11... | collective-permute-start | bytes 147464 | tf_op jit(solution)/shard_map/ppermute | solution.py:404

commit v3 on v2

--- a/solution.py
+++ b/solution.py
@@ -392,11 +392,13 @@
 
 
 def exchange_order(devices):
-    half = devices // 2
-    order = [0, half]
-    for step in range(1, half):
-        order += [step, half + step]
-    return order
+    half, quarter = devices // 2, devices // 4
+    order = [0]
+    for far_step, near_step in zip(
+        range(half, devices - 1), [*range(quarter, half), *range(1, quarter)]
+    ):
+        order += [far_step, near_step]
+    return order + [devices - 1]
 
 
 def swap(array, step):

time: 68.6 us -> 68.4 us (level)
  starting transfers between devices: 30.5 us -> 33.5 us
  waiting for transfers between devices: 17 us -> 14.2 us
    ppermute x23, starting transfers between devices: 30.5 us -> 33.5 us  [swap(): lax.ppermute(array, 'seq', [(i, i ^ step) for i in range(devices)])]
    ppermute x23, waiting for transfers between devices: 17 us -> 14.2 us  [swap(): lax.ppermute(array, 'seq', [(i, i ^ step) for i in range(devices)])]
  transfers between devices with their start and end apart: 23 -> 23, of which waited for: 10 -> 12; matrix products, arithmetic and copies ran while one was open for 0% -> 0% of each run, Pallas kernels for 4% -> 4%
where the time goes in v3:
time: 68.4 us; the launch traced here: 68.1 us
  starting transfers between devices  33.5 us (49%)
  waiting for transfers between devices  14.2 us (21%)
  Pallas kernels  10.2 us (15%)
  blocking collectives  10.1 us (15%)
    ppermute x23, starting transfers between devices, swap(): lax.ppermute(array, 'seq', [(i, i ^ step) for i in range(devices)])  33.5 us
    ppermute x23, waiting for transfers between devices, swap(): lax.ppermute(array, 'seq', [(i, i ^ step) for i in range(devices)])  14.2 us
    all_to_all x1, blocking collectives, whole_heads(): lax.all_to_all(columns, 'seq', split_axis=0, concat_axis=0, tiled=True)  10.1 us
    pallas_call x8, Pallas kernels, launch(): pl.pallas_call(body, out_shape=outs, in_specs=in_specs, out_specs=jax.tre...  9.26 us
  transfers between devices with their start and end apart: 23, of which 12 were waited for; matrix products, arithmetic and copies ran while one was open for 0% of the time, Pallas kernels for 4%

profile of v3, /device:TPU:0, one launch (start us, length us, event | category | flops | bytes accessed | tf_op | source)
XLA Modules:
  0.0 68.1 jit_solution(11014961360579548093)
XLA Ops:
  0.0 1.0 %shard_map.83 = (bf16[3,48,256]{2,1,0:T(8,128)(2,1)S(1)}, bf16[3,48,256]{2,1,0:T(8,128)(2,1)S(1)}) custom-call(bf16[48,4096]{1,0:T(8,128)(2,1)} %query_ref.3, bf16[48,4096]{1,0:T(8,128)(2,1)} %key_ref.3, bf16[48,4096]{1,0:T(8,128)(2,1)} %value_ref.3), custom_call_target="tpu_custom_call" | custom-call | tf_op jit(solution)/shard_map/pallas_call | solution.py:384
  1.0 4.1 %collective-permute-start = (bf16[3,48,256]{2,1,0:T(8,128)(2,1)S(1)}, bf16[3,48,256]{2,1,0:T(8,128)(2,1)S(1)}, u32[]{:S(2)}, u32[]{:S(2)}) collective-permute-start(bf16[3,48,256]{2,1,0:T(8,128)(2,1)S(1)} %get-tuple-element.31), channel_id=1, source_target_pairs={{0,8},{1,9},{2,10},{3,11},{4,12},{5,13},{6,14},{7,15},{8,0},{9,1},... | collective-permute-start | bytes 221192 | tf_op jit(solution)/shard_map/ppermute | solution.py:406
  5.2 1.6 %collective-permute-start.1 = (bf16[3,48,256]{2,1,0:T(8,128)(2,1)S(1)}, bf16[3,48,256]{2,1,0:T(8,128)(2,1)S(1)}, u32[]{:S(2)}, u32[]{:S(2)}) collective-permute-start(bf16[3,48,256]{2,1,0:T(8,128)(2,1)S(1)} %get-tuple-element.32), channel_id=1, source_target_pairs={{0,4},{1,5},{2,6},{3,7},{4,0},{5,1},{6,2},{7,3},{8,12},{9,13},{10,... | collective-permute-start | bytes 221192 | tf_op jit(solution)/shard_map/ppermute | solution.py:406
  6.8 1.6 %shard_map.84 = (bf16[3,48,256]{2,1,0:T(8,128)(2,1)S(1)}, bf16[3,48,256]{2,1,0:T(8,128)(2,1)S(1)}, bf16[3,48,256]{2,1,0:T(8,128)(2,1)S(1)}, bf16[3,48,256]{2,1,0...) custom-call(bf16[48,4096]{1,0:T(8,128)(2,1)} %query_ref.3, ...), custom_call_target="tpu_custom_call" | custom-call | tf_op jit(solution)/shard_map/pallas_call | solution.py:384
  8.3 0.1 collective-permute-start.2
  8.4 0.2 collective-permute-start.3
  8.6 3.8 %collective-permute-start.4 = (bf16[3,48,256]{2,1,0:T(8,128)(2,1)S(1)}, bf16[3,48,256]{2,1,0:T(8,128)(2,1)S(1)}, u32[]{:S(2)}, u32[]{:S(2)}) collective-permute-start(bf16[3,48,256]{2,1,0:T(8,128)(2,1)S(1)} %get-tuple-element.35), channel_id=1, source_target_pairs={{0,10},{1,11},{2,8},{3,9},{4,14},{5,15},{6,12},{7,13},{8,2},{9,3},... | collective-permute-start | bytes 221192 | tf_op jit(solution)/shard_map/ppermute | solution.py:406
  12.4 0.0 collective-permute-done.rest_0_
  12.4 1.5 %collective-permute-start.5 = (bf16[3,48,256]{2,1,0:T(8,128)(2,1)S(1)}, bf16[3,48,256]{2,1,0:T(8,128)(2,1)S(1)}, u32[]{:S(2)}, u32[]{:S(2)}) collective-permute-start(bf16[3,48,256]{2,1,0:T(8,128)(2,1)S(1)} %get-tuple-element.36), channel_id=1, source_target_pairs={{0,6},{1,7},{2,4},{3,5},{4,2},{5,3},{6,0},{7,1},{8,14},{9,15},{10,... | collective-permute-start | bytes 221192 | tf_op jit(solution)/shard_map/ppermute | solution.py:406
  14.0 0.0 collective-permute-done.1.rest_1_
  14.0 0.5 collective-permute-start.6
  14.4 0.7 %collective-permute-done.2.rest_2_ = bf16[3,48,256]{2,1,0:T(8,128)(2,1)S(1)} collective-permute-done((bf16[3,48,256]{2,1,0:T(8,128)(2,1)S(1)}, bf16[3,48,256]{2,1,0:T(8,128)(2,1)S(1)}, u32[]{:S(2)}, u32[]{:S(2)}) %collective-permute-start.2) | collective-permute-done | bytes 73760 | tf_op jit(solution)/shard_map/ppermute | solution.py:406
  15.2 3.8 %collective-permute-start.8 = (bf16[3,48,256]{2,1,0:T(8,128)(2,1)S(1)}, bf16[3,48,256]{2,1,0:T(8,128)(2,1)S(1)}, u32[]{:S(2)}, u32[]{:S(2)}) collective-permute-start(bf16[3,48,256]{2,1,0:T(8,128)(2,1)S(1)} %get-tuple-element.39), channel_id=1, source_target_pairs={{0,12},{1,13},{2,14},{3,15},{4,8},{5,9},{6,10},{7,11},{8,4},{9,5},... | collective-permute-start | bytes 221192 | tf_op jit(solution)/shard_map/ppermute | solution.py:406
  19.0 0.0 collective-permute-done.4.rest_4_
  19.0 0.1 collective-permute-start.9
  19.1 0.4 collective-permute-done.5.rest_5_
  19.6 2.0 %collective-permute-start.10 = (bf16[3,48,256]{2,1,0:T(8,128)(2,1)S(1)}, bf16[3,48,256]{2,1,0:T(8,128)(2,1)S(1)}, u32[]{:S(2)}, u32[]{:S(2)}) collective-permute-start(bf16[3,48,256]{2,1,0:T(8,128)(2,1)S(1)} %get-tuple-element.41), channel_id=1, source_target_pairs={{0,13},{1,12},{2,15},{3,14},{4,9},{5,8},{6,11},{7,10},{8,5},{9,4},... | collective-permute-start | bytes 221192 | tf_op jit(solution)/shard_map/ppermute | solution.py:406
  21.6 1.4 %collective-permute-done.6.rest_6_ = bf16[3,48,256]{2,1,0:T(8,128)(2,1)S(1)} collective-permute-done((bf16[3,48,256]{2,1,0:T(8,128)(2,1)S(1)}, bf16[3,48,256]{2,1,0:T(8,128)(2,1)S(1)}, u32[]{:S(2)}, u32[]{:S(2)}) %collective-permute-start.6) | collective-permute-done | bytes 73760 | tf_op jit(solution)/shard_map/ppermute | solution.py:406
  22.9 0.3 collective-permute-start.11
  23.3 0.5 collective-permute-done.7.rest_7_
  23.8 0.6 collective-permute-start.12
  24.4 0.9 %collective-permute-start.13 = (bf16[3,48,256]{2,1,0:T(8,128)(2,1)S(1)}, bf16[3,48,256]{2,1,0:T(8,128)(2,1)S(1)}, u32[]{:S(2)}, u32[]{:S(2)}) collective-permute-start(bf16[3,48,256]{2,1,0:T(8,128)(2,1)S(1)} %get-tuple-element.44), channel_id=1, source_target_pairs={{0,3},{1,2},{2,1},{3,0},{4,7},{5,6},{6,5},{7,4},{8,11},{9,10},{10,... | collective-permute-start | bytes 221192 | tf_op jit(solution)/shard_map/ppermute | solution.py:406
  25.4 4.5 %collective-permute-start.14 = (bf16[3,48,256]{2,1,0:T(8,128)(2,1)S(1)}, bf16[3,48,256]{2,1,0:T(8,128)(2,1)S(1)}, u32[]{:S(2)}, u32[]{:S(2)}) collective-permute-start(bf16[3,48,256]{2,1,0:T(8,128)(2,1)S(1)} %get-tuple-element.45), channel_id=1, source_target_pairs={{0,15},{1,14},{2,13},{3,12},{4,11},{5,10},{6,9},{7,8},{8,7},{9,6},... | collective-permute-start | bytes 221192 | tf_op jit(solution)/shard_map/ppermute | solution.py:406
  29.8 1.2 %shard_map.82 = (bf16[256,128]{1,0:T(8,128)(2,1)S(1)}, bf16[3,288,512]{2,1,0:T(8,128)(2,1)S(1)}) custom-call(bf16[4096,128]{1,0:T(8,128)(2,1)} %proj_ref.1, bf16[3,288,512]{2,1,0:T(8,128)(2,1)} %bitcast.9), custom_call_target="tpu_custom_call" | custom-call | tf_op jit(solution)/shard_map/pallas_call | solution.py:384
  31.1 0.0 collective-permute-done.10.rest_10_
  31.1 0.0 collective-permute-done.13.rest_13_
  31.1 0.8 %collective-permute-done.14.rest_14_ = bf16[3,48,256]{2,1,0:T(8,128)(2,1)S(1)} collective-permute-done((bf16[3,48,256]{2,1,0:T(8,128)(2,1)S(1)}, bf16[3,48,256]{2,1,0:T(8,128)(2,1)S(1)}, u32[]{:S(2)}, u32[]{:S(2)}) %collective-permute-start.14) | collective-permute-done | bytes 73760 | tf_op jit(solution)/shard_map/ppermute | solution.py:406
  31.9 1.9 %shard_map.85 = (f32[392,128]{1,0:T(8,128)S(1)}, bf16[400,128]{1,0:T(8,128)(2,1)S(1)}) custom-call(bf16[256,128]{1,0:T(8,128)(2,1)S(1)} %get-tuple-element.30.proj_ref, bf16[3,48,256]{2,1,0:T(8,128)(2,1)S(1)} %collective-permute-done.rest_0_, bf16[3,48,256]{2,1,0:T(8,128)(2,1)S(1)} %collective-permute-done.1.rest_1_, ...), custom_call_target="tpu_custom_call" | custom-call | tf_op jit(solution)/shard_map/pallas_call | solution.py:384
  33.8 0.7 %collective-permute-start.15 = (bf16[400,128]{1,0:T(8,128)(2,1)S(1)}, bf16[400,128]{1,0:T(8,128)(2,1)S(1)}, u32[]{:S(2)}, u32[]{:S(2)}) collective-permute-start(bf16[400,128]{1,0:T(8,128)(2,1)S(1)} %get-tuple-element.48), channel_id=1, source_target_pairs={{0,1},{1,0},{2,3},{3,2},{4,5},{5,4},{6,7},{7,6},{8,9},{9,8},{10,11... | collective-permute-start | bytes 307208 | tf_op jit(solution)/shard_map/ppermute | solution.py:406
  34.5 0.9 %collective-permute-done.15.got_ref = bf16[400,128]{1,0:T(8,128)(2,1)S(1)} collective-permute-done((bf16[400,128]{1,0:T(8,128)(2,1)S(1)}, bf16[400,128]{1,0:T(8,128)(2,1)S(1)}, u32[]{:S(2)}, u32[]{:S(2)}) %collective-permute-start.15) | collective-permute-done | bytes 102432 | tf_op jit(solution)/shard_map/ppermute | solution.py:406
  35.5 2.0 %collective-permute-start.16 = (bf16[200,128]{1,0:T(8,128)(2,1)S(1)}, bf16[200,128]{1,0:T(8,128)(2,1)S(1)}, u32[]{:S(2)}, u32[]{:S(2)}) collective-permute-start(bf16[200,128]{1,0:T(8,128)(2,1)S(1)} %get-tuple-element.50), channel_id=1, source_target_pairs={{0,2},{1,3},{2,0},{3,1},{4,6},{5,7},{6,4},{7,5},{8,10},{9,11},{10,... | collective-permute-start | bytes 153608 | tf_op jit(solution)/shard_map/ppermute | solution.py:406
  37.6 2.1 %collective-permute-done.16.got_ref = bf16[200,128]{1,0:T(8,128)(2,1)S(1)} collective-permute-done((bf16[200,128]{1,0:T(8,128)(2,1)S(1)}, bf16[200,128]{1,0:T(8,128)(2,1)S(1)}, u32[]{:S(2)}, u32[]{:S(2)}) %collective-permute-start.16) | collective-permute-done | bytes 51232 | tf_op jit(solution)/shard_map/ppermute | solution.py:406
  39.7 3.3 %collective-permute-start.19 = (bf16[200,128]{1,0:T(8,128)(2,1)S(1)}, bf16[200,128]{1,0:T(8,128)(2,1)S(1)}, u32[]{:S(2)}, u32[]{:S(2)}) collective-permute-start(bf16[200,128]{1,0:T(8,128)(2,1)S(1)} %get-tuple-element.52), channel_id=1, source_target_pairs={{0,12},{1,13},{2,14},{3,15},{4,8},{5,9},{6,10},{7,11},{8,4},{9,5},... | collective-permute-start | bytes 153608 | tf_op jit(solution)/shard_map/ppermute | solution.py:406
  43.1 1.3 %collective-permute-start.18 = (bf16[200,128]{1,0:T(8,128)(2,1)S(1)}, bf16[200,128]{1,0:T(8,128)(2,1)S(1)}, u32[]{:S(2)}, u32[]{:S(2)}) collective-permute-start(bf16[200,128]{1,0:T(8,128)(2,1)S(1)} %get-tuple-element.52), channel_id=1, source_target_pairs={{0,8},{1,9},{2,10},{3,11},{4,12},{5,13},{6,14},{7,15},{8,0},{9,1},... | collective-permute-start | bytes 153608 | tf_op jit(solution)/shard_map/ppermute | solution.py:406
  44.4 0.0 collective-permute-start.17
  44.4 1.7 %collective-permute-done.19.rest_2_ = bf16[200,128]{1,0:T(8,128)(2,1)S(1)} collective-permute-done((bf16[200,128]{1,0:T(8,128)(2,1)S(1)}, bf16[200,128]{1,0:T(8,128)(2,1)S(1)}, u32[]{:S(2)}, u32[]{:S(2)}) %collective-permute-start.19) | collective-permute-done | bytes 51232 | tf_op jit(solution)/shard_map/ppermute | solution.py:406
  46.1 2.2 %collective-permute-done.18.rest_1_ = bf16[200,128]{1,0:T(8,128)(2,1)S(1)} collective-permute-done((bf16[200,128]{1,0:T(8,128)(2,1)S(1)}, bf16[200,128]{1,0:T(8,128)(2,1)S(1)}, u32[]{:S(2)}, u32[]{:S(2)}) %collective-permute-start.18) | collective-permute-done | bytes 51232 | tf_op jit(solution)/shard_map/ppermute | solution.py:406
  48.3 0.5 collective-permute-done.17.rest_0_
  48.9 0.1 shard_map.88.rest_0_
  49.0 0.1 collective-permute-start.22
  49.1 1.3 %collective-permute-start.21 = (bf16[192,128]{1,0:T(8,128)(2,1)S(1)}, bf16[192,128]{1,0:T(8,128)(2,1)S(1)}, u32[]{:S(2)}, u32[]{:S(2)}) collective-permute-start(bf16[192,128]{1,0:T(8,128)(2,1)S(1)} %shard_map.88.rest_0_), channel_id=1, source_target_pairs={{0,2},{1,3},{2,0},{3,1},{4,6},{5,7},{6,4},{7,5},{8,10},{9,11},{10,... | collective-permute-start | bytes 147464 | tf_op jit(solution)/shard_map/ppermute | solution.py:406
  50.4 0.6 collective-permute-start.20
  50.9 2.1 %collective-permute-done.22.rest_3_ = bf16[192,128]{1,0:T(8,128)(2,1)S(1)} collective-permute-done((bf16[192,128]{1,0:T(8,128)(2,1)S(1)}, bf16[192,128]{1,0:T(8,128)(2,1)S(1)}, u32[]{:S(2)}, u32[]{:S(2)}) %collective-permute-start.22) | collective-permute-done | bytes 49184 | tf_op jit(solution)/shard_map/ppermute | solution.py:406
  53.1 0.7 %collective-permute-done.21.rest_2_ = bf16[192,128]{1,0:T(8,128)(2,1)S(1)} collective-permute-done((bf16[192,128]{1,0:T(8,128)(2,1)S(1)}, bf16[192,128]{1,0:T(8,128)(2,1)S(1)}, u32[]{:S(2)}, u32[]{:S(2)}) %collective-permute-start.21) | collective-permute-done | bytes 49184 | tf_op jit(solution)/shard_map/ppermute | solution.py:406
  53.7 0.0 collective-permute-done.20.rest_1_
  53.8 3.3 %shard_map.89 = bf16[16,16,128]{2,1,0:T(8,128)(2,1)S(1)} custom-call(bf16[3456,512]{1,0:T(8,128)(2,1)S(1)} %bitcast.6, f32[1,512]{1,0:T(1,128)S(1)} %bitcast.7, bf16[3,288,512]{2,1,0:T(8,128)(2,1)S(1)} %get-tuple-element.29.mid_weight_ref, f32[1,512]{1,0:T(1,128)S(1)} %bitcast.8, bf16[192,128]{1,0:T(8,128)(2,1)S(1)} %shard_map.88.rest_0_, ...), custom_call_target="tpu_custom_call" | custom-call | tf_op jit(solution)/shard_map/pallas_call | solution.py:384
  57.1 10.1 %all_to_all.5.rows_ref = bf16[16,16,128]{2,1,0:T(8,128)(2,1)S(1)} all-to-all(bf16[16,16,128]{2,1,0:T(8,128)(2,1)S(1)} %shard_map.89), channel_id=1, replica_groups=mesh['groups'=2,'seq'=16] {'seq'}, dimensions={0} | all-to-all | bytes 131072 | tf_op jit(solution)/shard_map/all_to_all | solution.py:497
  67.2 0.9 %shuffle.1 = bf16[1,2,2,48,128]{4,3,2,1,0:T(8,128)(2,1)} custom-call(bf16[16,16,128]{2,1,0:T(8,128)(2,1)S(1)} %all_to_all.5.rows_ref), custom_call_target="tpu_custom_call" | custom-call | tf_op jit(solution)/shard_map/shuffle/pallas_call | solution.py:498
  (14 shorter events, 0.1 us)
Async XLA Ops:
  0.0 53.7 %copy-start.2 = (f32[512]{0:T(512)S(1)}, f32[512]{0:T(512)}, u32[]{:S(2)}) copy-start(f32[512]{0:T(512)} %param.15) | copy-start | bytes 6148
  0.0 53.7 %copy-start.1 = (f32[512]{0:T(512)S(1)}, f32[512]{0:T(512)}, u32[]{:S(2)}) copy-start(f32[512]{0:T(512)} %param.13) | copy-start | bytes 6148
  0.0 53.7 %copy-start = (bf16[3,3,3,128,512]{4,3,2,1,0:T(8,128)(2,1)S(1)}, bf16[3,3,3,128,512]{4,3,2,1,0:T(8,128)(2,1)}, u32[]{:S(2)}) copy-start(bf16[3,3,3,128,512]{4,3,2,1,0:T(8,128)(2,1)} %param.12) | copy-start | bytes 10616836
  1.0 11.4 %collective-permute-start = (bf16[3,48,256]{2,1,0:T(8,128)(2,1)S(1)}, bf16[3,48,256]{2,1,0:T(8,128)(2,1)S(1)}, u32[]{:S(2)}, u32[]{:S(2)}) collective-permute-start(bf16[3,48,256]{2,1,0:T(8,128)(2,1)S(1)} %get-tuple-element.31), channel_id=1, source_target_pairs={{0,8},{1,9},{2,10},{3,11},{4,12},{5,13},{6,14},{7,15},{8,0},{9,1},... | collective-permute-start | bytes 221192 | tf_op jit(solution)/shard_map/ppermute | solution.py:406
  5.2 8.8 %collective-permute-start.1 = (bf16[3,48,256]{2,1,0:T(8,128)(2,1)S(1)}, bf16[3,48,256]{2,1,0:T(8,128)(2,1)S(1)}, u32[]{:S(2)}, u32[]{:S(2)}) collective-permute-start(bf16[3,48,256]{2,1,0:T(8,128)(2,1)S(1)} %get-tuple-element.32), channel_id=1, source_target_pairs={{0,4},{1,5},{2,6},{3,7},{4,0},{5,1},{6,2},{7,3},{8,12},{9,13},{10,... | collective-permute-start | bytes 221192 | tf_op jit(solution)/shard_map/ppermute | solution.py:406
  8.3 6.8 %collective-permute-start.2 = (bf16[3,48,256]{2,1,0:T(8,128)(2,1)S(1)}, bf16[3,48,256]{2,1,0:T(8,128)(2,1)S(1)}, u32[]{:S(2)}, u32[]{:S(2)}) collective-permute-start(bf16[3,48,256]{2,1,0:T(8,128)(2,1)S(1)} %get-tuple-element.33), channel_id=1, source_target_pairs={{0,9},{1,8},{2,11},{3,10},{4,13},{5,12},{6,15},{7,14},{8,1},{9,0},... | collective-permute-start | bytes 221192 | tf_op jit(solution)/shard_map/ppermute | solution.py:406
  8.4 6.7 %collective-permute-start.3 = (bf16[3,48,256]{2,1,0:T(8,128)(2,1)S(1)}, bf16[3,48,256]{2,1,0:T(8,128)(2,1)S(1)}, u32[]{:S(2)}, u32[]{:S(2)}) collective-permute-start(bf16[3,48,256]{2,1,0:T(8,128)(2,1)S(1)} %get-tuple-element.34), channel_id=1, source_target_pairs={{0,5},{1,4},{2,7},{3,6},{4,1},{5,0},{6,3},{7,2},{8,13},{9,12},{10,... | collective-permute-start | bytes 221192 | tf_op jit(solution)/shard_map/ppermute | solution.py:406
  8.6 10.4 %collective-permute-start.4 = (bf16[3,48,256]{2,1,0:T(8,128)(2,1)S(1)}, bf16[3,48,256]{2,1,0:T(8,128)(2,1)S(1)}, u32[]{:S(2)}, u32[]{:S(2)}) collective-permute-start(bf16[3,48,256]{2,1,0:T(8,128)(2,1)S(1)} %get-tuple-element.35), channel_id=1, source_target_pairs={{0,10},{1,11},{2,8},{3,9},{4,14},{5,15},{6,12},{7,13},{8,2},{9,3},... | collective-permute-start | bytes 221192 | tf_op jit(solution)/shard_map/ppermute | solution.py:406
  12.4 7.1 %collective-permute-start.5 = (bf16[3,48,256]{2,1,0:T(8,128)(2,1)S(1)}, bf16[3,48,256]{2,1,0:T(8,128)(2,1)S(1)}, u32[]{:S(2)}, u32[]{:S(2)}) collective-permute-start(bf16[3,48,256]{2,1,0:T(8,128)(2,1)S(1)} %get-tuple-element.36), channel_id=1, source_target_pairs={{0,6},{1,7},{2,4},{3,5},{4,2},{5,3},{6,0},{7,1},{8,14},{9,15},{10,... | collective-permute-start | bytes 221192 | tf_op jit(solution)/shard_map/ppermute | solution.py:406
  14.0 9.0 %collective-permute-start.6 = (bf16[3,48,256]{2,1,0:T(8,128)(2,1)S(1)}, bf16[3,48,256]{2,1,0:T(8,128)(2,1)S(1)}, u32[]{:S(2)}, u32[]{:S(2)}) collective-permute-start(bf16[3,48,256]{2,1,0:T(8,128)(2,1)S(1)} %get-tuple-element.37), channel_id=1, source_target_pairs={{0,11},{1,10},{2,9},{3,8},{4,15},{5,14},{6,13},{7,12},{8,3},{9,2},... | collective-permute-start | bytes 221192 | tf_op jit(solution)/shard_map/ppermute | solution.py:406
  15.1 8.7 %collective-permute-start.7 = (bf16[3,48,256]{2,1,0:T(8,128)(2,1)S(1)}, bf16[3,48,256]{2,1,0:T(8,128)(2,1)S(1)}, u32[]{:S(2)}, u32[]{:S(2)}) collective-permute-start(bf16[3,48,256]{2,1,0:T(8,128)(2,1)S(1)} %get-tuple-element.38), channel_id=1, source_target_pairs={{0,7},{1,6},{2,5},{3,4},{4,3},{5,2},{6,1},{7,0},{8,15},{9,14},{10,... | collective-permute-start | bytes 221192 | tf_op jit(solution)/shard_map/ppermute | solution.py:406
  15.2 9.3 %collective-permute-start.8 = (bf16[3,48,256]{2,1,0:T(8,128)(2,1)S(1)}, bf16[3,48,256]{2,1,0:T(8,128)(2,1)S(1)}, u32[]{:S(2)}, u32[]{:S(2)}) collective-permute-start(bf16[3,48,256]{2,1,0:T(8,128)(2,1)S(1)} %get-tuple-element.39), channel_id=1, source_target_pairs={{0,12},{1,13},{2,14},{3,15},{4,8},{5,9},{6,10},{7,11},{8,4},{9,5},... | collective-permute-start | bytes 221192 | tf_op jit(solution)/shard_map/ppermute | solution.py:406
  19.0 6.3 %collective-permute-start.9 = (bf16[3,48,256]{2,1,0:T(8,128)(2,1)S(1)}, bf16[3,48,256]{2,1,0:T(8,128)(2,1)S(1)}, u32[]{:S(2)}, u32[]{:S(2)}) collective-permute-start(bf16[3,48,256]{2,1,0:T(8,128)(2,1)S(1)} %get-tuple-element.40), channel_id=1, source_target_pairs={{0,1},{1,0},{2,3},{3,2},{4,5},{5,4},{6,7},{7,6},{8,9},{9,8},{10,11... | collective-permute-start | bytes 221192 | tf_op jit(solution)/shard_map/ppermute | solution.py:406
  19.6 11.5 %collective-permute-start.10 = (bf16[3,48,256]{2,1,0:T(8,128)(2,1)S(1)}, bf16[3,48,256]{2,1,0:T(8,128)(2,1)S(1)}, u32[]{:S(2)}, u32[]{:S(2)}) collective-permute-start(bf16[3,48,256]{2,1,0:T(8,128)(2,1)S(1)} %get-tuple-element.41), channel_id=1, source_target_pairs={{0,13},{1,12},{2,15},{3,14},{4,9},{5,8},{6,11},{7,10},{8,5},{9,4},... | collective-permute-start | bytes 221192 | tf_op jit(solution)/shard_map/ppermute | solution.py:406
  22.9 8.1 %collective-permute-start.11 = (bf16[3,48,256]{2,1,0:T(8,128)(2,1)S(1)}, bf16[3,48,256]{2,1,0:T(8,128)(2,1)S(1)}, u32[]{:S(2)}, u32[]{:S(2)}) collective-permute-start(bf16[3,48,256]{2,1,0:T(8,128)(2,1)S(1)} %get-tuple-element.42), channel_id=1, source_target_pairs={{0,2},{1,3},{2,0},{3,1},{4,6},{5,7},{6,4},{7,5},{8,10},{9,11},{10,... | collective-permute-start | bytes 221192 | tf_op jit(solution)/shard_map/ppermute | solution.py:406
  23.8 7.3 %collective-permute-start.12 = (bf16[3,48,256]{2,1,0:T(8,128)(2,1)S(1)}, bf16[3,48,256]{2,1,0:T(8,128)(2,1)S(1)}, u32[]{:S(2)}, u32[]{:S(2)}) collective-permute-start(bf16[3,48,256]{2,1,0:T(8,128)(2,1)S(1)} %get-tuple-element.43), channel_id=1, source_target_pairs={{0,14},{1,15},{2,12},{3,13},{4,10},{5,11},{6,8},{7,9},{8,6},{9,7},... | collective-permute-start | bytes 221192 | tf_op jit(solution)/shard_map/ppermute | solution.py:406
  24.4 6.7 %collective-permute-start.13 = (bf16[3,48,256]{2,1,0:T(8,128)(2,1)S(1)}, bf16[3,48,256]{2,1,0:T(8,128)(2,1)S(1)}, u32[]{:S(2)}, u32[]{:S(2)}) collective-permute-start(bf16[3,48,256]{2,1,0:T(8,128)(2,1)S(1)} %get-tuple-element.44), channel_id=1, source_target_pairs={{0,3},{1,2},{2,1},{3,0},{4,7},{5,6},{6,5},{7,4},{8,11},{9,10},{10,... | collective-permute-start | bytes 221192 | tf_op jit(solution)/shard_map/ppermute | solution.py:406
  25.4 6.5 %collective-permute-start.14 = (bf16[3,48,256]{2,1,0:T(8,128)(2,1)S(1)}, bf16[3,48,256]{2,1,0:T(8,128)(2,1)S(1)}, u32[]{:S(2)}, u32[]{:S(2)}) collective-permute-start(bf16[3,48,256]{2,1,0:T(8,128)(2,1)S(1)} %get-tuple-element.45), channel_id=1, source_target_pairs={{0,15},{1,14},{2,13},{3,12},{4,11},{5,10},{6,9},{7,8},{8,7},{9,6},... | collective-permute-start | bytes 221192 | tf_op jit(solution)/shard_map/ppermute | solution.py:406
  33.8 1.7 %collective-permute-start.15 = (bf16[400,128]{1,0:T(8,128)(2,1)S(1)}, bf16[400,128]{1,0:T(8,128)(2,1)S(1)}, u32[]{:S(2)}, u32[]{:S(2)}) collective-permute-start(bf16[400,128]{1,0:T(8,128)(2,1)S(1)} %get-tuple-element.48), channel_id=1, source_target_pairs={{0,1},{1,0},{2,3},{3,2},{4,5},{5,4},{6,7},{7,6},{8,9},{9,8},{10,11... | collective-permute-start | bytes 307208 | tf_op jit(solution)/shard_map/ppermute | solution.py:406
  35.5 4.2 %collective-permute-start.16 = (bf16[200,128]{1,0:T(8,128)(2,1)S(1)}, bf16[200,128]{1,0:T(8,128)(2,1)S(1)}, u32[]{:S(2)}, u32[]{:S(2)}) collective-permute-start(bf16[200,128]{1,0:T(8,128)(2,1)S(1)} %get-tuple-element.50), channel_id=1, source_target_pairs={{0,2},{1,3},{2,0},{3,1},{4,6},{5,7},{6,4},{7,5},{8,10},{9,11},{10,... | collective-permute-start | bytes 153608 | tf_op jit(solution)/shard_map/ppermute | solution.py:406
  39.7 6.4 %collective-permute-start.19 = (bf16[200,128]{1,0:T(8,128)(2,1)S(1)}, bf16[200,128]{1,0:T(8,128)(2,1)S(1)}, u32[]{:S(2)}, u32[]{:S(2)}) collective-permute-start(bf16[200,128]{1,0:T(8,128)(2,1)S(1)} %get-tuple-element.52), channel_id=1, source_target_pairs={{0,12},{1,13},{2,14},{3,15},{4,8},{5,9},{6,10},{7,11},{8,4},{9,5},... | collective-permute-start | bytes 153608 | tf_op jit(solution)/shard_map/ppermute | solution.py:406
  43.1 5.2 %collective-permute-start.18 = (bf16[200,128]{1,0:T(8,128)(2,1)S(1)}, bf16[200,128]{1,0:T(8,128)(2,1)S(1)}, u32[]{:S(2)}, u32[]{:S(2)}) collective-permute-start(bf16[200,128]{1,0:T(8,128)(2,1)S(1)} %get-tuple-element.52), channel_id=1, source_target_pairs={{0,8},{1,9},{2,10},{3,11},{4,12},{5,13},{6,14},{7,15},{8,0},{9,1},... | collective-permute-start | bytes 153608 | tf_op jit(solution)/shard_map/ppermute | solution.py:406
  44.4 4.5 %collective-permute-start.17 = (bf16[200,128]{1,0:T(8,128)(2,1)S(1)}, bf16[200,128]{1,0:T(8,128)(2,1)S(1)}, u32[]{:S(2)}, u32[]{:S(2)}) collective-permute-start(bf16[200,128]{1,0:T(8,128)(2,1)S(1)} %get-tuple-element.52), channel_id=1, source_target_pairs={{0,4},{1,5},{2,6},{3,7},{4,0},{5,1},{6,2},{7,3},{8,12},{9,13},{10,... | collective-permute-start | bytes 153608 | tf_op jit(solution)/shard_map/ppermute | solution.py:406
  49.0 4.1 %collective-permute-start.22 = (bf16[192,128]{1,0:T(8,128)(2,1)S(1)}, bf16[192,128]{1,0:T(8,128)(2,1)S(1)}, u32[]{:S(2)}, u32[]{:S(2)}) collective-permute-start(bf16[192,128]{1,0:T(8,128)(2,1)S(1)} %shard_map.88.rest_0_), channel_id=1, source_target_pairs={{0,3},{1,2},{2,1},{3,0},{4,7},{5,6},{6,5},{7,4},{8,11},{9,10},{10,... | collective-permute-start | bytes 147464 | tf_op jit(solution)/shard_map/ppermute | solution.py:406
  49.1 4.7 %collective-permute-start.21 = (bf16[192,128]{1,0:T(8,128)(2,1)S(1)}, bf16[192,128]{1,0:T(8,128)(2,1)S(1)}, u32[]{:S(2)}, u32[]{:S(2)}) collective-permute-start(bf16[192,128]{1,0:T(8,128)(2,1)S(1)} %shard_map.88.rest_0_), channel_id=1, source_target_pairs={{0,2},{1,3},{2,0},{3,1},{4,6},{5,7},{6,4},{7,5},{8,10},{9,11},{10,... | collective-permute-start | bytes 147464 | tf_op jit(solution)/shard_map/ppermute | solution.py:406
  50.4 3.4 %collective-permute-start.20 = (bf16[192,128]{1,0:T(8,128)(2,1)S(1)}, bf16[192,128]{1,0:T(8,128)(2,1)S(1)}, u32[]{:S(2)}, u32[]{:S(2)}) collective-permute-start(bf16[192,128]{1,0:T(8,128)(2,1)S(1)} %shard_map.88.rest_0_), channel_id=1, source_target_pairs={{0,1},{1,0},{2,3},{3,2},{4,5},{5,4},{6,7},{7,6},{8,9},{9,8},{10,11... | collective-permute-start | bytes 147464 | tf_op jit(solution)/shard_map/ppermute | solution.py:406

commit v4 on v2

--- a/solution.py
+++ b/solution.py
@@ -293,15 +293,14 @@
                 at = ((index * 3 + row_off) * 3 + col_off) * C_LAT
                 cols[:, at : at + C_LAT] = piece.astype(jnp.bfloat16)
     deep = 9 * C_LAT
-    firsts = []
-    actives = []
+    products = []
     for index in range(F):
         low = (F - 1 - index) * deep
-        first = (
-            dot_f32(cols[...], in_weight_ref[low : low + F * deep, :]) + in_bias_ref[...]
-        ).astype(jnp.bfloat16)
+        products.append(dot_f32(cols[...], in_weight_ref[low : low + F * deep, :]))
+    firsts = [(product + in_bias_ref[...]).astype(jnp.bfloat16) for product in products]
+    actives = []
+    for first in firsts:
         wide = first.astype(jnp.float32)
-        firsts.append(first)
         actives.append((wide * lax.logistic(wide)).astype(jnp.bfloat16))
     channel = lax.broadcasted_iota(jnp.int32, (own, CH), 1)
     mine = channel == lax.broadcasted_iota(jnp.int32, (own, CH), 0) + rank * own

time: 68.6 us -> 68.6 us (level)
  no operation moved by 1% of the time
where the time goes in v4:
time: 68.6 us; the launch traced here: 68.3 us
  starting transfers between devices  30.5 us (44%)
  waiting for transfers between devices  17 us (25%)
  blocking collectives  10.6 us (15%)
  Pallas kernels  10.2 us (15%)
    ppermute x23, starting transfers between devices, swap(): lax.ppermute(array, 'seq', [(i, i ^ step) for i in range(devices)])  30.5 us
    ppermute x23, waiting for transfers between devices, swap(): lax.ppermute(array, 'seq', [(i, i ^ step) for i in range(devices)])  17 us
    all_to_all x1, blocking collectives, whole_heads(): lax.all_to_all(columns, 'seq', split_axis=0, concat_axis=0, tiled=True)  10.6 us
    pallas_call x8, Pallas kernels, launch(): pl.pallas_call(body, out_shape=outs, in_specs=in_specs, out_specs=jax.tre...  9.25 us
  transfers between devices with their start and end apart: 23, of which 10 were waited for; matrix products, arithmetic and copies ran while one was open for 0% of the time, Pallas kernels for 4%

profile of v4, /device:TPU:0, one launch (start us, length us, event | category | flops | bytes accessed | tf_op | source)
XLA Modules:
  0.0 68.3 jit_solution(7731646754839454951)
XLA Ops:
  0.0 1.0 %shard_map.83 = (bf16[3,48,256]{2,1,0:T(8,128)(2,1)S(1)}, bf16[3,48,256]{2,1,0:T(8,128)(2,1)S(1)}) custom-call(bf16[48,4096]{1,0:T(8,128)(2,1)} %query_ref.3, bf16[48,4096]{1,0:T(8,128)(2,1)} %key_ref.3, bf16[48,4096]{1,0:T(8,128)(2,1)} %value_ref.3), custom_call_target="tpu_custom_call" | custom-call | tf_op jit(solution)/shard_map/pallas_call | solution.py:383
  1.0 4.1 %collective-permute-start = (bf16[3,48,256]{2,1,0:T(8,128)(2,1)S(1)}, bf16[3,48,256]{2,1,0:T(8,128)(2,1)S(1)}, u32[]{:S(2)}, u32[]{:S(2)}) collective-permute-start(bf16[3,48,256]{2,1,0:T(8,128)(2,1)S(1)} %get-tuple-element.31), channel_id=1, source_target_pairs={{0,8},{1,9},{2,10},{3,11},{4,12},{5,13},{6,14},{7,15},{8,0},{9,1},... | collective-permute-start | bytes 221192 | tf_op jit(solution)/shard_map/ppermute | solution.py:403
  5.2 0.0 collective-permute-start.1
  5.2 1.6 %shard_map.84 = (bf16[3,48,256]{2,1,0:T(8,128)(2,1)S(1)}, bf16[3,48,256]{2,1,0:T(8,128)(2,1)S(1)}, bf16[3,48,256]{2,1,0:T(8,128)(2,1)S(1)}, bf16[3,48,256]{2,1,0...) custom-call(bf16[48,4096]{1,0:T(8,128)(2,1)} %query_ref.3, ...), custom_call_target="tpu_custom_call" | custom-call | tf_op jit(solution)/shard_map/pallas_call | solution.py:383
  6.8 0.3 collective-permute-start.2
  7.0 1.8 %collective-permute-start.3 = (bf16[3,48,256]{2,1,0:T(8,128)(2,1)S(1)}, bf16[3,48,256]{2,1,0:T(8,128)(2,1)S(1)}, u32[]{:S(2)}, u32[]{:S(2)}) collective-permute-start(bf16[3,48,256]{2,1,0:T(8,128)(2,1)S(1)} %get-tuple-element.34), channel_id=1, source_target_pairs={{0,2},{1,3},{2,0},{3,1},{4,6},{5,7},{6,4},{7,5},{8,10},{9,11},{10,... | collective-permute-start | bytes 221192 | tf_op jit(solution)/shard_map/ppermute | solution.py:403
  8.8 2.5 %collective-permute-start.4 = (bf16[3,48,256]{2,1,0:T(8,128)(2,1)S(1)}, bf16[3,48,256]{2,1,0:T(8,128)(2,1)S(1)}, u32[]{:S(2)}, u32[]{:S(2)}) collective-permute-start(bf16[3,48,256]{2,1,0:T(8,128)(2,1)S(1)} %get-tuple-element.35), channel_id=1, source_target_pairs={{0,10},{1,11},{2,8},{3,9},{4,14},{5,15},{6,12},{7,13},{8,2},{9,3},... | collective-permute-start | bytes 221192 | tf_op jit(solution)/shard_map/ppermute | solution.py:403
  11.3 0.0 collective-permute-done.rest_0_
  11.3 0.6 collective-permute-start.5
  11.9 0.0 collective-permute-done.1.rest_1_
  11.9 0.7 %collective-permute-start.6 = (bf16[3,48,256]{2,1,0:T(8,128)(2,1)S(1)}, bf16[3,48,256]{2,1,0:T(8,128)(2,1)S(1)}, u32[]{:S(2)}, u32[]{:S(2)}) collective-permute-start(bf16[3,48,256]{2,1,0:T(8,128)(2,1)S(1)} %get-tuple-element.37), channel_id=1, source_target_pairs={{0,11},{1,10},{2,9},{3,8},{4,15},{5,14},{6,13},{7,12},{8,3},{9,2},... | collective-permute-start | bytes 221192 | tf_op jit(solution)/shard_map/ppermute | solution.py:403
  12.6 0.0 collective-permute-done.2.rest_2_
  12.6 3.6 %collective-permute-start.7 = (bf16[3,48,256]{2,1,0:T(8,128)(2,1)S(1)}, bf16[3,48,256]{2,1,0:T(8,128)(2,1)S(1)}, u32[]{:S(2)}, u32[]{:S(2)}) collective-permute-start(bf16[3,48,256]{2,1,0:T(8,128)(2,1)S(1)} %get-tuple-element.38), channel_id=1, source_target_pairs={{0,4},{1,5},{2,6},{3,7},{4,0},{5,1},{6,2},{7,3},{8,12},{9,13},{10,... | collective-permute-start | bytes 221192 | tf_op jit(solution)/shard_map/ppermute | solution.py:403
  16.2 0.7 collective-permute-start.8
  16.9 3.2 %collective-permute-done.4.rest_4_ = bf16[3,48,256]{2,1,0:T(8,128)(2,1)S(1)} collective-permute-done((bf16[3,48,256]{2,1,0:T(8,128)(2,1)S(1)}, bf16[3,48,256]{2,1,0:T(8,128)(2,1)S(1)}, u32[]{:S(2)}, u32[]{:S(2)}) %collective-permute-start.4) | collective-permute-done | bytes 73760 | tf_op jit(solution)/shard_map/ppermute | solution.py:403
  20.1 0.8 %collective-permute-start.10 = (bf16[3,48,256]{2,1,0:T(8,128)(2,1)S(1)}, bf16[3,48,256]{2,1,0:T(8,128)(2,1)S(1)}, u32[]{:S(2)}, u32[]{:S(2)}) collective-permute-start(bf16[3,48,256]{2,1,0:T(8,128)(2,1)S(1)} %get-tuple-element.41), channel_id=1, source_target_pairs={{0,13},{1,12},{2,15},{3,14},{4,9},{5,8},{6,11},{7,10},{8,5},{9,4},... | collective-permute-start | bytes 221192 | tf_op jit(solution)/shard_map/ppermute | solution.py:403
  21.0 1.5 %collective-permute-start.11 = (bf16[3,48,256]{2,1,0:T(8,128)(2,1)S(1)}, bf16[3,48,256]{2,1,0:T(8,128)(2,1)S(1)}, u32[]{:S(2)}, u32[]{:S(2)}) collective-permute-start(bf16[3,48,256]{2,1,0:T(8,128)(2,1)S(1)} %get-tuple-element.42), channel_id=1, source_target_pairs={{0,6},{1,7},{2,4},{3,5},{4,2},{5,3},{6,0},{7,1},{8,14},{9,15},{10,... | collective-permute-start | bytes 221192 | tf_op jit(solution)/shard_map/ppermute | solution.py:403
  22.5 0.0 collective-permute-done.7.rest_7_
  22.5 3.6 %collective-permute-start.12 = (bf16[3,48,256]{2,1,0:T(8,128)(2,1)S(1)}, bf16[3,48,256]{2,1,0:T(8,128)(2,1)S(1)}, u32[]{:S(2)}, u32[]{:S(2)}) collective-permute-start(bf16[3,48,256]{2,1,0:T(8,128)(2,1)S(1)} %get-tuple-element.43), channel_id=1, source_target_pairs={{0,14},{1,15},{2,12},{3,13},{4,10},{5,11},{6,8},{7,9},{8,6},{9,7},... | collective-permute-start | bytes 221192 | tf_op jit(solution)/shard_map/ppermute | solution.py:403
  26.1 0.0 collective-permute-done.8.rest_8_
  26.1 0.0 collective-permute-start.13
  26.1 2.9 %collective-permute-start.14 = (bf16[3,48,256]{2,1,0:T(8,128)(2,1)S(1)}, bf16[3,48,256]{2,1,0:T(8,128)(2,1)S(1)}, u32[]{:S(2)}, u32[]{:S(2)}) collective-permute-start(bf16[3,48,256]{2,1,0:T(8,128)(2,1)S(1)} %get-tuple-element.45), channel_id=1, source_target_pairs={{0,15},{1,14},{2,13},{3,12},{4,11},{5,10},{6,9},{7,8},{8,7},{9,6},... | collective-permute-start | bytes 221192 | tf_op jit(solution)/shard_map/ppermute | solution.py:403
  28.9 1.2 %shard_map.82 = (bf16[256,128]{1,0:T(8,128)(2,1)S(1)}, bf16[3,288,512]{2,1,0:T(8,128)(2,1)S(1)}) custom-call(bf16[4096,128]{1,0:T(8,128)(2,1)} %proj_ref.1, bf16[3,288,512]{2,1,0:T(8,128)(2,1)} %bitcast.9), custom_call_target="tpu_custom_call" | custom-call | tf_op jit(solution)/shard_map/pallas_call | solution.py:383
  30.2 0.0 collective-permute-done.10.rest_10_
  30.2 0.0 collective-permute-done.11.rest_11_
  30.2 0.2 collective-permute-done.12.rest_12_
  30.4 1.3 %collective-permute-done.13.rest_13_ = bf16[3,48,256]{2,1,0:T(8,128)(2,1)S(1)} collective-permute-done((bf16[3,48,256]{2,1,0:T(8,128)(2,1)S(1)}, bf16[3,48,256]{2,1,0:T(8,128)(2,1)S(1)}, u32[]{:S(2)}, u32[]{:S(2)}) %collective-permute-start.13) | collective-permute-done | bytes 73760 | tf_op jit(solution)/shard_map/ppermute | solution.py:403
  31.7 1.7 %collective-permute-done.14.rest_14_ = bf16[3,48,256]{2,1,0:T(8,128)(2,1)S(1)} collective-permute-done((bf16[3,48,256]{2,1,0:T(8,128)(2,1)S(1)}, bf16[3,48,256]{2,1,0:T(8,128)(2,1)S(1)}, u32[]{:S(2)}, u32[]{:S(2)}) %collective-permute-start.14) | collective-permute-done | bytes 73760 | tf_op jit(solution)/shard_map/ppermute | solution.py:403
  33.5 1.9 %shard_map.85 = (f32[392,128]{1,0:T(8,128)S(1)}, bf16[400,128]{1,0:T(8,128)(2,1)S(1)}) custom-call(bf16[256,128]{1,0:T(8,128)(2,1)S(1)} %get-tuple-element.30.proj_ref, bf16[3,48,256]{2,1,0:T(8,128)(2,1)S(1)} %collective-permute-done.rest_0_, bf16[3,48,256]{2,1,0:T(8,128)(2,1)S(1)} %collective-permute-done.1.rest_1_, ...), custom_call_target="tpu_custom_call" | custom-call | tf_op jit(solution)/shard_map/pallas_call | solution.py:383
  35.4 0.1 collective-permute-start.15
  35.6 1.2 %collective-permute-done.15.got_ref = bf16[400,128]{1,0:T(8,128)(2,1)S(1)} collective-permute-done((bf16[400,128]{1,0:T(8,128)(2,1)S(1)}, bf16[400,128]{1,0:T(8,128)(2,1)S(1)}, u32[]{:S(2)}, u32[]{:S(2)}) %collective-permute-start.15) | collective-permute-done | bytes 102432 | tf_op jit(solution)/shard_map/ppermute | solution.py:403
  36.8 0.9 %collective-permute-start.16 = (bf16[200,128]{1,0:T(8,128)(2,1)S(1)}, bf16[200,128]{1,0:T(8,128)(2,1)S(1)}, u32[]{:S(2)}, u32[]{:S(2)}) collective-permute-start(bf16[200,128]{1,0:T(8,128)(2,1)S(1)} %get-tuple-element.50), channel_id=1, source_target_pairs={{0,2},{1,3},{2,0},{3,1},{4,6},{5,7},{6,4},{7,5},{8,10},{9,11},{10,... | collective-permute-start | bytes 153608 | tf_op jit(solution)/shard_map/ppermute | solution.py:403
  37.8 3.2 %collective-permute-done.16.got_ref = bf16[200,128]{1,0:T(8,128)(2,1)S(1)} collective-permute-done((bf16[200,128]{1,0:T(8,128)(2,1)S(1)}, bf16[200,128]{1,0:T(8,128)(2,1)S(1)}, u32[]{:S(2)}, u32[]{:S(2)}) %collective-permute-start.16) | collective-permute-done | bytes 51232 | tf_op jit(solution)/shard_map/ppermute | solution.py:403
  41.0 2.0 %collective-permute-start.19 = (bf16[200,128]{1,0:T(8,128)(2,1)S(1)}, bf16[200,128]{1,0:T(8,128)(2,1)S(1)}, u32[]{:S(2)}, u32[]{:S(2)}) collective-permute-start(bf16[200,128]{1,0:T(8,128)(2,1)S(1)} %get-tuple-element.52), channel_id=1, source_target_pairs={{0,12},{1,13},{2,14},{3,15},{4,8},{5,9},{6,10},{7,11},{8,4},{9,5},... | collective-permute-start | bytes 153608 | tf_op jit(solution)/shard_map/ppermute | solution.py:403
  43.1 0.2 collective-permute-start.18
  43.2 2.3 %collective-permute-start.17 = (bf16[200,128]{1,0:T(8,128)(2,1)S(1)}, bf16[200,128]{1,0:T(8,128)(2,1)S(1)}, u32[]{:S(2)}, u32[]{:S(2)}) collective-permute-start(bf16[200,128]{1,0:T(8,128)(2,1)S(1)} %get-tuple-element.52), channel_id=1, source_target_pairs={{0,4},{1,5},{2,6},{3,7},{4,0},{5,1},{6,2},{7,3},{8,12},{9,13},{10,... | collective-permute-start | bytes 153608 | tf_op jit(solution)/shard_map/ppermute | solution.py:403
  45.5 2.2 %collective-permute-done.19.rest_2_ = bf16[200,128]{1,0:T(8,128)(2,1)S(1)} collective-permute-done((bf16[200,128]{1,0:T(8,128)(2,1)S(1)}, bf16[200,128]{1,0:T(8,128)(2,1)S(1)}, u32[]{:S(2)}, u32[]{:S(2)}) %collective-permute-start.19) | collective-permute-done | bytes 51232 | tf_op jit(solution)/shard_map/ppermute | solution.py:403
  47.6 1.0 %collective-permute-done.18.rest_1_ = bf16[200,128]{1,0:T(8,128)(2,1)S(1)} collective-permute-done((bf16[200,128]{1,0:T(8,128)(2,1)S(1)}, bf16[200,128]{1,0:T(8,128)(2,1)S(1)}, u32[]{:S(2)}, u32[]{:S(2)}) %collective-permute-start.18) | collective-permute-done | bytes 51232 | tf_op jit(solution)/shard_map/ppermute | solution.py:403
  48.6 0.0 collective-permute-done.17.rest_0_
  48.6 0.1 shard_map.88.rest_0_
  48.8 0.1 collective-permute-start.22
  48.8 1.2 %collective-permute-start.21 = (bf16[192,128]{1,0:T(8,128)(2,1)S(1)}, bf16[192,128]{1,0:T(8,128)(2,1)S(1)}, u32[]{:S(2)}, u32[]{:S(2)}) collective-permute-start(bf16[192,128]{1,0:T(8,128)(2,1)S(1)} %shard_map.88.rest_0_), channel_id=1, source_target_pairs={{0,2},{1,3},{2,0},{3,1},{4,6},{5,7},{6,4},{7,5},{8,10},{9,11},{10,... | collective-permute-start | bytes 147464 | tf_op jit(solution)/shard_map/ppermute | solution.py:403
  50.0 0.7 collective-permute-start.20
  50.7 1.9 %collective-permute-done.22.rest_3_ = bf16[192,128]{1,0:T(8,128)(2,1)S(1)} collective-permute-done((bf16[192,128]{1,0:T(8,128)(2,1)S(1)}, bf16[192,128]{1,0:T(8,128)(2,1)S(1)}, u32[]{:S(2)}, u32[]{:S(2)}) %collective-permute-start.22) | collective-permute-done | bytes 49184 | tf_op jit(solution)/shard_map/ppermute | solution.py:403
  52.6 0.9 %collective-permute-done.21.rest_2_ = bf16[192,128]{1,0:T(8,128)(2,1)S(1)} collective-permute-done((bf16[192,128]{1,0:T(8,128)(2,1)S(1)}, bf16[192,128]{1,0:T(8,128)(2,1)S(1)}, u32[]{:S(2)}, u32[]{:S(2)}) %collective-permute-start.21) | collective-permute-done | bytes 49184 | tf_op jit(solution)/shard_map/ppermute | solution.py:403
  53.5 3.3 %shard_map.89 = bf16[16,16,128]{2,1,0:T(8,128)(2,1)S(1)} custom-call(bf16[3456,512]{1,0:T(8,128)(2,1)S(1)} %bitcast.6, f32[1,512]{1,0:T(1,128)S(1)} %bitcast.7, bf16[3,288,512]{2,1,0:T(8,128)(2,1)S(1)} %get-tuple-element.29.mid_weight_ref, f32[1,512]{1,0:T(1,128)S(1)} %bitcast.8, bf16[192,128]{1,0:T(8,128)(2,1)S(1)} %shard_map.88.rest_0_, ...), custom_call_target="tpu_custom_call" | custom-call | tf_op jit(solution)/shard_map/pallas_call | solution.py:383
  56.9 10.6 %all_to_all.5.rows_ref = bf16[16,16,128]{2,1,0:T(8,128)(2,1)S(1)} all-to-all(bf16[16,16,128]{2,1,0:T(8,128)(2,1)S(1)} %shard_map.89), channel_id=1, replica_groups=mesh['groups'=2,'seq'=16] {'seq'}, dimensions={0} | all-to-all | bytes 131072 | tf_op jit(solution)/shard_map/all_to_all | solution.py:494
  67.4 0.9 %shuffle.1 = bf16[1,2,2,48,128]{4,3,2,1,0:T(8,128)(2,1)} custom-call(bf16[16,16,128]{2,1,0:T(8,128)(2,1)S(1)} %all_to_all.5.rows_ref), custom_call_target="tpu_custom_call" | custom-call | tf_op jit(solution)/shard_map/shuffle/pallas_call | solution.py:495
  (14 shorter events, 0.1 us)
Async XLA Ops:
  0.0 53.5 %copy-start.2 = (f32[512]{0:T(512)S(1)}, f32[512]{0:T(512)}, u32[]{:S(2)}) copy-start(f32[512]{0:T(512)} %param.15) | copy-start | bytes 6148
  0.0 53.5 %copy-start.1 = (f32[512]{0:T(512)S(1)}, f32[512]{0:T(512)}, u32[]{:S(2)}) copy-start(f32[512]{0:T(512)} %param.13) | copy-start | bytes 6148
  0.0 53.5 %copy-start = (bf16[3,3,3,128,512]{4,3,2,1,0:T(8,128)(2,1)S(1)}, bf16[3,3,3,128,512]{4,3,2,1,0:T(8,128)(2,1)}, u32[]{:S(2)}) copy-start(bf16[3,3,3,128,512]{4,3,2,1,0:T(8,128)(2,1)} %param.12) | copy-start | bytes 10616836
  1.0 10.3 %collective-permute-start = (bf16[3,48,256]{2,1,0:T(8,128)(2,1)S(1)}, bf16[3,48,256]{2,1,0:T(8,128)(2,1)S(1)}, u32[]{:S(2)}, u32[]{:S(2)}) collective-permute-start(bf16[3,48,256]{2,1,0:T(8,128)(2,1)S(1)} %get-tuple-element.31), channel_id=1, source_target_pairs={{0,8},{1,9},{2,10},{3,11},{4,12},{5,13},{6,14},{7,15},{8,0},{9,1},... | collective-permute-start | bytes 221192 | tf_op jit(solution)/shard_map/ppermute | solution.py:403
  5.2 6.7 %collective-permute-start.1 = (bf16[3,48,256]{2,1,0:T(8,128)(2,1)S(1)}, bf16[3,48,256]{2,1,0:T(8,128)(2,1)S(1)}, u32[]{:S(2)}, u32[]{:S(2)}) collective-permute-start(bf16[3,48,256]{2,1,0:T(8,128)(2,1)S(1)} %get-tuple-element.32), channel_id=1, source_target_pairs={{0,1},{1,0},{2,3},{3,2},{4,5},{5,4},{6,7},{7,6},{8,9},{9,8},{10,11... | collective-permute-start | bytes 221192 | tf_op jit(solution)/shard_map/ppermute | solution.py:403
  6.8 5.8 %collective-permute-start.2 = (bf16[3,48,256]{2,1,0:T(8,128)(2,1)S(1)}, bf16[3,48,256]{2,1,0:T(8,128)(2,1)S(1)}, u32[]{:S(2)}, u32[]{:S(2)}) collective-permute-start(bf16[3,48,256]{2,1,0:T(8,128)(2,1)S(1)} %get-tuple-element.33), channel_id=1, source_target_pairs={{0,9},{1,8},{2,11},{3,10},{4,13},{5,12},{6,15},{7,14},{8,1},{9,0},... | collective-permute-start | bytes 221192 | tf_op jit(solution)/shard_map/ppermute | solution.py:403
  7.0 9.2 %collective-permute-start.3 = (bf16[3,48,256]{2,1,0:T(8,128)(2,1)S(1)}, bf16[3,48,256]{2,1,0:T(8,128)(2,1)S(1)}, u32[]{:S(2)}, u32[]{:S(2)}) collective-permute-start(bf16[3,48,256]{2,1,0:T(8,128)(2,1)S(1)} %get-tuple-element.34), channel_id=1, source_target_pairs={{0,2},{1,3},{2,0},{3,1},{4,6},{5,7},{6,4},{7,5},{8,10},{9,11},{10,... | collective-permute-start | bytes 221192 | tf_op jit(solution)/shard_map/ppermute | solution.py:403
  8.8 11.3 %collective-permute-start.4 = (bf16[3,48,256]{2,1,0:T(8,128)(2,1)S(1)}, bf16[3,48,256]{2,1,0:T(8,128)(2,1)S(1)}, u32[]{:S(2)}, u32[]{:S(2)}) collective-permute-start(bf16[3,48,256]{2,1,0:T(8,128)(2,1)S(1)} %get-tuple-element.35), channel_id=1, source_target_pairs={{0,10},{1,11},{2,8},{3,9},{4,14},{5,15},{6,12},{7,13},{8,2},{9,3},... | collective-permute-start | bytes 221192 | tf_op jit(solution)/shard_map/ppermute | solution.py:403
  11.3 8.8 %collective-permute-start.5 = (bf16[3,48,256]{2,1,0:T(8,128)(2,1)S(1)}, bf16[3,48,256]{2,1,0:T(8,128)(2,1)S(1)}, u32[]{:S(2)}, u32[]{:S(2)}) collective-permute-start(bf16[3,48,256]{2,1,0:T(8,128)(2,1)S(1)} %get-tuple-element.36), channel_id=1, source_target_pairs={{0,3},{1,2},{2,1},{3,0},{4,7},{5,6},{6,5},{7,4},{8,11},{9,10},{10,... | collective-permute-start | bytes 221192 | tf_op jit(solution)/shard_map/ppermute | solution.py:403
  11.9 9.1 %collective-permute-start.6 = (bf16[3,48,256]{2,1,0:T(8,128)(2,1)S(1)}, bf16[3,48,256]{2,1,0:T(8,128)(2,1)S(1)}, u32[]{:S(2)}, u32[]{:S(2)}) collective-permute-start(bf16[3,48,256]{2,1,0:T(8,128)(2,1)S(1)} %get-tuple-element.37), channel_id=1, source_target_pairs={{0,11},{1,10},{2,9},{3,8},{4,15},{5,14},{6,13},{7,12},{8,3},{9,2},... | collective-permute-start | bytes 221192 | tf_op jit(solution)/shard_map/ppermute | solution.py:403
  12.6 9.9 %collective-permute-start.7 = (bf16[3,48,256]{2,1,0:T(8,128)(2,1)S(1)}, bf16[3,48,256]{2,1,0:T(8,128)(2,1)S(1)}, u32[]{:S(2)}, u32[]{:S(2)}) collective-permute-start(bf16[3,48,256]{2,1,0:T(8,128)(2,1)S(1)} %get-tuple-element.38), channel_id=1, source_target_pairs={{0,4},{1,5},{2,6},{3,7},{4,0},{5,1},{6,2},{7,3},{8,12},{9,13},{10,... | collective-permute-start | bytes 221192 | tf_op jit(solution)/shard_map/ppermute | solution.py:403
  16.2 9.8 %collective-permute-start.8 = (bf16[3,48,256]{2,1,0:T(8,128)(2,1)S(1)}, bf16[3,48,256]{2,1,0:T(8,128)(2,1)S(1)}, u32[]{:S(2)}, u32[]{:S(2)}) collective-permute-start(bf16[3,48,256]{2,1,0:T(8,128)(2,1)S(1)} %get-tuple-element.39), channel_id=1, source_target_pairs={{0,12},{1,13},{2,14},{3,15},{4,8},{5,9},{6,10},{7,11},{8,4},{9,5},... | collective-permute-start | bytes 221192 | tf_op jit(solution)/shard_map/ppermute | solution.py:403
  20.1 5.9 %collective-permute-start.9 = (bf16[3,48,256]{2,1,0:T(8,128)(2,1)S(1)}, bf16[3,48,256]{2,1,0:T(8,128)(2,1)S(1)}, u32[]{:S(2)}, u32[]{:S(2)}) collective-permute-start(bf16[3,48,256]{2,1,0:T(8,128)(2,1)S(1)} %get-tuple-element.40), channel_id=1, source_target_pairs={{0,5},{1,4},{2,7},{3,6},{4,1},{5,0},{6,3},{7,2},{8,13},{9,12},{10,... | collective-permute-start | bytes 221192 | tf_op jit(solution)/shard_map/ppermute | solution.py:403
  20.1 10.0 %collective-permute-start.10 = (bf16[3,48,256]{2,1,0:T(8,128)(2,1)S(1)}, bf16[3,48,256]{2,1,0:T(8,128)(2,1)S(1)}, u32[]{:S(2)}, u32[]{:S(2)}) collective-permute-start(bf16[3,48,256]{2,1,0:T(8,128)(2,1)S(1)} %get-tuple-element.41), channel_id=1, source_target_pairs={{0,13},{1,12},{2,15},{3,14},{4,9},{5,8},{6,11},{7,10},{8,5},{9,4},... | collective-permute-start | bytes 221192 | tf_op jit(solution)/shard_map/ppermute | solution.py:403
  21.0 9.2 %collective-permute-start.11 = (bf16[3,48,256]{2,1,0:T(8,128)(2,1)S(1)}, bf16[3,48,256]{2,1,0:T(8,128)(2,1)S(1)}, u32[]{:S(2)}, u32[]{:S(2)}) collective-permute-start(bf16[3,48,256]{2,1,0:T(8,128)(2,1)S(1)} %get-tuple-element.42), channel_id=1, source_target_pairs={{0,6},{1,7},{2,4},{3,5},{4,2},{5,3},{6,0},{7,1},{8,14},{9,15},{10,... | collective-permute-start | bytes 221192 | tf_op jit(solution)/shard_map/ppermute | solution.py:403
  22.5 7.9 %collective-permute-start.12 = (bf16[3,48,256]{2,1,0:T(8,128)(2,1)S(1)}, bf16[3,48,256]{2,1,0:T(8,128)(2,1)S(1)}, u32[]{:S(2)}, u32[]{:S(2)}) collective-permute-start(bf16[3,48,256]{2,1,0:T(8,128)(2,1)S(1)} %get-tuple-element.43), channel_id=1, source_target_pairs={{0,14},{1,15},{2,12},{3,13},{4,10},{5,11},{6,8},{7,9},{8,6},{9,7},... | collective-permute-start | bytes 221192 | tf_op jit(solution)/shard_map/ppermute | solution.py:403
  26.1 5.7 %collective-permute-start.13 = (bf16[3,48,256]{2,1,0:T(8,128)(2,1)S(1)}, bf16[3,48,256]{2,1,0:T(8,128)(2,1)S(1)}, u32[]{:S(2)}, u32[]{:S(2)}) collective-permute-start(bf16[3,48,256]{2,1,0:T(8,128)(2,1)S(1)} %get-tuple-element.44), channel_id=1, source_target_pairs={{0,7},{1,6},{2,5},{3,4},{4,3},{5,2},{6,1},{7,0},{8,15},{9,14},{10,... | collective-permute-start | bytes 221192 | tf_op jit(solution)/shard_map/ppermute | solution.py:403
  26.1 7.4 %collective-permute-start.14 = (bf16[3,48,256]{2,1,0:T(8,128)(2,1)S(1)}, bf16[3,48,256]{2,1,0:T(8,128)(2,1)S(1)}, u32[]{:S(2)}, u32[]{:S(2)}) collective-permute-start(bf16[3,48,256]{2,1,0:T(8,128)(2,1)S(1)} %get-tuple-element.45), channel_id=1, source_target_pairs={{0,15},{1,14},{2,13},{3,12},{4,11},{5,10},{6,9},{7,8},{8,7},{9,6},... | collective-permute-start | bytes 221192 | tf_op jit(solution)/shard_map/ppermute | solution.py:403
  35.4 1.4 %collective-permute-start.15 = (bf16[400,128]{1,0:T(8,128)(2,1)S(1)}, bf16[400,128]{1,0:T(8,128)(2,1)S(1)}, u32[]{:S(2)}, u32[]{:S(2)}) collective-permute-start(bf16[400,128]{1,0:T(8,128)(2,1)S(1)} %get-tuple-element.48), channel_id=1, source_target_pairs={{0,1},{1,0},{2,3},{3,2},{4,5},{5,4},{6,7},{7,6},{8,9},{9,8},{10,11... | collective-permute-start | bytes 307208 | tf_op jit(solution)/shard_map/ppermute | solution.py:403
  36.8 4.2 %collective-permute-start.16 = (bf16[200,128]{1,0:T(8,128)(2,1)S(1)}, bf16[200,128]{1,0:T(8,128)(2,1)S(1)}, u32[]{:S(2)}, u32[]{:S(2)}) collective-permute-start(bf16[200,128]{1,0:T(8,128)(2,1)S(1)} %get-tuple-element.50), channel_id=1, source_target_pairs={{0,2},{1,3},{2,0},{3,1},{4,6},{5,7},{6,4},{7,5},{8,10},{9,11},{10,... | collective-permute-start | bytes 153608 | tf_op jit(solution)/shard_map/ppermute | solution.py:403
  41.0 6.6 %collective-permute-start.19 = (bf16[200,128]{1,0:T(8,128)(2,1)S(1)}, bf16[200,128]{1,0:T(8,128)(2,1)S(1)}, u32[]{:S(2)}, u32[]{:S(2)}) collective-permute-start(bf16[200,128]{1,0:T(8,128)(2,1)S(1)} %get-tuple-element.52), channel_id=1, source_target_pairs={{0,12},{1,13},{2,14},{3,15},{4,8},{5,9},{6,10},{7,11},{8,4},{9,5},... | collective-permute-start | bytes 153608 | tf_op jit(solution)/shard_map/ppermute | solution.py:403
  43.1 5.6 %collective-permute-start.18 = (bf16[200,128]{1,0:T(8,128)(2,1)S(1)}, bf16[200,128]{1,0:T(8,128)(2,1)S(1)}, u32[]{:S(2)}, u32[]{:S(2)}) collective-permute-start(bf16[200,128]{1,0:T(8,128)(2,1)S(1)} %get-tuple-element.52), channel_id=1, source_target_pairs={{0,8},{1,9},{2,10},{3,11},{4,12},{5,13},{6,14},{7,15},{8,0},{9,1},... | collective-permute-start | bytes 153608 | tf_op jit(solution)/shard_map/ppermute | solution.py:403
  43.2 5.4 %collective-permute-start.17 = (bf16[200,128]{1,0:T(8,128)(2,1)S(1)}, bf16[200,128]{1,0:T(8,128)(2,1)S(1)}, u32[]{:S(2)}, u32[]{:S(2)}) collective-permute-start(bf16[200,128]{1,0:T(8,128)(2,1)S(1)} %get-tuple-element.52), channel_id=1, source_target_pairs={{0,4},{1,5},{2,6},{3,7},{4,0},{5,1},{6,2},{7,3},{8,12},{9,13},{10,... | collective-permute-start | bytes 153608 | tf_op jit(solution)/shard_map/ppermute | solution.py:403
  48.8 3.9 %collective-permute-start.22 = (bf16[192,128]{1,0:T(8,128)(2,1)S(1)}, bf16[192,128]{1,0:T(8,128)(2,1)S(1)}, u32[]{:S(2)}, u32[]{:S(2)}) collective-permute-start(bf16[192,128]{1,0:T(8,128)(2,1)S(1)} %shard_map.88.rest_0_), channel_id=1, source_target_pairs={{0,3},{1,2},{2,1},{3,0},{4,7},{5,6},{6,5},{7,4},{8,11},{9,10},{10,... | collective-permute-start | bytes 147464 | tf_op jit(solution)/shard_map/ppermute | solution.py:403
  48.8 4.6 %collective-permute-start.21 = (bf16[192,128]{1,0:T(8,128)(2,1)S(1)}, bf16[192,128]{1,0:T(8,128)(2,1)S(1)}, u32[]{:S(2)}, u32[]{:S(2)}) collective-permute-start(bf16[192,128]{1,0:T(8,128)(2,1)S(1)} %shard_map.88.rest_0_), channel_id=1, source_target_pairs={{0,2},{1,3},{2,0},{3,1},{4,6},{5,7},{6,4},{7,5},{8,10},{9,11},{10,... | collective-permute-start | bytes 147464 | tf_op jit(solution)/shard_map/ppermute | solution.py:403
  50.0 3.5 %collective-permute-start.20 = (bf16[192,128]{1,0:T(8,128)(2,1)S(1)}, bf16[192,128]{1,0:T(8,128)(2,1)S(1)}, u32[]{:S(2)}, u32[]{:S(2)}) collective-permute-start(bf16[192,128]{1,0:T(8,128)(2,1)S(1)} %shard_map.88.rest_0_), channel_id=1, source_target_pairs={{0,1},{1,0},{2,3},{3,2},{4,5},{5,4},{6,7},{7,6},{8,9},{9,8},{10,11... | collective-permute-start | bytes 147464 | tf_op jit(solution)/shard_map/ppermute | solution.py:403
